TPU v7x, 256 devices: a whole 4x4x8 slice. The times are simulated.
256 devices in a mesh: freq: 64 (over y, z, x_hi), inp: 4 (over x_lo, core).
Axes of the slice: x: 4 (x_hi: 2, x_lo: 2; x = x_hi * 2 + x_lo), y: 4, z: 8, core: 2. Of those that a mesh axis runs over, the one named last changes fastest.
Arguments:
- voltages: int32 [192, 2048, 1024], P('freq', None, 'inp'), may hold values from -128 to 127
- taps: float32 [12, 2048], replicated, may hold values from -0.013671875 to 0.013671875
- start: int32 [8, 2, 1024], replicated, may hold values from -127 to 127
Outputs:
- cleaned: bfloat16 [1024, 192, 2, 1024], P('freq', None, None, 'inp')
- ritz_matrix: float32 [1024, 8, 8], P('freq')
Inputs may be any that keep to these rules, and one draw needn't show every extreme that they name: `voltages`: 8-bit voltage samples.
All inputs are finite; a program needn't handle non-finite values.
Results may differ from a plain program's by a relative error of at most 0.0052.
Values may be sent and summed in bfloat16 or wider, within the bound.
No kernel may reach another device: no remote copies, remote signals or barrier semaphores. Data moves between devices by JAX's collectives and lax.ppermute only.
A program may use at most 192 MiB of HBM per device.

v0:
```python
import math

import jax
import jax.numpy as jnp
from jax import lax
from jax.sharding import PartitionSpec as P

ITERS = 4


def from_behind(value, axis, steps):
    count = lax.axis_size(axis)
    pairs = [(source, (source + steps) % count) for source in range(count)]
    return lax.ppermute(value, axis, pairs)


def project_rows(basis_rows, channel_data):
    projected = jnp.einsum(
        "ckr,cmr->ckm", basis_rows, channel_data, precision=lax.Precision.HIGHEST
    )
    return lax.psum(projected, "inp")


def subspace_clean(turned, start_block):
    highest = lax.Precision.HIGHEST
    channel_local, spectra_count, part_count, inputs_width = turned.shape
    row_count = part_count * inputs_width
    channel_data = turned.reshape(channel_local, spectra_count, row_count).astype(jnp.float32)
    start_rows = start_block.reshape(start_block.shape[0], row_count).astype(jnp.float32)
    basis_rows = jnp.broadcast_to(start_rows[None], (channel_local,) + start_rows.shape)
    for iteration in range(ITERS):
        projected = project_rows(basis_rows, channel_data)
        mapped = (
            jnp.einsum("ckm,cmr->ckr", projected, channel_data, precision=highest) / spectra_count
        )
        gram_matrix = jnp.einsum("ckr,cjr->ckj", mapped, mapped, precision=highest)
        gram_matrix = lax.psum(gram_matrix, "inp")
        lower_factor = jnp.linalg.cholesky(gram_matrix)
        basis_rows = lax.linalg.triangular_solve(lower_factor, mapped, left_side=True, lower=True)
    projected = project_rows(basis_rows, channel_data)
    ritz_matrix = (
        jnp.einsum("ckm,cjm->ckj", projected, projected, precision=highest) / spectra_count
    )
    cleaned = channel_data - jnp.einsum("ckm,ckr->cmr", projected, basis_rows, precision=highest)
    cleaned = cleaned.reshape(channel_local, spectra_count, part_count, inputs_width).astype(
        jnp.bfloat16
    )
    return (cleaned, ritz_matrix)


def shards(voltages, taps, start):
    slot_count = voltages.shape[0]
    frame_len = voltages.shape[1]
    inputs_local = voltages.shape[2]
    channel_count = frame_len // 2
    tap_count = taps.shape[0]
    frame_stack = voltages.astype(jnp.bfloat16)
    history_len = tap_count - 1
    group_count = lax.axis_size("freq")
    portions = [frame_stack]
    shift_count = (history_len - 1) // slot_count + 1
    for distance in range(1, shift_count + 1):
        first_frame = max(0, distance * slot_count - history_len)
        portion = frame_stack[first_frame:]
        offset_mod = distance % group_count
        arrived = from_behind(portion, "freq", offset_mod)
        portions = [arrived] + portions
    extended = jnp.concatenate(portions, axis=0)
    filtered = jnp.zeros((slot_count, frame_len, inputs_local), jnp.float32)
    for tap_index in range(tap_count):
        window = extended[tap_index : tap_index + slot_count].astype(jnp.float32)
        filtered = filtered + taps[tap_index][None, :, None] * window
    channel_idx = lax.broadcasted_iota(jnp.int32, (channel_count, frame_len), 0)
    sample_idx = lax.broadcasted_iota(jnp.int32, (channel_count, frame_len), 1)
    angles = (channel_idx * sample_idx % frame_len).astype(jnp.float32) * (
        2.0 * math.pi / frame_len
    )
    dft_scale = 1.0 / math.sqrt(channel_count)
    cosine = jnp.cos(angles)
    sine_table = jnp.sin(angles)
    real_part = (
        jnp.einsum("kn,sni->ksi", cosine, filtered, precision=lax.Precision.HIGHEST) * dft_scale
    )
    imag_part = (
        -jnp.einsum("kn,sni->ksi", sine_table, filtered, precision=lax.Precision.HIGHEST)
        * dft_scale
    )
    spectra = jnp.stack([real_part, imag_part], axis=2).astype(jnp.bfloat16)
    turned = lax.all_to_all(spectra, "freq", split_axis=0, concat_axis=1, tiled=True)
    start_local = lax.dynamic_slice_in_dim(
        start, lax.axis_index("inp") * inputs_local, inputs_local, 2
    )
    cleaned, ritz_matrix = subspace_clean(turned, start_local)
    return (cleaned, ritz_matrix)


def solution(mesh):
    placed = (P("freq", None, "inp"), P(), P())
    return jax.shard_map(
        shards,
        mesh=mesh,
        in_specs=placed,
        out_specs=(P("freq", None, None, "inp"), P("freq", None, None)),
        check_vma=False,
    )
```

profile of v0, /device:TPU:1, one launch (start us, length us, event | category | flops | bytes accessed | tf_op | source)
XLA Modules:
  0.0 1002.1 jit_solution(7785082553652282310)
XLA Ops:
  7.2 3.3 convert_element_type.65
  10.5 5.0 collective-permute-start.1
  15.5 1.6 collective-permute-start.2
  17.2 1.6 collective-permute-start.3
  18.9 3.4 collective-permute-start
  22.3 181.6 %collective-permute-done = bf16[2,2048,256]{2,1,0:T(8,128)(2,1)S(1)} collective-permute-done((bf16[2,2048,256]{2,1,0:T(8,128)(2,1)S(1)}, bf16[2,2048,256]{2,1,0:T(8,128)(2,1)S(1)}, u32[]{:S(2)}, u32[]{:S(2)}) %collective-permute-start) | collective-permute-done | bytes 2097184 | tf_op jit(solution)/shard_map/ppermute | solution.py:14
  204.6 16.6 %collective-permute-done.2 = bf16[3,2048,256]{2,1,0:T(8,128)(2,1)S(1)} collective-permute-done((bf16[3,2048,256]{2,1,0:T(8,128)(2,1)S(1)}, bf16[3,2048,256]{2,1,0:T(8,128)(2,1)S(1)}, u32[]{:S(2)}, u32[]{:S(2)}) %collective-permute-start.2) | collective-permute-done | bytes 3145760 | tf_op jit(solution)/shard_map/ppermute | solution.py:14
  221.6 70.7 %collective-permute-done.3 = bf16[3,2048,256]{2,1,0:T(8,128)(2,1)S(1)} collective-permute-done((bf16[3,2048,256]{2,1,0:T(8,128)(2,1)S(1)}, bf16[3,2048,256]{2,1,0:T(8,128)(2,1)S(1)}, u32[]{:S(2)}, u32[]{:S(2)}) %collective-permute-start.3) | collective-permute-done | bytes 3145760 | tf_op jit(solution)/shard_map/ppermute | solution.py:14
  292.5 9.7 multiply_add_fusion
  302.2 64.8 %fusion.19 = bf16[1024,3,1,256]{3,0,1,2:T(8,128)(2,1)S(1)} fusion(f32[3,2048,256]{2,1,0:T(8,128)} %multiply_add_fusion), kind=kOutput, calls=%fused_computation.25 | convolution fusion | flops 19358285824 | bytes 7864320 | tf_op jit(solution)/shard_map/kn,sni->ksi/dot_general | solution.py:82
  367.0 53.0 %fusion.22 = bf16[1024,3,1,256]{3,0,1,2:T(8,128)(2,1)S(1)} fusion(f32[3,2048,256]{2,1,0:T(8,128)S(1)} %copy-done), kind=kOutput, calls=%fused_computation.26 | convolution fusion | flops 19359072256 | bytes 7864320 | tf_op jit(solution)/shard_map/kn,sni->ksi/dot_general | solution.py:85
  420.3 4.9 copy.77
  425.2 98.1 %all-to-all-start = ((bf16[1024,3,2,256]{3,2,1,0:T(2,128)(2,1)}), bf16[1024,3,2,256]{3,2,1,0:T(2,128)(2,1)S(1)}, u32[]{:S(2)}, u32[]{:S(2)}) async-start(bf16[1024,3,2,256]{3,2,1,0:T(2,128)(2,1)} %copy.77), calls=%async_computation | async-start | bytes 6291456 | tf_op jit(solution)/shard_map/all_to_all | solution.py:89
  523.4 0.7 convert_bitcast_fusion
  524.1 71.6 %all-to-all-done = bf16[1024,3,2,256]{3,2,1,0:T(2,128)(2,1)S(1)} async-done(((bf16[1024,3,2,256]{3,2,1,0:T(2,128)(2,1)}), bf16[1024,3,2,256]{3,2,1,0:T(2,128)(2,1)S(1)}, u32[]{:S(2)}, u32[]{:S(2)}) %all-to-all-start) | async-done | bytes 3145760 | tf_op jit(solution)/shard_map/all_to_all | solution.py:89
  595.7 4.7 copy.110
  600.4 4.6 reshape.41
  605.0 3.2 fusion.25
  608.3 38.9 %all-reduce.6.cloned.1.call-done = f32[16,8,192]{2,1,0:T(8,128)} async-done(((f32[16,8,192]{2,1,0:T(8,128)}), f32[16,8,192]{2,1,0:T(8,128)}) %all-reduce.6.cloned.1.call-update) | async-done | bytes 98320 | tf_op jit(solution)/shard_map/psum | solution.py:21
  647.2 2.2 convolution_multiply_fusion.3
  650.1 10.6 %psum.64 = f32[16,8,8]{1,2,0:T(8,128)S(1)} all-reduce(f32[16,8,8]{1,2,0:T(8,128)S(1)} %fusion.48), channel_id=1, replica_groups=mesh['freq'=64,'inp'=4] {'inp'}, use_global_device_ids=true, to_apply=%region_1.2 | all-reduce | flops 1024 | bytes 8192 | tf_op jit(solution)/shard_map/psum | solution.py:37
  660.8 0.6 fusion.38
  661.4 12.4 %custom-call.12 = f32[16,8,8]{2,1,0:T(8,128)S(1)} custom-call(f32[16,8,8]{2,1,0:T(8,128)} %fusion.38), custom_call_target="Cholesky" | custom-call | tf_op jit(solution)/shard_map/jit(cholesky)/cholesky | solution.py:38
  674.1 10.0 custom-call.13
  684.6 3.2 fusion.49
  688.3 42.2 %all-reduce.8.cloned.1.call-done = f32[16,8,192]{2,1,0:T(8,128)} async-done(((f32[16,8,192]{2,1,0:T(8,128)}), f32[16,8,192]{2,1,0:T(8,128)}) %all-reduce.8.cloned.1.call-update) | async-done | bytes 98320 | tf_op jit(solution)/shard_map/psum | solution.py:21
  730.5 2.2 convolution_multiply_fusion.2
  733.3 10.6 %psum.66 = f32[16,8,8]{1,2,0:T(8,128)S(1)} all-reduce(f32[16,8,8]{1,2,0:T(8,128)S(1)} %fusion.50), channel_id=1, replica_groups=mesh['freq'=64,'inp'=4] {'inp'}, use_global_device_ids=true, to_apply=%region_5.8 | all-reduce | flops 1024 | bytes 8192 | tf_op jit(solution)/shard_map/psum | solution.py:37
  744.7 12.4 %custom-call.14 = f32[16,8,8]{2,1,0:T(8,128)S(1)} custom-call(f32[16,8,8]{2,1,0:T(8,128)} %fusion.35), custom_call_target="Cholesky" | custom-call | tf_op jit(solution)/shard_map/jit(cholesky)/cholesky | solution.py:38
  757.3 10.0 custom-call.15
  767.8 3.2 fusion.51
  771.1 42.6 %all-reduce.10.cloned.1.call-done = f32[16,8,192]{2,1,0:T(8,128)} async-done(((f32[16,8,192]{2,1,0:T(8,128)}), f32[16,8,192]{2,1,0:T(8,128)}) %all-reduce.10.cloned.1.call-update) | async-done | bytes 98320 | tf_op jit(solution)/shard_map/psum | solution.py:21
  813.8 2.2 convolution_multiply_fusion.1
  816.6 10.6 %psum.68 = f32[16,8,8]{1,2,0:T(8,128)S(1)} all-reduce(f32[16,8,8]{1,2,0:T(8,128)S(1)} %fusion.52), channel_id=1, replica_groups=mesh['freq'=64,'inp'=4] {'inp'}, use_global_device_ids=true, to_apply=%region_7.10 | all-reduce | flops 1024 | bytes 8192 | tf_op jit(solution)/shard_map/psum | solution.py:37
  827.9 12.4 %custom-call.16 = f32[16,8,8]{2,1,0:T(8,128)S(1)} custom-call(f32[16,8,8]{2,1,0:T(8,128)} %fusion.32), custom_call_target="Cholesky" | custom-call | tf_op jit(solution)/shard_map/jit(cholesky)/cholesky | solution.py:38
  840.6 10.0 custom-call.17
  851.1 3.2 fusion.53
  854.4 42.6 %all-reduce.12.cloned.1.call-done = f32[16,8,192]{2,1,0:T(8,128)} async-done(((f32[16,8,192]{2,1,0:T(8,128)}), f32[16,8,192]{2,1,0:T(8,128)}) %all-reduce.12.cloned.1.call-update) | async-done | bytes 98320 | tf_op jit(solution)/shard_map/psum | solution.py:21
  897.0 2.2 convolution_multiply_fusion
  899.9 10.8 %psum.70 = f32[16,8,8]{1,2,0:T(8,128)S(1)} all-reduce(f32[16,8,8]{1,2,0:T(8,128)S(1)} %fusion.54), channel_id=1, replica_groups=mesh['freq'=64,'inp'=4] {'inp'}, use_global_device_ids=true, to_apply=%region_9.12 | all-reduce | flops 1024 | bytes 8192 | tf_op jit(solution)/shard_map/psum | solution.py:37
  911.4 12.4 %custom-call.18 = f32[16,8,8]{2,1,0:T(8,128)S(1)} custom-call(f32[16,8,8]{2,1,0:T(8,128)} %fusion.29), custom_call_target="Cholesky" | custom-call | tf_op jit(solution)/shard_map/jit(cholesky)/cholesky | solution.py:38
  924.0 10.0 custom-call.19
  934.6 0.7 copy-done.1
  935.3 3.2 fusion.55
  938.5 42.7 %all-reduce.14.cloned.1.call-done = f32[16,8,192]{2,1,0:T(8,128)} async-done(((f32[16,8,192]{2,1,0:T(8,128)}), f32[16,8,192]{2,1,0:T(8,128)}) %all-reduce.14.cloned.1.call-update) | async-done | bytes 98320 | tf_op jit(solution)/shard_map/psum | solution.py:21
  981.2 7.7 subtract_convert_fusion
  988.9 5.5 convert_element_type.82
  994.7 0.7 copy.99
  (60 shorter events, 10.3 us)
Async XLA Ops:
  7.2 15.1 %copy-start.3 = (f32[12,2048]{1,0:T(8,128)S(1)}, f32[12,2048]{1,0:T(8,128)}, u32[]{:S(2)}) copy-start(f32[12,2048]{1,0:T(8,128)} %param.7) | copy-start | bytes 294916
  10.5 193.6 %collective-permute-start.1 = (bf16[3,2048,256]{2,1,0:T(8,128)(2,1)S(1)}, bf16[3,2048,256]{2,1,0:T(8,128)(2,1)S(1)}, u32[]{:S(2)}, u32[]{:S(2)}) collective-permute-start(bf16[3,2048,256]{2,1,0:T(8,128)(2,1)S(1)} %convert_element_type.65), channel_id=1, source_target_pairs={{0,12},{4,16},{8,20},{12,24},{16,28},{20,32},{24,36},{28,40},{32,4... | collective-permute-start | bytes 9437192 | tf_op jit(solution)/shard_map/ppermute | solution.py:14
  15.5 205.7 %collective-permute-start.2 = (bf16[3,2048,256]{2,1,0:T(8,128)(2,1)S(1)}, bf16[3,2048,256]{2,1,0:T(8,128)(2,1)S(1)}, u32[]{:S(2)}, u32[]{:S(2)}) collective-permute-start(bf16[3,2048,256]{2,1,0:T(8,128)(2,1)S(1)} %convert_element_type.65), channel_id=1, source_target_pairs={{0,8},{4,12},{8,16},{12,20},{16,24},{20,28},{24,32},{28,36},{32,40... | collective-permute-start | bytes 9437192 | tf_op jit(solution)/shard_map/ppermute | solution.py:14
  17.2 275.1 %collective-permute-start.3 = (bf16[3,2048,256]{2,1,0:T(8,128)(2,1)S(1)}, bf16[3,2048,256]{2,1,0:T(8,128)(2,1)S(1)}, u32[]{:S(2)}, u32[]{:S(2)}) collective-permute-start(bf16[3,2048,256]{2,1,0:T(8,128)(2,1)S(1)} %convert_element_type.65), channel_id=1, source_target_pairs={{0,4},{4,8},{8,12},{12,16},{16,20},{20,24},{24,28},{28,32},{32,36}... | collective-permute-start | bytes 9437192 | tf_op jit(solution)/shard_map/ppermute | solution.py:14
  18.9 185.1 %collective-permute-start = (bf16[2,2048,256]{2,1,0:T(8,128)(2,1)S(1)}, bf16[2,2048,256]{2,1,0:T(8,128)(2,1)S(1)}, u32[]{:S(2)}, u32[]{:S(2)}) collective-permute-start(bf16[2,2048,256]{2,1,0:T(8,128)(2,1)S(1)} %slice.98), channel_id=1, source_target_pairs={{0,16},{4,20},{8,24},{12,28},{16,32},{20,36},{24,40},{28,44},{32,4... | collective-permute-start | bytes 6291464 | tf_op jit(solution)/shard_map/ppermute | solution.py:14
  302.2 64.8 %copy-start = (f32[3,2048,256]{2,1,0:T(8,128)S(1)}, f32[3,2048,256]{2,1,0:T(8,128)}, u32[]{:S(2)}) copy-start(f32[3,2048,256]{2,1,0:T(8,128)} %multiply_add_fusion) | copy-start | bytes 18874372
  425.2 170.6 %all-to-all-start = ((bf16[1024,3,2,256]{3,2,1,0:T(2,128)(2,1)}), bf16[1024,3,2,256]{3,2,1,0:T(2,128)(2,1)S(1)}, u32[]{:S(2)}, u32[]{:S(2)}) async-start(bf16[1024,3,2,256]{3,2,1,0:T(2,128)(2,1)} %copy.77), calls=%async_computation | async-start | bytes 6291456 | tf_op jit(solution)/shard_map/all_to_all | solution.py:89
  523.3 123.9 %all-reduce.6.cloned.1.call-start = ((), (), s32[]{:S(2)}) async-start(), calls=%async_computation.1 | async-start | bytes 262144 | tf_op jit(solution)/shard_map/psum | solution.py:21
  608.2 122.3 %all-reduce.8.cloned.1.call-start = ((), (), s32[]{:S(2)}) async-start(), calls=%async_computation.2 | async-start | bytes 262144 | tf_op jit(solution)/shard_map/psum | solution.py:21
  687.8 126.0 %all-reduce.10.cloned.1.call-start = ((), (), s32[]{:S(2)}) async-start(), calls=%async_computation.3 | async-start | bytes 262144 | tf_op jit(solution)/shard_map/psum | solution.py:21
  771.1 126.0 %all-reduce.12.cloned.1.call-start = ((), (), s32[]{:S(2)}) async-start(), calls=%async_computation.4 | async-start | bytes 262144 | tf_op jit(solution)/shard_map/psum | solution.py:21
  854.3 126.8 %all-reduce.14.cloned.1.call-start = ((), (), s32[]{:S(2)}) async-start(), calls=%async_computation.5 | async-start | bytes 262144 | tf_op jit(solution)/shard_map/psum | solution.py:21
  934.6 0.7 copy-start.1
  981.2 13.2 %copy-start.2 = (f32[16,8,192]{2,1,0:T(8,128)S(1)}, f32[16,8,192]{2,1,0:T(8,128)}, u32[]{:S(2)}) copy-start(f32[16,8,192]{2,1,0:T(8,128)} %all-reduce.14.cloned.1.call-done) | copy-start | bytes 294916
Sparse Core Ops, SparseCore 0:
  608.4 38.8 all-reduce.5
  687.9 42.5 all-reduce.7
  771.2 42.5 all-reduce.9
  854.4 42.5 all-reduce.11
  938.6 42.5 all-reduce.13
where the time goes:
time: 1010 us; the launch traced here: 1000 us
  waiting for transfers between devices  550 us (54%)
  matrix products  155 us (15%)
  starting transfers between devices  110 us (11%)
  other arithmetic  107 us (11%)
  blocking collectives  42.7 us (4%)
  local copies, waits for them, and re-layouts  23 us (2%)
  between operations  14.2 us (1%)
    ppermute x4, waiting for transfers between devices, from_behind(): return lax.ppermute(value, axis, pairs)  269 us
    psum x5, waiting for transfers between devices, project_rows(): return lax.psum(projected, 'inp')  209 us
    all_to_all x1, starting transfers between devices, shards(): lax.all_to_all(spectra, 'freq', split_axis=0, concat_axis=1, tiled=True)  98.1 us
    all_to_all x1, waiting for transfers between devices, shards(): lax.all_to_all(spectra, 'freq', split_axis=0, concat_axis=1, tiled=True)  71.6 us
    dot_general x1, matrix products, shards(): jnp.einsum('kn,sni->ksi', cosine, filtered, precision=lax.Precision.HIGHEST)  64.8 us
    dot_general x1, matrix products, shards(): jnp.einsum('kn,sni->ksi', sine_table, filtered, precision=lax.Precision.H...  53 us
    another operation x13, other arithmetic, subspace_clean(): lower_factor = jnp.linalg.cholesky(gram_matrix)  49.9 us
    psum x4, blocking collectives, subspace_clean(): gram_matrix = lax.psum(gram_matrix, 'inp')  42.7 us
  transfers between devices with their start and end apart: 10, of which 9 were waited for; matrix products, arithmetic and copies ran while one was open for 0% of the time, Pallas kernels for 0%

commit v1 on v0

v1 whole, which is shorter than its diff:
```python
import math

import jax
import jax.numpy as jnp
import numpy as np
from jax import lax
from jax.experimental import pallas as pl
from jax.experimental.pallas import tpu as pltpu
from jax.sharding import Mesh, PartitionSpec as P

ITERS = 4
FREQ = ("y", "z", "h")
INP = ("l", "k")
LANES = 128
SLOTS = 3
SHIFT = 5
BF = jnp.bfloat16
F32 = jnp.float32


def cyclic(count, steps):
    return [(i, (i + steps) % count) for i in range(count)]


def split2(value):
    high = lax.reduce_precision(value, 8, 7)
    return high.astype(BF), (value - high).astype(BF)


def dft_tables(frame_len, groups):
    half = frame_len // 2
    per = half // groups
    unit = 2.0 * math.pi / frame_len
    scale = 1.0 / math.sqrt(half)
    n_a = lax.broadcasted_iota(jnp.int32, (groups, half), 1)
    f_a = lax.broadcasted_iota(jnp.int32, (groups, half), 0)
    ang_a = ((f_a * per * n_a) % frame_len).astype(F32) * unit
    n_b = lax.broadcasted_iota(jnp.int32, (per, half), 1)
    j_b = lax.broadcasted_iota(jnp.int32, (per, half), 0)
    ang_b = ((j_b * n_b) % frame_len).astype(F32) * unit
    ca, sa = lax.optimization_barrier((jnp.cos(ang_a), jnp.sin(ang_a)))
    cb, sb = lax.optimization_barrier((jnp.cos(ang_b) * scale, jnp.sin(ang_b) * scale))
    rows = []
    for kind in range(2):
        for par in range(2):
            c2, s2 = cb[par::2][None], sb[par::2][None]
            c1, s1 = ca[:, None], sa[:, None]
            table = c1 * c2 - s1 * s2 if kind == 0 else -(s1 * c2 + c1 * s2)
            rows.append(table.reshape(groups * (per // 2), half))
    return split2(jnp.stack(rows))


def filter_dft_kernel(up, own, down, par, rec, coef, wh, wl, out, fold):
    half = own.shape[2]
    step = 32
    width = SLOTS * LANES

    @pl.when(pl.program_id(0) == 0)
    def _():
        def body(idx, carry):
            rows = pl.ds(pl.multiple_of(idx * step, step), step)
            results = []
            for side in range(2):
                cols = coef[side, rows, :]
                col = lambda t: jnp.broadcast_to(cols[:, t : t + 1], (step, LANES))
                taps = [col(t) for t in range(22)]
                acc = [None] * SLOTS
                for ref, base in ((up, 0), (rec, 19), (own, 6), (par, 14), (down, 12)):
                    for a in range(SLOTS):
                        frame = ref[a, side, rows, :].astype(F32)
                        for r in range(SLOTS):
                            t = base + a - r
                            if base in (0, 12) and not 0 <= t < 12:
                                continue
                            term = taps[t] * frame
                            acc[r] = term if acc[r] is None else acc[r] + term
                results.append(acc)
            for kind in range(2):
                for r in range(SLOTS):
                    lo, hi = results[0][r], results[1][r]
                    value = lo + hi if kind == 0 else lo - hi
                    top = value.astype(BF)
                    rest = (value - top.astype(F32)).astype(BF)
                    fold[kind, rows, r * LANES : (r + 1) * LANES] = top
                    fold[kind, rows, width + r * LANES : width + (r + 1) * LANES] = rest
            return carry

        lax.fori_loop(0, half // step, body, 0)

    groups = out.shape[0]
    for kind in range(2):
        parts = []
        for parity in range(2):
            index = kind * 2 + parity
            full = jnp.dot(wh[index], fold[parity], preferred_element_type=F32)
            rest = jnp.dot(wl[index], fold[parity, :, :width], preferred_element_type=F32)
            total = full[:, :width] + full[:, width:] + rest
            parts.append(total.reshape(groups, total.shape[0] // groups, width))
        both = jnp.concatenate(parts, axis=1).astype(BF)
        out[:, :, kind * width : (kind + 1) * width] = both


def filter_dft(blocks, coef, table_h, table_l, groups):
    frame_len = blocks[0].shape[1]
    half = frame_len // 2
    rows = table_h.shape[1]
    per = half // groups
    width = SLOTS * LANES
    steps = 2
    blocks = [b.reshape(SLOTS, 2, half, LANES) for b in blocks]
    whole = pl.BlockSpec((SLOTS, 2, half, LANES), lambda i: (0, 0, 0, 0))
    table = pl.BlockSpec((4, rows // steps, half), lambda i: (0, i, 0))
    return pl.pallas_call(
        filter_dft_kernel,
        out_shape=jax.ShapeDtypeStruct((groups, per, 2 * width), BF),
        grid=(steps,),
        in_specs=[whole] * 5
        + [pl.BlockSpec((2, half, coef.shape[2]), lambda i: (0, 0, 0)), table, table],
        out_specs=pl.BlockSpec((groups // steps, per, 2 * width), lambda i: (i, 0, 0)),
        scratch_shapes=[pltpu.VMEM((2, half, 2 * width), BF)],
        compiler_params=pltpu.CompilerParams(vmem_limit_bytes=58 << 20),
        name="filter_dft",
    )(*blocks, coef, table_h, table_l)


def split3(value):
    first = value.astype(BF)
    left = value - first.astype(F32)
    second = left.astype(BF)
    third = (left - second.astype(F32)).astype(BF)
    return first, second, third


def wide_dot(a, b, dims):
    return lax.dot_general(
        a, b, (dims, ((), ())), precision=lax.Precision.HIGHEST, preferred_element_type=F32
    )


def iterate_kernel(gram_ref, out, *, spectra):
    count = gram_ref.shape[0]
    block = gram_ref.shape[1] - spectra
    inverse = 1.0 / spectra
    rows = lax.broadcasted_iota(jnp.int32, (block, 1), 0)
    covs = [gram_ref[c, :spectra, :] for c in range(count)]
    proj = [gram_ref[c, spectra:, :] for c in range(count)]
    coef = [None] * count
    for iteration in range(ITERS):
        mapped = [wide_dot(proj[c], covs[c], ((1,), (0,))) * inverse for c in range(count)]
        gram = [wide_dot(mapped[c], proj[c], ((1,), (1,))) * inverse for c in range(count)]
        before = [proj[c] * inverse for c in range(count)]
        scale = [jnp.zeros((block, 1), F32)] * count
        for j in range(block):
            for c in range(count):
                pivot = gram[c][j : j + 1, j : j + 1]
                factor = jnp.where(rows > j, gram[c][:, j : j + 1] / pivot, 0.0)
                scale[c] = jnp.where(rows == j, 1.0 / jnp.sqrt(pivot), scale[c])
                gram[c] = gram[c] - factor * gram[c][j : j + 1, :]
                mapped[c] = mapped[c] - factor * mapped[c][j : j + 1, :]
                before[c] = before[c] - factor * before[c][j : j + 1, :]
        proj = [mapped[c] * scale[c] for c in range(count)]
        coef = [before[c] * scale[c] for c in range(count)]
    for c in range(count):
        out[c, :block, :] = coef[c]
        out[c, block:, :] = wide_dot(coef[c], covs[c], ((1,), (0,)))


def iterate(gram, spectra):
    count, rows, _ = gram.shape
    block = rows - spectra
    return pl.pallas_call(
        lambda g, o: iterate_kernel(g, o, spectra=spectra),
        out_shape=jax.ShapeDtypeStruct((count, 2 * block, spectra), F32),
        compiler_params=pltpu.CompilerParams(vmem_limit_bytes=32 << 20),
        name="iterate",
    )(gram)


def clean_kernel(xa, xb, pair, perm, out, ritz, *, spectra):
    block = pair.shape[1] // 2
    coef = pair[0, :block, :]
    proj = pair[0, block:, :]
    ritz[0] = wide_dot(proj, proj, ((1,), (1,))) * (1.0 / spectra)
    coef3 = jnp.concatenate(split3(coef), axis=0)
    order = perm[...]
    turned = sum(
        jnp.dot(order, part.T, preferred_element_type=F32) for part in split3(proj)
    )
    ph, pm, pt = split3(-turned)
    left = jnp.concatenate([order, ph, ph, ph, pm, pm, pt], axis=1)
    for chunk, ref in enumerate((xa, xb)):
        x = ref[0]
        base = jnp.dot(coef3, x, preferred_element_type=F32)
        base = base[:block] + base[block : 2 * block] + base[2 * block :]
        bh, bm, bt = split3(base)
        right = jnp.concatenate([x, bh, bm, bt, bh, bm, bh], axis=0)
        result = jnp.dot(left, right, preferred_element_type=F32).astype(BF)
        for part in range(2):
            lane = part * 2 * LANES + chunk * LANES
            out[0, :, lane : lane + LANES] = result[:, part * LANES : (part + 1) * LANES]


def clean(xs, pair, spectra):
    channels = pair.shape[0]
    block = pair.shape[1] // 2
    width = 2 * LANES
    order = np.zeros((spectra, spectra), np.float32)
    for m in range(spectra):
        order[m, (m - SHIFT) % spectra] = 1.0
    x_spec = pl.BlockSpec((1, spectra, width), lambda c: (c, 0, 0))
    return pl.pallas_call(
        lambda *refs: clean_kernel(*refs, spectra=spectra),
        out_shape=(
            jax.ShapeDtypeStruct((channels, spectra, 2 * width), BF),
            jax.ShapeDtypeStruct((channels, block, block), F32),
        ),
        grid=(channels,),
        in_specs=[
            x_spec,
            x_spec,
            pl.BlockSpec((1, 2 * block, spectra), lambda c: (c, 0, 0)),
            pl.BlockSpec((spectra, spectra), lambda c: (0, 0)),
        ],
        out_specs=(
            pl.BlockSpec((1, spectra, 2 * width), lambda c: (c, 0, 0)),
            pl.BlockSpec((1, block, block), lambda c: (c, 0, 0)),
        ),
        compiler_params=pltpu.CompilerParams(vmem_limit_bytes=32 << 20),
        name="clean",
    )(*xs, pair, jnp.asarray(order, BF))


def reduce_inputs(gram):
    for axis in ("k", "l"):
        half = gram.shape[0] // 2
        me = lax.axis_index(axis)
        keep = lax.dynamic_slice_in_dim(gram, me * half, half, 0)
        send = lax.dynamic_slice_in_dim(gram, (1 - me) * half, half, 0)
        gram = keep + lax.ppermute(send, axis, cyclic(2, 1))
    return gram


def gather_inputs(value):
    for axis in ("l", "k"):
        value = lax.all_gather(value, axis, tiled=True)
    return value


def shards(voltages, taps, start):
    slots, frame_len, inputs = voltages.shape
    half = frame_len // 2
    block = start.shape[0]
    groups = lax.axis_size("y") * lax.axis_size("z") * 2
    rings = groups // 2
    spectra = groups * slots
    per = half // groups
    chunks = inputs // LANES
    me = lax.axis_index("h")
    frames = voltages.astype(BF)

    by_sample = taps.T
    near = by_sample[:, 1:6]
    far = by_sample[:, 7:12]
    coef = jnp.concatenate(
        [by_sample, jnp.where(me == 0, far, near), jnp.where(me == 0, near, far)], axis=1
    ).reshape(2, half, 22)
    table_h, table_l = dft_tables(frame_len, groups)

    rank = lax.axis_index("l") * 2 + lax.axis_index("k")
    start_local = lax.dynamic_slice_in_dim(start, rank * inputs, inputs, 2).astype(BF)

    xs = []
    gram = None
    last = None
    for chunk in range(chunks):
        own = frames[:, :, chunk * LANES : (chunk + 1) * LANES]
        if last is not None:
            own = lax.optimization_barrier((own,) + last)[0]
        up = lax.ppermute(own, ("y", "z"), cyclic(rings, 1))
        down = lax.ppermute(own, ("y", "z"), cyclic(rings, -1))
        par = lax.ppermute(own, "h", cyclic(2, 1))
        rec = lax.ppermute(jnp.where(me == 0, down, up), "h", cyclic(2, 1))
        last = (up, down)
        spec = filter_dft((up, own, down, par, rec), coef, table_h, table_l, groups)
        turned = lax.all_to_all(spec, FREQ, split_axis=0, concat_axis=0, tiled=True)
        turned = turned.reshape(groups, 2, per // 2, 2, slots, LANES)
        x = turned.transpose(2, 1, 0, 4, 3, 5).reshape(per, spectra, 2 * LANES)
        xs.append(x)
        begin = start_local[:, :, chunk * LANES : (chunk + 1) * LANES].reshape(block, -1)
        square = jnp.einsum("cma,cna->cmn", x, x, preferred_element_type=F32)
        first = jnp.einsum("ka,cma->ckm", begin, x, preferred_element_type=F32)
        part = jnp.concatenate([square, first], axis=1)
        gram = part if gram is None else gram + part
    pair = gather_inputs(iterate(reduce_inputs(gram), spectra))
    cleaned, ritz = clean(xs, pair, spectra)
    return cleaned.reshape(per, spectra, 2, inputs), ritz


def on_mesh(mesh):
    return jax.shard_map(
        shards,
        mesh=mesh,
        in_specs=(P(FREQ, None, INP), P(), P()),
        out_specs=(P(FREQ, None, None, INP), P(FREQ, None, None)),
        check_vma=False,
    )


def solution(mesh):
    freq = mesh.shape["freq"]
    devices = mesh.devices.reshape(freq // 16, 8, 2, 2, 2)
    return on_mesh(Mesh(devices, FREQ + INP))
```

time: 1010 us -> 361 us (0.36)
  waiting for transfers between devices: 550 us -> 180 us
  matrix products: 155 us -> 3.86 us
  other arithmetic: 107 us -> 22.8 us
  starting transfers between devices: 110 us -> 46.6 us
  Pallas kernels: 0 us -> 57.6 us
  blocking collectives: 42.7 us -> 7.76 us
  local copies, waits for them, and re-layouts: 23 us -> 40.1 us
  between operations: 14.2 us -> 0.81 us
    psum x5 -> x0, waiting for transfers between devices: 209 us -> none  [project_rows(): return lax.psum(projected, 'inp')]
    dot_general x17 -> x4, matrix products: 153 us -> 3.86 us  [the longest x2 2.86 us: shards(): square = jnp.einsum('cma,cna->cmn', x, x, preferred_element_type=F32)]
    ppermute x4 -> x10, waiting for transfers between devices: 269 us -> 150 us  [the longest x2 51.9 us: shards(): rec = lax.ppermute(jnp.where(me == 0, down, up), 'h', cyclic(2, 1))]
    another operation x23 -> x0, other arithmetic: 90.6 us -> none  [the longest x13 49.9 us: subspace_clean(): lower_factor = jnp.linalg.cholesky(gram_matrix)]
    all_to_all x1 -> x2, starting transfers between devices: 98.1 us -> 20.5 us  [shards(): turned = lax.all_to_all(spec, FREQ, split_axis=0, concat_axis=0, tiled=True)]
    pallas_call x0 -> x4, Pallas kernels: none -> 57.6 us  [the longest x2 43.3 us: filter_dft(): pl.pallas_call(filter_dft_kernel, out_shape=jax.ShapeDtypeStruct((groups,...]
    psum x4 -> x0, blocking collectives: 42.7 us -> none  [subspace_clean(): gram_matrix = lax.psum(gram_matrix, 'inp')]
    all_to_all x1 -> x2, waiting for transfers between devices: 71.6 us -> 30.2 us  [shards(): turned = lax.all_to_all(spec, FREQ, split_axis=0, concat_axis=0, tiled=True)]
  transfers between devices with their start and end apart: 10 -> 12, of which waited for: 9 -> 7; matrix products, arithmetic and copies ran while one was open for 0% -> 7% of each run, Pallas kernels for 0% -> 12%
where the time goes in v1:
time: 361 us; the launch traced here: 360 us
  waiting for transfers between devices  180 us (50%)
  Pallas kernels  57.6 us (16%)
  starting transfers between devices  46.6 us (13%)
  local copies, waits for them, and re-layouts  40.1 us (11%)
  other arithmetic  22.8 us (6%)
  blocking collectives  7.76 us (2%)
  matrix products  3.86 us (1%)
    ppermute x2, waiting for transfers between devices, shards(): rec = lax.ppermute(jnp.where(me == 0, down, up), 'h', cyclic(2, 1))  51.9 us
    ppermute x2, waiting for transfers between devices, shards(): par = lax.ppermute(own, 'h', cyclic(2, 1))  47 us
    pallas_call x2, Pallas kernels, filter_dft(): pl.pallas_call(filter_dft_kernel, out_shape=jax.ShapeDtypeStruct((groups,...  43.3 us
    all_to_all x2, waiting for transfers between devices, shards(): turned = lax.all_to_all(spec, FREQ, split_axis=0, concat_axis=0, tiled=True)  30.2 us
    ppermute x2, waiting for transfers between devices, shards(): up = lax.ppermute(own, ('y', 'z'), cyclic(rings, 1))  29.3 us
    ppermute x2, waiting for transfers between devices, reduce_inputs(): gram = keep + lax.ppermute(send, axis, cyclic(2, 1))  22 us
    all_to_all x2, starting transfers between devices, shards(): turned = lax.all_to_all(spec, FREQ, split_axis=0, concat_axis=0, tiled=True)  20.5 us
    ppermute x2, starting transfers between devices, shards(): down = lax.ppermute(own, ('y', 'z'), cyclic(rings, -1))  11.2 us
  transfers between devices with their start and end apart: 12, of which 7 were waited for; matrix products, arithmetic and copies ran while one was open for 7% of the time, Pallas kernels for 12%

profile of v1, /device:TPU:1, one launch (start us, length us, event | category | flops | bytes accessed | tf_op | source)
XLA Modules:
  0.0 360.0 jit_solution(8633878356351357580)
XLA Ops:
  0.6 3.3 convert_element_type.22
  3.9 2.2 fusion.15
  6.1 2.5 collective-permute-start
  8.6 6.4 %collective-permute-start.1 = (bf16[3,2048,128]{2,1,0:T(8,128)(2,1)}, bf16[3,2048,128]{2,1,0:T(8,128)(2,1)S(1)}, u32[]{:S(2)}, u32[]{:S(2)}) collective-permute-start(bf16[3,2048,128]{2,1,0:T(8,128)(2,1)} %get-tuple-element.23), channel_id=1, source_target_pairs={{0,248},{8,0},{16,8},{24,16},{32,24},{40,32},{48,40},{56,48},{64,5... | collective-permute-start | bytes 4718600 | tf_op jit(solution)/shard_map/ppermute | solution.py:280
  15.0 2.7 collective-permute-start.2
  18.1 1.9 fusion.7
  20.0 29.3 %collective-permute-done = bf16[3,2048,128]{2,1,0:T(8,128)(2,1)S(1)} collective-permute-done((bf16[3,2048,128]{2,1,0:T(8,128)(2,1)}, bf16[3,2048,128]{2,1,0:T(8,128)(2,1)S(1)}, u32[]{:S(2)}, u32[]{:S(2)}) %collective-permute-start) | collective-permute-done | bytes 1572896 | tf_op jit(solution)/shard_map/ppermute | solution.py:279
  49.3 1.5 broadcast_select_fusion.1
  51.6 2.7 collective-permute-start.3
  54.4 3.2 subtract_bitcast_fusion.1
  57.6 4.8 %collective-permute-start.5 = (bf16[3,2048,128]{2,1,0:T(8,128)(2,1)}, bf16[3,2048,128]{2,1,0:T(8,128)(2,1)}, u32[]{:S(2)}, u32[]{:S(2)}) collective-permute-start(bf16[3,2048,128]{2,1,0:T(8,128)(2,1)} %get-tuple-element.13), channel_id=1, source_target_pairs={{0,248},{8,0},{16,8},{24,16},{32,24},{40,32},{48,40},{56,48},{64,5... | collective-permute-start | bytes 4718600 | tf_op jit(solution)/shard_map/ppermute | solution.py:280
  62.5 1.3 copy.12
  63.8 6.1 %fusion = (bf16[4,512,1024]{2,1,0:T(8,128)(2,1)}, bf16[4,512,1024]{2,1,0:T(8,128)(2,1)}) fusion(f32[1,512,1024]{2,1,0:T(8,128)} %get-tuple-element.28, f32[1,512,1024]{2,1,0:T(8,128)} %get-tuple-element.25, f32[1,512,1024]{2,1,0:T(8,128)} %get-tuple-element.29, f32[1,512,1024]{2,1,0:T(8,128)S(1)} %get-tuple-element.24), kind=kLoop, calls=%fused_computation.2 | loop fusion | flops 14680064 | bytes 16777216 | tf_op jit(solution)/shard_map/convert_element_type | solution.py:27
  69.9 18.2 %collective-permute-done.3 = bf16[3,2048,128]{2,1,0:T(8,128)(2,1)} collective-permute-done((bf16[3,2048,128]{2,1,0:T(8,128)(2,1)}, bf16[3,2048,128]{2,1,0:T(8,128)(2,1)}, u32[]{:S(2)}, u32[]{:S(2)}) %collective-permute-start.3) | collective-permute-done | bytes 1572896 | tf_op jit(solution)/shard_map/ppermute | solution.py:282
  88.1 21.6 %filter_dft.2 = bf16[64,16,768]{2,1,0:T(8,128)(2,1)} custom-call(bf16[3,2,1024,128]{3,2,1,0:T(8,128)(2,1)} %bitcast.42, bf16[3,2,1024,128]{3,2,1,0:T(8,128)(2,1)} %bitcast.1.own, bf16[3,2,1024,128]{3,2,1,0:T(8,128)(2,1)} %bitcast.43, bf16[3,2,1024,128]{3,2,1,0:T(8,128)(2,1)} %bitcast.3.par, bf16[3,2,1024,128]{3,2,1,0:T(8,128)(2,1)} %bitcast.4.rec, ...), custom_call_target="tpu_custom_call" | custom-call | tf_op jit(solution)/shard_map/filter_dft/pallas_call | solution.py:113
  109.7 8.3 %all-to-all-start = ((bf16[64,16,768]{2,1,0:T(8,128)(2,1)}), bf16[64,16,768]{2,1,0:T(8,128)(2,1)S(1)}, u32[]{:S(2)}, u32[]{:S(2)}) async-start(bf16[64,16,768]{2,1,0:T(8,128)(2,1)} %filter_dft.2), calls=%async_computation | async-start | bytes 3145728 | tf_op jit(solution)/shard_map/all_to_all | solution.py:285
  118.1 2.6 collective-permute-start.6
  120.7 1.6 broadcast_select_fusion
  122.8 46.9 %collective-permute-done.6 = bf16[3,2048,128]{2,1,0:T(8,128)(2,1)S(1)} collective-permute-done((bf16[3,2048,128]{2,1,0:T(8,128)(2,1)}, bf16[3,2048,128]{2,1,0:T(8,128)(2,1)S(1)}, u32[]{:S(2)}, u32[]{:S(2)}) %collective-permute-start.6) | collective-permute-done | bytes 1572896 | tf_op jit(solution)/shard_map/ppermute | solution.py:281
  169.8 33.7 %collective-permute-done.7 = bf16[3,2048,128]{2,1,0:T(8,128)(2,1)S(1)} collective-permute-done((bf16[3,2048,128]{2,1,0:T(8,128)(2,1)S(1)}, bf16[3,2048,128]{2,1,0:T(8,128)(2,1)S(1)}, u32[]{:S(2)}, u32[]{:S(2)}) %collective-permute-start.7) | collective-permute-done | bytes 1572896 | tf_op jit(solution)/shard_map/ppermute | solution.py:282
  203.5 1.2 copy-done.8
  204.7 21.6 %filter_dft.3 = bf16[64,16,768]{2,1,0:T(8,128)(2,1)} custom-call(bf16[3,2,1024,128]{3,2,1,0:T(8,128)(2,1)} %bitcast.13.up, bf16[3,2,1024,128]{3,2,1,0:T(8,128)(2,1)} %bitcast.14.own, bf16[3,2,1024,128]{3,2,1,0:T(8,128)(2,1)} %bitcast.15.down, bf16[3,2,1024,128]{3,2,1,0:T(8,128)(2,1)} %bitcast.48, bf16[3,2,1024,128]{3,2,1,0:T(8,128)(2,1)} %bitcast.49, ...), custom_call_target="tpu_custom_call" | custom-call | tf_op jit(solution)/shard_map/filter_dft/pallas_call | solution.py:113
  226.3 12.2 %all-to-all-start.1 = ((bf16[64,16,768]{2,1,0:T(8,128)(2,1)}), bf16[64,16,768]{2,1,0:T(8,128)(2,1)S(1)}, u32[]{:S(2)}, u32[]{:S(2)}) async-start(bf16[64,16,768]{2,1,0:T(8,128)(2,1)} %filter_dft.3), calls=%async_computation.1 | async-start | bytes 3145728 | tf_op jit(solution)/shard_map/all_to_all | solution.py:285
  239.2 2.6 copy.27
  241.8 2.8 reshape.271.refs_0_
  245.1 2.3 fusion.17
  247.4 30.2 %all-to-all-done.1 = bf16[64,16,768]{2,1,0:T(8,128)(2,1)S(1)} async-done(((bf16[64,16,768]{2,1,0:T(8,128)(2,1)}), bf16[64,16,768]{2,1,0:T(8,128)(2,1)S(1)}, u32[]{:S(2)}, u32[]{:S(2)}) %all-to-all-start.1) | async-done | bytes 1572896 | tf_op jit(solution)/shard_map/all_to_all | solution.py:285
  277.6 2.6 copy.26
  280.2 2.8 reshape.278.refs_1_
  285.4 1.7 copy-done.2
  287.1 1.3 constant_dynamic-slice_fusion.1
  288.3 2.7 copy.17
  291.0 3.4 collective-permute-start.8
  294.4 3.4 collective-permute-done.8
  297.7 2.7 copy.18
  300.4 2.1 dynamic-slice_add_fusion
  302.6 1.2 copy-done.4
  303.7 1.0 constant_dynamic-slice_fusion
  304.7 2.4 copy.19
  307.6 18.6 %collective-permute-done.9 = f32[4,200,192]{1,2,0:T(8,128)} collective-permute-done((f32[4,200,192]{1,2,0:T(8,128)}, f32[4,200,192]{1,2,0:T(8,128)}, u32[]{:S(2)}, u32[]{:S(2)}) %collective-permute-start.9) | collective-permute-done | bytes 614432 | tf_op jit(solution)/shard_map/ppermute | solution.py:239
  326.2 2.4 copy.20
  328.5 1.5 dynamic-slice_add_fusion.1.g
  330.1 5.4 %iterate.1 = f32[4,16,192]{2,1,0:T(8,128)S(1)} custom-call(f32[4,200,192]{2,1,0:T(8,128)S(1)} %dynamic-slice_add_fusion.1.g), custom_call_target="tpu_custom_call" | custom-call | tf_op jit(solution)/shard_map/iterate/pallas_call | solution.py:171
  335.5 3.8 %all_gather.6 = f32[8,16,192]{2,1,0:T(8,128)S(1)} all-gather(f32[4,16,192]{2,1,0:T(8,128)S(1)} %iterate.1), channel_id=1, replica_groups=mesh['y'=4,'z'=8,'h'=2,'l'=2,'k'=2] {'l'}, dimensions={0}, use_global_device_ids=true | all-gather | bytes 147456 | tf_op jit(solution)/shard_map/all_gather | solution.py:245
  339.3 4.0 %all_gather.7.refs_2_ = f32[16,16,192]{2,1,0:T(8,128)S(1)} all-gather(f32[8,16,192]{2,1,0:T(8,128)S(1)} %all_gather.6), channel_id=1, replica_groups=mesh['y'=4,'z'=8,'h'=2,'l'=2,'k'=2] {'k'}, dimensions={0}, use_global_device_ids=true | all-gather | bytes 294912 | tf_op jit(solution)/shard_map/all_gather | solution.py:245
  343.3 8.9 %clean.1 = (bf16[16,192,512]{2,1,0:T(8,128)(2,1)S(1)}, f32[16,8,8]{2,1,0:T(8,128)S(1)}) custom-call(bf16[16,192,256]{2,1,0:T(8,128)(2,1)S(1)} %reshape.271.refs_0_, bf16[16,192,256]{2,1,0:T(8,128)(2,1)S(1)} %reshape.278.refs_1_, f32[16,16,192]{2,1,0:T(8,128)S(1)} %all_gather.7.refs_2_, bf16[192,192]{1,0:T(8,128)(2,1)S(1)} %copy-done.1), custom_call_target="tpu_custom_call" | custom-call | tf_op jit(solution)/shard_map/clean/pallas_call | solution.py:211
  352.2 1.6 copy-done
  353.8 5.5 %reshape.281 = bf16[16,192,2,256]{3,2,1,0:T(2,128)(2,1)} reshape(bf16[16,192,512]{2,1,0:T(8,128)(2,1)} %copy-done) | data formatting | bytes 6291456 | tf_op jit(solution)/shard_map/reshape | solution.py:296
  (43 shorter events, 6.6 us)
Async XLA Ops:
  6.1 43.2 %collective-permute-start = (bf16[3,2048,128]{2,1,0:T(8,128)(2,1)}, bf16[3,2048,128]{2,1,0:T(8,128)(2,1)S(1)}, u32[]{:S(2)}, u32[]{:S(2)}) collective-permute-start(bf16[3,2048,128]{2,1,0:T(8,128)(2,1)} %get-tuple-element.23), channel_id=1, source_target_pairs={{0,8},{8,16},{16,24},{24,32},{32,40},{40,48},{48,56},{56,64},{64,7... | collective-permute-start | bytes 4718600 | tf_op jit(solution)/shard_map/ppermute | solution.py:279
  8.6 40.7 %collective-permute-start.1 = (bf16[3,2048,128]{2,1,0:T(8,128)(2,1)}, bf16[3,2048,128]{2,1,0:T(8,128)(2,1)S(1)}, u32[]{:S(2)}, u32[]{:S(2)}) collective-permute-start(bf16[3,2048,128]{2,1,0:T(8,128)(2,1)} %get-tuple-element.23), channel_id=1, source_target_pairs={{0,248},{8,0},{16,8},{24,16},{32,24},{40,32},{48,40},{56,48},{64,5... | collective-permute-start | bytes 4718600 | tf_op jit(solution)/shard_map/ppermute | solution.py:280
  15.0 54.9 %collective-permute-start.2 = (bf16[3,2048,128]{2,1,0:T(8,128)(2,1)}, bf16[3,2048,128]{2,1,0:T(8,128)(2,1)}, u32[]{:S(2)}, u32[]{:S(2)}) collective-permute-start(bf16[3,2048,128]{2,1,0:T(8,128)(2,1)} %get-tuple-element.23), channel_id=1, source_target_pairs={{0,4},{4,0},{1,5},{5,1},{2,6},{6,2},{3,7},{7,3},{8,12},{12,8},{9,1... | collective-permute-start | bytes 4718600 | tf_op jit(solution)/shard_map/ppermute | solution.py:281
  20.0 34.4 %copy-start.10 = (f32[12,2048]{1,0:T(8,128)S(1)}, f32[12,2048]{1,0:T(8,128)}, u32[]{:S(2)}) copy-start(f32[12,2048]{1,0:T(8,128)} %param.5) | copy-start | bytes 294916
  20.0 34.4 %copy-start.9 = (f32[64,1024]{1,0:T(8,128)S(1)}, f32[64,1024]{1,0:T(8,128)}, u32[]{:S(2)}) copy-start(f32[64,1024]{1,0:T(8,128)} %get-tuple-element.9) | copy-start | bytes 786436
  49.3 1.8 copy-start.5
  49.3 2.3 copy-start.6
  51.6 36.5 %collective-permute-start.3 = (bf16[3,2048,128]{2,1,0:T(8,128)(2,1)}, bf16[3,2048,128]{2,1,0:T(8,128)(2,1)}, u32[]{:S(2)}, u32[]{:S(2)}) collective-permute-start(bf16[3,2048,128]{2,1,0:T(8,128)(2,1)} %broadcast_select_fusion.1), channel_id=1, source_target_pairs={{0,4},{4,0},{1,5},{5,1},{2,6},{6,2},{3,7},{7,3},{8,12},{12,8},{9,1... | collective-permute-start | bytes 4718600 | tf_op jit(solution)/shard_map/ppermute | solution.py:282
  57.6 63.1 %collective-permute-start.4 = (bf16[3,2048,128]{2,1,0:T(8,128)(2,1)}, bf16[3,2048,128]{2,1,0:T(8,128)(2,1)}, u32[]{:S(2)}, u32[]{:S(2)}) collective-permute-start(bf16[3,2048,128]{2,1,0:T(8,128)(2,1)} %get-tuple-element.13), channel_id=1, source_target_pairs={{0,8},{8,16},{16,24},{24,32},{32,40},{40,48},{48,56},{56,64},{64,7... | collective-permute-start | bytes 4718600 | tf_op jit(solution)/shard_map/ppermute | solution.py:279
  57.6 63.1 %collective-permute-start.5 = (bf16[3,2048,128]{2,1,0:T(8,128)(2,1)}, bf16[3,2048,128]{2,1,0:T(8,128)(2,1)}, u32[]{:S(2)}, u32[]{:S(2)}) collective-permute-start(bf16[3,2048,128]{2,1,0:T(8,128)(2,1)} %get-tuple-element.13), channel_id=1, source_target_pairs={{0,248},{8,0},{16,8},{24,16},{32,24},{40,32},{48,40},{56,48},{64,5... | collective-permute-start | bytes 4718600 | tf_op jit(solution)/shard_map/ppermute | solution.py:280
  109.7 116.5 %all-to-all-start = ((bf16[64,16,768]{2,1,0:T(8,128)(2,1)}), bf16[64,16,768]{2,1,0:T(8,128)(2,1)S(1)}, u32[]{:S(2)}, u32[]{:S(2)}) async-start(bf16[64,16,768]{2,1,0:T(8,128)(2,1)} %filter_dft.2), calls=%async_computation | async-start | bytes 3145728 | tf_op jit(solution)/shard_map/all_to_all | solution.py:285
  118.1 51.7 %collective-permute-start.6 = (bf16[3,2048,128]{2,1,0:T(8,128)(2,1)}, bf16[3,2048,128]{2,1,0:T(8,128)(2,1)S(1)}, u32[]{:S(2)}, u32[]{:S(2)}) collective-permute-start(bf16[3,2048,128]{2,1,0:T(8,128)(2,1)} %get-tuple-element.13), channel_id=1, source_target_pairs={{0,4},{4,0},{1,5},{5,1},{2,6},{6,2},{3,7},{7,3},{8,12},{12,8},{9,1... | collective-permute-start | bytes 4718600 | tf_op jit(solution)/shard_map/ppermute | solution.py:281
  122.3 81.2 %collective-permute-start.7 = (bf16[3,2048,128]{2,1,0:T(8,128)(2,1)S(1)}, bf16[3,2048,128]{2,1,0:T(8,128)(2,1)S(1)}, u32[]{:S(2)}, u32[]{:S(2)}) collective-permute-start(bf16[3,2048,128]{2,1,0:T(8,128)(2,1)S(1)} %broadcast_select_fusion), channel_id=1, source_target_pairs={{0,4},{4,0},{1,5},{5,1},{2,6},{6,2},{3,7},{7,3},{8,12},{12,8},{9,1... | collective-permute-start | bytes 4718600 | tf_op jit(solution)/shard_map/ppermute | solution.py:282
  169.8 33.7 %copy-start.7 = (bf16[3,2048,128]{2,1,0:T(8,128)(2,1)}, bf16[3,2048,128]{2,1,0:T(8,128)(2,1)S(1)}, u32[]{:S(2)}) copy-start(bf16[3,2048,128]{2,1,0:T(8,128)(2,1)S(1)} %collective-permute-done.6) | copy-start | bytes 4718596
  203.5 1.2 copy-start.8
  226.3 51.3 %all-to-all-start.1 = ((bf16[64,16,768]{2,1,0:T(8,128)(2,1)}), bf16[64,16,768]{2,1,0:T(8,128)(2,1)S(1)}, u32[]{:S(2)}, u32[]{:S(2)}) async-start(bf16[64,16,768]{2,1,0:T(8,128)(2,1)} %filter_dft.3), calls=%async_computation.1 | async-start | bytes 3145728 | tf_op jit(solution)/shard_map/all_to_all | solution.py:285
  283.0 1.9 copy-start.3
  285.4 1.7 copy-start.2
  291.0 6.7 %collective-permute-start.8 = (f32[8,200,192]{1,2,0:T(8,128)}, f32[8,200,192]{1,2,0:T(8,128)}, u32[]{:S(2)}, u32[]{:S(2)}) collective-permute-start(f32[8,200,192]{1,2,0:T(8,128)} %copy.17), channel_id=1, source_target_pairs={{0,1},{1,0},{2,3},{3,2},{4,5},{5,4},{6,7},{7,6},{8,9},{9,8},{10,11... | collective-permute-start | bytes 3686408 | tf_op jit(solution)/shard_map/ppermute | solution.py:239
  302.6 1.2 copy-start.4
  307.1 19.1 %collective-permute-start.9 = (f32[4,200,192]{1,2,0:T(8,128)}, f32[4,200,192]{1,2,0:T(8,128)}, u32[]{:S(2)}, u32[]{:S(2)}) collective-permute-start(f32[4,200,192]{1,2,0:T(8,128)} %copy.19), channel_id=1, source_target_pairs={{0,2},{2,0},{1,3},{3,1},{4,6},{6,4},{5,7},{7,5},{8,10},{10,8},{9,1... | collective-permute-start | bytes 1843208 | tf_op jit(solution)/shard_map/ppermute | solution.py:239
  328.5 14.7 %copy-start.1 = (bf16[192,192]{1,0:T(8,128)(2,1)S(1)}, bf16[192,192]{1,0:T(8,128)(2,1)}, u32[]{:S(2)}) copy-start(bf16[192,192]{1,0:T(8,128)(2,1)} %constant.56.clone.refs_3_) | copy-start | bytes 221188
  352.2 1.6 copy-start

commit v2 on v1

v2 whole, which is shorter than its diff:
```python
import math

import jax
import jax.numpy as jnp
import numpy as np
from jax import lax
from jax.experimental import pallas as pl
from jax.experimental.pallas import tpu as pltpu
from jax.sharding import Mesh, PartitionSpec as P

ITERS = 4
FREQ = ("y", "z", "h")
INP = ("l", "k")
LANES = 128
SLOTS = 3
SHIFT = 5
BF = jnp.bfloat16
F32 = jnp.float32


def cyclic(count, steps):
    return [(i, (i + steps) % count) for i in range(count)]


def split2(value):
    high = lax.reduce_precision(value, 8, 7)
    return high.astype(BF), (value - high).astype(BF)


def dft_tables(frame_len, groups):
    half = frame_len // 2
    per = half // groups
    unit = 2.0 * math.pi / frame_len
    scale = 1.0 / math.sqrt(half)
    n_a = lax.broadcasted_iota(jnp.int32, (groups, half), 1)
    f_a = lax.broadcasted_iota(jnp.int32, (groups, half), 0)
    ang_a = ((f_a * per * n_a) % frame_len).astype(F32) * unit
    n_b = lax.broadcasted_iota(jnp.int32, (per, half), 1)
    j_b = lax.broadcasted_iota(jnp.int32, (per, half), 0)
    ang_b = ((j_b * n_b) % frame_len).astype(F32) * unit
    ca, sa = lax.optimization_barrier((jnp.cos(ang_a), jnp.sin(ang_a)))
    cb, sb = lax.optimization_barrier((jnp.cos(ang_b) * scale, jnp.sin(ang_b) * scale))
    rows = []
    for par in range(2):
        for kind in range(2):
            c2, s2 = cb[par::2][None], sb[par::2][None]
            c1, s1 = ca[:, None], sa[:, None]
            table = c1 * c2 - s1 * s2 if kind == 0 else -(s1 * c2 + c1 * s2)
            rows.append(table.reshape(groups * (per // 2), half))
    return split2(jnp.stack(rows).reshape(2, half, half))


def filter_kernel(side, up_own, up_rec, own, rec, down_own, down_rec, coef, kept, sent):
    step = 16
    pair = 2 * SLOTS

    def run(first, second, mine):
        def body(idx, carry):
            rows = pl.ds(pl.multiple_of(idx * step, step), step)
            cols = coef[rows, :]
            taps = [jnp.broadcast_to(cols[:, t : t + 1], (step, LANES)) for t in range(12)]
            acc = [None] * pair
            for block in range(3):
                for half in range(2):
                    ref = (first, second)[half][block]
                    for a in range(SLOTS):
                        at = pair * block + SLOTS * half + a
                        frame = ref[a, rows, :].astype(F32)
                        for j in range(pair):
                            t = at - j + SHIFT - 5
                            if 0 <= t < 12:
                                term = taps[t] * frame
                                acc[j] = term if acc[j] is None else acc[j] + term
            for r in range(SLOTS):
                kept[r, rows, :] = acc[SLOTS * mine + r]
                sent[r, rows, :] = acc[SLOTS * (1 - mine) + r]
            return carry

        lax.fori_loop(0, own.shape[1] // step, body, 0, unroll=2)

    mine = (up_own, own, down_own)
    other = (up_rec, rec, down_rec)

    @pl.when(side[0] == 0)
    def _():
        run(mine, other, 0)

    @pl.when(side[0] != 0)
    def _():
        run(other, mine, 1)


def filtered(side, blocks, coef):
    shape = jax.ShapeDtypeStruct(blocks[0].shape, F32)
    in_vmem = pl.BlockSpec(memory_space=pltpu.VMEM)
    return pl.pallas_call(
        filter_kernel,
        out_shape=(shape, shape),
        in_specs=[pl.BlockSpec(memory_space=pltpu.SMEM)] + [in_vmem] * 7,
        out_specs=(in_vmem, in_vmem),
        compiler_params=pltpu.CompilerParams(vmem_limit_bytes=4 << 20),
        cost_estimate=pl.CostEstimate(flops=40_000_000_000, transcendentals=0, bytes_accessed=0),
        name="filter",
    )(side, *blocks, coef)


def dft_kernel(side, own, rec, wh, wl, out, fold):
    half = own.shape[1]
    step = 16
    width = SLOTS * LANES
    sign = jnp.where(side[0] == 0, 1.0, -1.0)

    def body(idx, carry):
        rows = pl.ds(pl.multiple_of(idx * step, step), step)
        for r in range(SLOTS):
            one, two = own[r, rows, :], rec[r, rows, :]
            for parity in range(2):
                value = one + two if parity == 0 else (one - two) * sign
                top = value.astype(BF)
                rest = (value - top.astype(F32)).astype(BF)
                fold[parity, rows, r * LANES : (r + 1) * LANES] = top
                fold[parity, rows, width + r * LANES : width + (r + 1) * LANES] = rest
        return carry

    lax.fori_loop(0, half // step, body, 0, unroll=2)
    groups, per, _ = out.shape
    parts = []
    for parity in range(2):
        full = jnp.dot(wh[parity], fold[parity], preferred_element_type=F32)
        rest = jnp.dot(wl[parity], fold[parity, :, :width], preferred_element_type=F32)
        total = full[:, :width] + full[:, width:] + rest
        parts.append(total.reshape(2, groups, per // 2, width))
    for kind in range(2):
        both = jnp.concatenate([parts[0][kind], parts[1][kind]], axis=1).astype(BF)
        out[:, :, kind * width : (kind + 1) * width] = both


def dft(side, own, rec, table_h, table_l, groups):
    half = own.shape[1]
    width = SLOTS * LANES
    in_vmem = pl.BlockSpec(memory_space=pltpu.VMEM)
    return pl.pallas_call(
        dft_kernel,
        out_shape=jax.ShapeDtypeStruct((groups, half // groups, 2 * width), BF),
        in_specs=[pl.BlockSpec(memory_space=pltpu.SMEM)] + [in_vmem] * 4,
        out_specs=in_vmem,
        scratch_shapes=[pltpu.VMEM((2, half, 2 * width), BF)],
        compiler_params=pltpu.CompilerParams(vmem_limit_bytes=16 << 20),
        cost_estimate=pl.CostEstimate(flops=40_000_000_000, transcendentals=0, bytes_accessed=0),
        name="dft",
    )(side, own, rec, table_h, table_l)


NT = (((1,), (1,)), ((), ()))


def gram_kernel(place, turned, begin, order, *refs):
    before = refs[0] if len(refs) == 3 else None
    x_out, packed = refs[-2:]
    groups, per, _ = turned.shape
    spectra = x_out.shape[1]
    block = begin.shape[0]
    tile = order.shape[0] // per
    for base in range(0, groups, tile):
        rows = turned[base : base + tile].reshape(tile * per, -1)
        rows = jnp.dot(order[...], rows, preferred_element_type=F32).astype(BF)
        for c in range(per):
            for part in range(2):
                for r in range(SLOTS):
                    lane = (part * SLOTS + r) * LANES
                    at = r * groups + base
                    x_out[c, at : at + tile, part * LANES : (part + 1) * LANES] = rows[
                        c * tile : (c + 1) * tile, lane : lane + LANES
                    ]
    cut = min(spectra, LANES)
    tail = spectra - cut
    quarter = per // 4
    dot = lambda a, b: lax.dot_general(a, b, NT, preferred_element_type=F32)
    for c in range(per):
        top = (c // (2 * quarter) + place[0]) % 2
        low = ((c // quarter) % 2 + place[1]) % 2
        pos = top * (2 * quarter) + low * quarter + c % quarter

        def put(r0, r1, l0, l1, value):
            if before is not None:
                value = value + before[pos, r0:r1, l0:l1]
            packed[pos, r0:r1, l0:l1] = value

        x = x_out[c]
        put(0, spectra, 0, cut, dot(x, x[:cut]))
        first = dot(begin[...], x)
        at = spectra + tail // 2
        put(at, at + block, 0, cut, first[:, :cut])
        if tail:
            corner = dot(x[cut:], x[cut:])
            put(spectra, at, 0, tail, corner[: tail // 2])
            put(spectra, at, tail, 2 * tail, corner[tail // 2 :])
            put(at + block, at + 2 * block, 0, tail, first[:, cut:])


def packed_rows(spectra, block):
    return spectra + max(spectra - LANES, 0) // 2 + 2 * block


def gram(place, turned, begin, before):
    groups, per, _ = turned.shape
    spectra = groups * SLOTS
    block = begin.shape[0]
    tile = min(16, groups)
    order = np.zeros((per, tile, tile, per), np.float32)
    for c in range(per):
        for src in range(tile):
            order[c, src, src, (c % 2) * (per // 2) + c // 2] = 1.0
    order = jnp.asarray(order.reshape(per * tile, per * tile), BF)
    in_vmem = pl.BlockSpec(memory_space=pltpu.VMEM)
    operands = [turned, begin, order] + ([] if before is None else [before])
    return pl.pallas_call(
        gram_kernel,
        out_shape=(
            jax.ShapeDtypeStruct((per, spectra, 2 * LANES), BF),
            jax.ShapeDtypeStruct((per, packed_rows(spectra, block), LANES), F32),
        ),
        in_specs=[pl.BlockSpec(memory_space=pltpu.SMEM)] + [in_vmem] * len(operands),
        out_specs=(in_vmem, in_vmem),
        compiler_params=pltpu.CompilerParams(vmem_limit_bytes=10 << 20),
        cost_estimate=pl.CostEstimate(flops=10_000_000_000, transcendentals=0, bytes_accessed=0),
        name="gram",
    )(place, *operands)


def split3(value):
    first = value.astype(BF)
    left = value - first.astype(F32)
    second = left.astype(BF)
    third = (left - second.astype(F32)).astype(BF)
    return first, second, third


def wide_dot(a, b, dims):
    return lax.dot_general(
        a, b, (dims, ((), ())), precision=lax.Precision.HIGHEST, preferred_element_type=F32
    )


def unpack(packed, spectra, block):
    cut = min(spectra, LANES)
    tail = spectra - cut
    square = packed[:spectra, :cut]
    if not tail:
        return square, packed[spectra : spectra + block, :cut]
    at = spectra + tail // 2
    corner = packed[spectra:at, : 2 * tail]
    corner = jnp.concatenate([corner[:, :tail], corner[:, tail:]], axis=0)
    side = jnp.concatenate([square[cut:].T, corner], axis=0)
    first = jnp.concatenate(
        [packed[at : at + block, :cut], packed[at + block : at + 2 * block, :tail]], axis=1
    )
    return jnp.concatenate([square, side], axis=1), first


def iterate_kernel(gram_ref, out, *, spectra):
    count = gram_ref.shape[0]
    block = out.shape[1] // 2
    inverse = 1.0 / spectra
    rows = lax.broadcasted_iota(jnp.int32, (block, 1), 0)
    both = [unpack(gram_ref[c], spectra, block) for c in range(count)]
    covs = [pair[0] for pair in both]
    proj = [pair[1] for pair in both]
    coef = [None] * count
    for iteration in range(ITERS):
        mapped = [wide_dot(proj[c], covs[c], ((1,), (0,))) * inverse for c in range(count)]
        gram = [wide_dot(mapped[c], proj[c], ((1,), (1,))) * inverse for c in range(count)]
        before = [proj[c] * inverse for c in range(count)]
        scale = [jnp.zeros((block, 1), F32)] * count
        for j in range(block):
            for c in range(count):
                pivot = gram[c][j : j + 1, j : j + 1]
                factor = jnp.where(rows > j, gram[c][:, j : j + 1] / pivot, 0.0)
                scale[c] = jnp.where(rows == j, 1.0 / jnp.sqrt(pivot), scale[c])
                gram[c] = gram[c] - factor * gram[c][j : j + 1, :]
                mapped[c] = mapped[c] - factor * mapped[c][j : j + 1, :]
                before[c] = before[c] - factor * before[c][j : j + 1, :]
        proj = [mapped[c] * scale[c] for c in range(count)]
        coef = [before[c] * scale[c] for c in range(count)]
    for c in range(count):
        out[c, :block, :] = coef[c]
        out[c, block:, :] = wide_dot(coef[c], covs[c], ((1,), (0,)))


def iterate(gram, spectra, block):
    count = gram.shape[0]
    return pl.pallas_call(
        lambda g, o: iterate_kernel(g, o, spectra=spectra),
        out_shape=jax.ShapeDtypeStruct((count, 2 * block, spectra), F32),
        compiler_params=pltpu.CompilerParams(vmem_limit_bytes=12 << 20),
        name="iterate",
    )(gram)


def clean_kernel(xa, xb, pair, perm, out, ritz):
    count, spectra, _ = xa.shape
    block = pair.shape[1] // 2
    order = perm[...]
    for c in range(count):
        coef = pair[c, :block, :]
        proj = pair[c, block:, :]
        ritz[c] = wide_dot(proj, proj, NT[0]) * (1.0 / spectra)
        coef3 = jnp.concatenate(split3(coef), axis=0)
        proj3 = jnp.concatenate(split3(proj), axis=0)
        turned = lax.dot_general(order, proj3, NT, preferred_element_type=F32)
        ph, pm, pt = [(-turned[:, i * block : (i + 1) * block]).astype(BF) for i in range(3)]
        left = jnp.concatenate([order, ph, ph, ph, pm, pm, pt], axis=1)
        for chunk, ref in enumerate((xa, xb)):
            x = ref[c]
            base = jnp.dot(coef3, x, preferred_element_type=F32)
            base = base[:block] + base[block : 2 * block] + base[2 * block :]
            bh, bm, bt = split3(base)
            right = jnp.concatenate([x, bh, bm, bt, bh, bm, bh], axis=0)
            result = jnp.dot(left, right, preferred_element_type=F32).astype(BF)
            for part in range(2):
                lane = part * 2 * LANES + chunk * LANES
                out[c, :, lane : lane + LANES] = result[:, part * LANES : (part + 1) * LANES]


def clean(xs, pair, spectra):
    channels = pair.shape[0]
    block = pair.shape[1] // 2
    width = 2 * LANES
    step = 4
    order = np.zeros((spectra, spectra), np.float32)
    groups = spectra // SLOTS
    for src in range(groups):
        for r in range(SLOTS):
            order[(SLOTS * src + r + SHIFT) % spectra, r * groups + src] = 1.0
    x_spec = pl.BlockSpec((step, spectra, width), lambda c: (c, 0, 0))
    return pl.pallas_call(
        clean_kernel,
        out_shape=(
            jax.ShapeDtypeStruct((channels, spectra, 2 * width), BF),
            jax.ShapeDtypeStruct((channels, block, block), F32),
        ),
        grid=(channels // step,),
        in_specs=[
            x_spec,
            x_spec,
            pl.BlockSpec((step, 2 * block, spectra), lambda c: (c, 0, 0)),
            pl.BlockSpec((spectra, spectra), lambda c: (0, 0)),
        ],
        out_specs=(
            pl.BlockSpec((step, spectra, 2 * width), lambda c: (c, 0, 0)),
            pl.BlockSpec((step, block, block), lambda c: (c, 0, 0)),
        ),
        compiler_params=pltpu.CompilerParams(vmem_limit_bytes=12 << 20),
        name="clean",
    )(*xs, pair, jnp.asarray(order, BF))


def reduce_inputs(packed):
    for axis in ("k", "l"):
        half = packed.shape[0] // 2
        packed = packed[:half] + lax.ppermute(packed[half:], axis, cyclic(2, 1))
    return packed


def gather_inputs(value):
    for axis in ("l", "k"):
        value = lax.all_gather(value, axis, tiled=True)
    return value


def shards(voltages, taps, start):
    slots, frame_len, inputs = voltages.shape
    half = frame_len // 2
    block = start.shape[0]
    groups = lax.axis_size("y") * lax.axis_size("z") * 2
    rings = groups // 2
    spectra = groups * slots
    per = half // groups
    chunks = inputs // LANES
    me = lax.axis_index("h")
    side = me.reshape(1)
    k_index, l_index = lax.axis_index("k"), lax.axis_index("l")
    coef = lax.dynamic_slice_in_dim(taps.T, me * half, half, 0)
    table_h, table_l = dft_tables(frame_len, groups)

    def piece(chunk, which):
        at = (0, which * half, chunk * LANES)
        return lax.dynamic_slice(voltages, at, (slots, half, LANES)).astype(BF)

    def swap(value):
        return lax.ppermute(value, "h", cyclic(2, 1))

    def both_ways(value):
        return (
            lax.ppermute(value, ("y", "z"), cyclic(rings, 1)),
            lax.ppermute(value, ("y", "z"), cyclic(rings, -1)),
        )

    rank = l_index * 2 + k_index
    begin = lax.dynamic_slice_in_dim(start, rank * inputs, inputs, 2).astype(BF)
    begin = begin.reshape(block, 2, chunks, LANES).transpose(2, 0, 1, 3).reshape(chunks, block, -1)

    sums = []
    gate_x = gate_z = None
    for chunk in range(chunks):
        own, send = piece(chunk, me), piece(chunk, 1 - me)
        if gate_x is not None:
            own, send, _ = lax.optimization_barrier((own, send, gate_x))
        rec = swap(send)
        gate_x = rec
        moving = (own, rec)
        if gate_z is not None:
            moving = lax.optimization_barrier((own, rec) + gate_z)[:2]
        up_own, down_own = both_ways(moving[0])
        up_rec, down_rec = both_ways(moving[1])
        gate_z = (up_rec, down_rec)
        blocks = (up_own, up_rec, own, rec, down_own, down_rec)
        if chunk == 0:
            blocks, (table_h, table_l) = lax.optimization_barrier((blocks, (table_h, table_l)))
        sums.append(filtered(side, blocks, coef))
    turned = []
    for chunk in range(chunks):
        kept, sent = sums[chunk]
        back = swap(sent)
        if chunk + 1 < chunks:
            kept, back, later = lax.optimization_barrier((kept, back, sums[chunk + 1]))
            sums[chunk + 1] = later
        spec = dft(side, kept, back, table_h, table_l, groups)
        turned.append(lax.all_to_all(spec, FREQ, split_axis=0, concat_axis=0, tiled=True))
    place = jnp.stack([k_index, l_index])
    xs, packed = [], None
    for chunk in range(chunks):
        x, packed = gram(place, turned[chunk], begin[chunk], packed)
        xs.append(x)
    pair = gather_inputs(iterate(reduce_inputs(packed), spectra, block))
    cleaned, ritz = clean(xs, pair, spectra)
    return cleaned.reshape(per, spectra, 2, inputs), ritz


def on_mesh(mesh):
    return jax.shard_map(
        shards,
        mesh=mesh,
        in_specs=(P(FREQ, None, INP), P(), P()),
        out_specs=(P(FREQ, None, None, INP), P(FREQ, None, None)),
        check_vma=False,
    )


def solution(mesh):
    freq = mesh.shape["freq"]
    devices = mesh.devices.reshape(freq // 16, 8, 2, 2, 2)
    return on_mesh(Mesh(devices, FREQ + INP))
```

time: 361 us -> 254 us (0.70)
  waiting for transfers between devices: 180 us -> 117 us
  local copies, waits for them, and re-layouts: 40.1 us -> 15 us
  Pallas kernels: 57.6 us -> 44.5 us
  other arithmetic: 22.8 us -> 17.2 us
  starting transfers between devices: 46.6 us -> 51.8 us
  matrix products: 3.86 us -> 0 us
    ppermute x10 -> x14, waiting for transfers between devices: 150 us -> 91.3 us  [the longest x4 50.8 us: swap(): return lax.ppermute(value, 'h', cyclic(2, 1))]
    ppermute x10 -> x14, starting transfers between devices: 26.1 us -> 41.8 us  [the longest x4 20.7 us: both_ways(): lax.ppermute(value, ('y', 'z'), cyclic(rings, -1))]
    pallas_call x3 -> x7, Pallas kernels: 52.1 us -> 39 us  [the longest x2 15.4 us: dft(): pl.pallas_call(dft_kernel, out_shape=jax.ShapeDtypeStruct((groups, half /...]
    reshape x6 -> x2, local copies, waits for them, and re-layouts: 10.7 us -> 0.02 us  [shards(): begin.reshape(block, 2, chunks, LANES).transpose(2, 0, 1, 3)]
    all_to_all x2, starting transfers between devices: 20.5 us -> 10.1 us  [shards(): lax.all_to_all(spec, FREQ, split_axis=0, concat_axis=0, tiled=True)]
    dynamic_slice x4 -> x0, local copies, waits for them, and re-layouts: 7.3 us -> none  [reduce_inputs(): send = lax.dynamic_slice_in_dim(gram, (1 - me) * half, half, 0)]
    ppermute x2 -> x0, local copies, waits for them, and re-layouts: 5.05 us -> none  [reduce_inputs(): gram = keep + lax.ppermute(send, axis, cyclic(2, 1))]
    all_to_all x2, waiting for transfers between devices: 30.2 us -> 25.2 us  [shards(): lax.all_to_all(spec, FREQ, split_axis=0, concat_axis=0, tiled=True)]
  transfers between devices with their start and end apart: 12 -> 16, of which waited for: 7 -> 9; matrix products, arithmetic and copies ran while one was open for 7% -> 5% of each run, Pallas kernels for 12% -> 12%
where the time goes in v2:
time: 254 us
  waiting for transfers between devices  117 us (46%)
  starting transfers between devices  51.8 us (20%)
  Pallas kernels  44.5 us (18%)
  other arithmetic  17.2 us (7%)
  local copies, waits for them, and re-layouts  15 us (6%)
  blocking collectives  7.76 us (3%)
    ppermute x4, waiting for transfers between devices, swap(): return lax.ppermute(value, 'h', cyclic(2, 1))  50.8 us
    ppermute x4, waiting for transfers between devices, both_ways(): lax.ppermute(value, ('y', 'z'), cyclic(rings, 1))  26.2 us
    all_to_all x2, waiting for transfers between devices, shards(): lax.all_to_all(spec, FREQ, split_axis=0, concat_axis=0, tiled=True)  25.2 us
    ppermute x4, starting transfers between devices, both_ways(): lax.ppermute(value, ('y', 'z'), cyclic(rings, -1))  20.7 us
    pallas_call x2, Pallas kernels, dft(): pl.pallas_call(dft_kernel, out_shape=jax.ShapeDtypeStruct((groups, half /...  15.4 us
    ppermute x2, waiting for transfers between devices, reduce_inputs(): packed = packed[:half] + lax.ppermute(packed[half:], axis, cyclic(2, 1))  14.3 us
    pallas_call x2, Pallas kernels, filtered(): pl.pallas_call(filter_kernel, out_shape=(shape, shape), in_specs=[pl.Bloc...  13.6 us
    ppermute x2, starting transfers between devices, reduce_inputs(): packed = packed[:half] + lax.ppermute(packed[half:], axis, cyclic(2, 1))  12.5 us
  transfers between devices with their start and end apart: 16, of which 9 were waited for; matrix products, arithmetic and copies ran while one was open for 5% of the time, Pallas kernels for 12%

profile of v2, /device:TPU:1, one launch (start us, length us, event | category | flops | bytes accessed | tf_op | source)
XLA Modules:
  0.0 253.7 jit_solution(7177746341892245766)
XLA Ops:
  0.7 4.8 %dynamic-slice_convert_fusion = (bf16[3,1024,128]{2,1,0:T(8,128)(2,1)}, bf16[3,1024,128]{2,1,0:T(8,128)(2,1)}, bf16[3,1024,128]{2,1,0:T(8,128)(2,1)S(1)}, bf16[3,1024,128]{2,1,0:T(8,128)(2,1)S(1)}) fusion(s32[3,2048,256]{2,1,0:T(8,128)} %param.6, s32[]{:T(128)S(6)} %select_n.30, s32[]{:T(128)S(6)} %select_n.29), kind=kLoop, calls=%fused_computation.8 | loop fusion | flops 1572864 | bytes 9437192 | tf_op jit(solution)/shard_map/convert_element_type | solution.py:388
  5.4 2.5 collective-permute-start
  7.9 6.4 %collective-permute-start.3 = (bf16[3,1024,128]{2,1,0:T(8,128)(2,1)S(1)}, bf16[3,1024,128]{2,1,0:T(8,128)(2,1)}, u32[]{:S(2)}, u32[]{:S(2)}) collective-permute-start(bf16[3,1024,128]{2,1,0:T(8,128)(2,1)S(1)} %get-tuple-element.38.own), channel_id=1, source_target_pairs={{0,248},{8,0},{16,8},{24,16},{32,24},{40,32},{48,40},{56,48},{64,5... | collective-permute-start | bytes 2359304 | tf_op jit(solution)/shard_map/ppermute | solution.py:396
  14.3 2.7 %collective-permute-start.1 = (bf16[3,1024,128]{2,1,0:T(8,128)(2,1)}, bf16[3,1024,128]{2,1,0:T(8,128)(2,1)}, u32[]{:S(2)}, u32[]{:S(2)}) collective-permute-start(bf16[3,1024,128]{2,1,0:T(8,128)(2,1)} %get-tuple-element.69), channel_id=1, source_target_pairs={{0,4},{4,0},{1,5},{5,1},{2,6},{6,2},{3,7},{7,3},{8,12},{12,8},{9,1... | collective-permute-start | bytes 2359304 | tf_op jit(solution)/shard_map/ppermute | solution.py:391
  17.0 0.3 sine_multiply_fusion
  17.4 1.1 fusion.7
  18.5 1.3 subtract_bitcast_fusion.1
  19.7 14.4 %collective-permute-done.1.rec = bf16[3,1024,128]{2,1,0:T(8,128)(2,1)} collective-permute-done((bf16[3,1024,128]{2,1,0:T(8,128)(2,1)}, bf16[3,1024,128]{2,1,0:T(8,128)(2,1)}, u32[]{:S(2)}, u32[]{:S(2)}) %collective-permute-start.1) | collective-permute-done | bytes 786464 | tf_op jit(solution)/shard_map/ppermute | solution.py:391
  34.2 2.7 %collective-permute-start.6 = (bf16[3,1024,128]{2,1,0:T(8,128)(2,1)}, bf16[3,1024,128]{2,1,0:T(8,128)(2,1)}, u32[]{:S(2)}, u32[]{:S(2)}) collective-permute-start(bf16[3,1024,128]{2,1,0:T(8,128)(2,1)} %get-tuple-element.45), channel_id=1, source_target_pairs={{0,4},{4,0},{1,5},{5,1},{2,6},{6,2},{3,7},{7,3},{8,12},{12,8},{9,1... | collective-permute-start | bytes 2359304 | tf_op jit(solution)/shard_map/ppermute | solution.py:391
  36.9 4.8 %collective-permute-start.4 = (bf16[3,1024,128]{2,1,0:T(8,128)(2,1)}, bf16[3,1024,128]{2,1,0:T(8,128)(2,1)}, u32[]{:S(2)}, u32[]{:S(2)}) collective-permute-start(bf16[3,1024,128]{2,1,0:T(8,128)(2,1)} %collective-permute-done.1.rec), channel_id=1, source_target_pairs={{0,248},{8,0},{16,8},{24,16},{32,24},{40,32},{48,40},{56,48},{64,5... | collective-permute-start | bytes 2359304 | tf_op jit(solution)/shard_map/ppermute | solution.py:396
  41.7 3.6 %pad_maximum_fusion = f32[4,512,1024]{2,1,0:T(8,128)} fusion(f32[1,512,1024]{2,1,0:T(8,128)S(1)} %get-tuple-element.76, f32[1,512,1024]{2,1,0:T(8,128)S(1)} %get-tuple-element.77, f32[1,512,1024]{2,1,0:T(8,128)S(1)} %get-tuple-element.73, f32[1,512,1024]{2,1,0:T(8,128)S(1)} %get-tuple-element.72), kind=kLoop, calls=%fused_computation.3 | loop fusion | flops 6291456 | bytes 16777216 | tf_op jit(solution)/shard_map/stack | solution.py:50
  45.6 5.3 %fusion = (bf16[2,1024,1024]{2,1,0:T(8,128)(2,1)S(1)}, bf16[2,1024,1024]{2,1,0:T(8,128)(2,1)S(1)}) fusion(f32[2,1024,1024]{2,1,0:T(8,128)} %bitcast.25), kind=kLoop, calls=%fused_computation.2 | loop fusion | flops 8388608 | bytes 16777216 | tf_op jit(solution)/shard_map/convert_element_type | solution.py:27
  50.9 6.6 %collective-permute-done.2.up_rec = bf16[3,1024,128]{2,1,0:T(8,128)(2,1)} collective-permute-done((bf16[3,1024,128]{2,1,0:T(8,128)(2,1)}, bf16[3,1024,128]{2,1,0:T(8,128)(2,1)}, u32[]{:S(2)}, u32[]{:S(2)}) %collective-permute-start.2) | collective-permute-done | bytes 786464 | tf_op jit(solution)/shard_map/ppermute | solution.py:395
  57.5 4.8 %collective-permute-start.9 = (bf16[3,1024,128]{2,1,0:T(8,128)(2,1)S(1)}, bf16[3,1024,128]{2,1,0:T(8,128)(2,1)S(1)}, u32[]{:S(2)}, u32[]{:S(2)}) collective-permute-start(bf16[3,1024,128]{2,1,0:T(8,128)(2,1)S(1)} %get-tuple-element.46.own), channel_id=1, source_target_pairs={{0,248},{8,0},{16,8},{24,16},{32,24},{40,32},{48,40},{56,48},{64,5... | collective-permute-start | bytes 2359304 | tf_op jit(solution)/shard_map/ppermute | solution.py:396
  62.3 4.8 %collective-permute-start.10 = (bf16[3,1024,128]{2,1,0:T(8,128)(2,1)}, bf16[3,1024,128]{2,1,0:T(8,128)(2,1)S(1)}, u32[]{:S(2)}, u32[]{:S(2)}) collective-permute-start(bf16[3,1024,128]{2,1,0:T(8,128)(2,1)} %collective-permute-done.6.rec), channel_id=1, source_target_pairs={{0,248},{8,0},{16,8},{24,16},{32,24},{40,32},{48,40},{56,48},{64,5... | collective-permute-start | bytes 2359304 | tf_op jit(solution)/shard_map/ppermute | solution.py:396
  67.0 6.6 %filter.2 = (f32[3,1024,128]{2,1,0:T(8,128)S(1)}, f32[3,1024,128]{2,1,0:T(8,128)S(1)}) custom-call(s32[1]{0:T(128)} %bitcast.2.side, bf16[3,1024,128]{2,1,0:T(8,128)(2,1)S(1)} %collective-permute-done.up_own, bf16[3,1024,128]{2,1,0:T(8,128)(2,1)} %collective-permute-done.2.up_rec, bf16[3,1024,128]{2,1,0:T(8,128)(2,1)S(1)} %get-tuple-element.38.own, ...), custom_call_target="tpu_custom_call" | custom-call | flops 40000000000 | tf_op jit(solution)/shard_map/filter/pallas_call | solution.py:96
  73.6 0.3 collective-permute-start.5
  74.0 2.8 %collective-permute-done.7.up_own = bf16[3,1024,128]{2,1,0:T(8,128)(2,1)S(1)} collective-permute-done((bf16[3,1024,128]{2,1,0:T(8,128)(2,1)S(1)}, bf16[3,1024,128]{2,1,0:T(8,128)(2,1)S(1)}, u32[]{:S(2)}, u32[]{:S(2)}) %collective-permute-start.7) | collective-permute-done | bytes 786464 | tf_op jit(solution)/shard_map/ppermute | solution.py:395
  76.7 16.9 %collective-permute-done.8.up_rec = bf16[3,1024,128]{2,1,0:T(8,128)(2,1)S(1)} collective-permute-done((bf16[3,1024,128]{2,1,0:T(8,128)(2,1)}, bf16[3,1024,128]{2,1,0:T(8,128)(2,1)S(1)}, u32[]{:S(2)}, u32[]{:S(2)}) %collective-permute-start.8) | collective-permute-done | bytes 786464 | tf_op jit(solution)/shard_map/ppermute | solution.py:395
  93.6 7.0 %filter.3 = (f32[3,1024,128]{2,1,0:T(8,128)S(1)}, f32[3,1024,128]{2,1,0:T(8,128)}) custom-call(s32[1]{0:T(128)} %bitcast.2.side, bf16[3,1024,128]{2,1,0:T(8,128)(2,1)S(1)} %collective-permute-done.7.up_own, bf16[3,1024,128]{2,1,0:T(8,128)(2,1)S(1)} %collective-permute-done.8.up_rec, bf16[3,1024,128]{2,1,0:T(8,128)(2,1)S(1)} %get-tuple-element.46.own, ...), custom_call_target="tpu_custom_call" | custom-call | flops 40000000000 | tf_op jit(solution)/shard_map/filter/pallas_call | solution.py:96
  100.7 1.1 copy-done.12
  101.8 5.1 %collective-permute-done.5.rec = f32[3,1024,128]{2,1,0:T(8,128)S(1)} collective-permute-done((f32[3,1024,128]{2,1,0:T(8,128)S(1)}, f32[3,1024,128]{2,1,0:T(8,128)S(1)}, u32[]{:S(2)}, u32[]{:S(2)}) %collective-permute-start.5) | collective-permute-done | bytes 1572896 | tf_op jit(solution)/shard_map/ppermute | solution.py:391
  106.9 0.2 collective-permute-start.11
  107.2 7.7 %dft.2 = bf16[64,16,768]{2,1,0:T(8,128)(2,1)} custom-call(s32[1]{0:T(128)} %bitcast.2.side, f32[3,1024,128]{2,1,0:T(8,128)S(1)} %get-tuple-element.50.own, f32[3,1024,128]{2,1,0:T(8,128)S(1)} %collective-permute-done.5.rec, bf16[2,1024,1024]{2,1,0:T(8,128)(2,1)S(1)} %get-tuple-element.52.wh, bf16[2,1024,1024]{2,1,0:T(8,128)(2,1)S(1)} %get-tuple-element.53.wl), custom_call_target="tpu_custom_call" | custom-call | flops 40000000000 | tf_op jit(solution)/shard_map/dft/pallas_call | solution.py:142
  114.9 5.0 %all-to-all-start = ((bf16[64,16,768]{2,1,0:T(8,128)(2,1)}), bf16[64,16,768]{2,1,0:T(8,128)(2,1)S(1)}, u32[]{:S(2)}, u32[]{:S(2)}) async-start(bf16[64,16,768]{2,1,0:T(8,128)(2,1)} %dft.2), calls=%async_computation | async-start | bytes 3145728 | tf_op jit(solution)/shard_map/all_to_all | solution.py:429
  119.9 31.2 %collective-permute-done.11.rec = f32[3,1024,128]{2,1,0:T(8,128)S(1)} collective-permute-done((f32[3,1024,128]{2,1,0:T(8,128)}, f32[3,1024,128]{2,1,0:T(8,128)S(1)}, u32[]{:S(2)}, u32[]{:S(2)}) %collective-permute-start.11) | collective-permute-done | bytes 1572896 | tf_op jit(solution)/shard_map/ppermute | solution.py:391
  151.1 2.2 copy-done.3
  153.3 2.2 copy-done.5
  155.5 1.4 copy-done.13
  156.9 7.7 %dft.3 = bf16[64,16,768]{2,1,0:T(8,128)(2,1)} custom-call(s32[1]{0:T(128)} %bitcast.2.side, f32[3,1024,128]{2,1,0:T(8,128)S(1)} %copy-done.13, f32[3,1024,128]{2,1,0:T(8,128)S(1)} %collective-permute-done.11.rec, bf16[2,1024,1024]{2,1,0:T(8,128)(2,1)S(1)} %copy-done.5, bf16[2,1024,1024]{2,1,0:T(8,128)(2,1)S(1)} %copy-done.3), custom_call_target="tpu_custom_call" | custom-call | flops 40000000000 | tf_op jit(solution)/shard_map/dft/pallas_call | solution.py:142
  164.7 5.0 %all-to-all-start.1 = ((bf16[64,16,768]{2,1,0:T(8,128)(2,1)}), bf16[64,16,768]{2,1,0:T(8,128)(2,1)S(1)}, u32[]{:S(2)}, u32[]{:S(2)}) async-start(bf16[64,16,768]{2,1,0:T(8,128)(2,1)} %dft.3), calls=%async_computation.1 | async-start | bytes 3145728 | tf_op jit(solution)/shard_map/all_to_all | solution.py:429
  169.7 0.7 dynamic-slice_convert_fusion.4
  170.5 2.3 gram.2
  172.8 1.2 copy-done.6
  174.0 1.3 copy-done.10
  175.3 25.2 %all-to-all-done.1.turned = bf16[64,16,768]{2,1,0:T(8,128)(2,1)S(1)} async-done(((bf16[64,16,768]{2,1,0:T(8,128)(2,1)}), bf16[64,16,768]{2,1,0:T(8,128)(2,1)S(1)}, u32[]{:S(2)}, u32[]{:S(2)}) %all-to-all-start.1) | async-done | bytes 1572896 | tf_op jit(solution)/shard_map/all_to_all | solution.py:429
  200.5 1.5 copy-done.11
  202.0 2.3 gram.3
  204.3 12.2 %collective-permute-start.12 = (f32[8,240,128]{2,1,0:T(8,128)S(1)}, f32[8,240,128]{2,1,0:T(8,128)S(1)}, u32[]{:S(2)}, u32[]{:S(2)}) collective-permute-start(f32[8,240,128]{2,1,0:T(8,128)S(1)} %slice.43), channel_id=1, source_target_pairs={{0,1},{1,0},{2,3},{3,2},{4,5},{5,4},{6,7},{7,6},{8,9},{9,8},{10,11... | collective-permute-start | bytes 2949128 | tf_op jit(solution)/shard_map/ppermute | solution.py:361
  216.5 2.2 collective-permute-done.12
  218.9 0.4 collective-permute-start.13
  219.3 12.1 %collective-permute-done.13 = f32[4,240,128]{2,1,0:T(8,128)S(1)} collective-permute-done((f32[4,240,128]{2,1,0:T(8,128)S(1)}, f32[4,240,128]{2,1,0:T(8,128)S(1)}, u32[]{:S(2)}, u32[]{:S(2)}) %collective-permute-start.13) | collective-permute-done | bytes 491552 | tf_op jit(solution)/shard_map/ppermute | solution.py:361
  231.4 5.5 %iterate.1 = f32[4,16,192]{2,1,0:T(8,128)S(1)} custom-call(f32[4,240,128]{2,1,0:T(8,128)S(1)} %slice_add_fusion.1.g), custom_call_target="tpu_custom_call" | custom-call | tf_op jit(solution)/shard_map/iterate/pallas_call | solution.py:292
  236.9 3.8 %all_gather.6 = f32[8,16,192]{2,1,0:T(8,128)S(1)} all-gather(f32[4,16,192]{2,1,0:T(8,128)S(1)} %iterate.1), channel_id=1, replica_groups=mesh['y'=4,'z'=8,'h'=2,'l'=2,'k'=2] {'l'}, dimensions={0}, use_global_device_ids=true | all-gather | bytes 147456 | tf_op jit(solution)/shard_map/all_gather | solution.py:367
  240.7 4.0 %all_gather.7.pair = f32[16,16,192]{2,1,0:T(8,128)S(1)} all-gather(f32[8,16,192]{2,1,0:T(8,128)S(1)} %all_gather.6), channel_id=1, replica_groups=mesh['y'=4,'z'=8,'h'=2,'l'=2,'k'=2] {'k'}, dimensions={0}, use_global_device_ids=true | all-gather | bytes 294912 | tf_op jit(solution)/shard_map/all_gather | solution.py:367
  244.7 5.4 %clean.1 = (bf16[16,192,512]{2,1,0:T(8,128)(2,1)S(1)}, f32[16,8,8]{2,1,0:T(8,128)S(1)}) custom-call(bf16[16,192,256]{2,1,0:T(8,128)(2,1)S(1)} %copy-done.7, bf16[16,192,256]{2,1,0:T(8,128)(2,1)S(1)} %get-tuple-element.58.xb, f32[16,16,192]{2,1,0:T(8,128)S(1)} %all_gather.7.pair, bf16[192,192]{1,0:T(8,128)(2,1)S(1)} %copy-done.8), custom_call_target="tpu_custom_call" | custom-call | tf_op jit(solution)/shard_map/clean/pallas_call | solution.py:336
  250.0 2.9 %reshape.230 = bf16[16,192,2,256]{3,2,1,0:T(2,128)(2,1)} reshape(bf16[16,192,512]{2,1,0:T(8,128)(2,1)S(1)} %get-tuple-element.60) | data formatting | bytes 6291456 | tf_op jit(solution)/shard_map/reshape | solution.py:437
  253.0 0.7 copy.13
  (46 shorter events, 0.7 us)
Async XLA Ops:
  0.6 44.7 %copy-start = (f32[12,2048]{1,0:T(8,128)S(1)}, f32[12,2048]{1,0:T(8,128)}, u32[]{:S(2)}) copy-start(f32[12,2048]{1,0:T(8,128)} %param.7) | copy-start | bytes 294916
  5.4 56.8 %collective-permute-start = (bf16[3,1024,128]{2,1,0:T(8,128)(2,1)S(1)}, bf16[3,1024,128]{2,1,0:T(8,128)(2,1)S(1)}, u32[]{:S(2)}, u32[]{:S(2)}) collective-permute-start(bf16[3,1024,128]{2,1,0:T(8,128)(2,1)S(1)} %get-tuple-element.38.own), channel_id=1, source_target_pairs={{0,8},{8,16},{16,24},{24,32},{32,40},{40,48},{48,56},{56,64},{64,7... | collective-permute-start | bytes 2359304 | tf_op jit(solution)/shard_map/ppermute | solution.py:395
  7.9 59.2 %collective-permute-start.3 = (bf16[3,1024,128]{2,1,0:T(8,128)(2,1)S(1)}, bf16[3,1024,128]{2,1,0:T(8,128)(2,1)}, u32[]{:S(2)}, u32[]{:S(2)}) collective-permute-start(bf16[3,1024,128]{2,1,0:T(8,128)(2,1)S(1)} %get-tuple-element.38.own), channel_id=1, source_target_pairs={{0,248},{8,0},{16,8},{24,16},{32,24},{40,32},{48,40},{56,48},{64,5... | collective-permute-start | bytes 2359304 | tf_op jit(solution)/shard_map/ppermute | solution.py:396
  14.3 19.9 %collective-permute-start.1 = (bf16[3,1024,128]{2,1,0:T(8,128)(2,1)}, bf16[3,1024,128]{2,1,0:T(8,128)(2,1)}, u32[]{:S(2)}, u32[]{:S(2)}) collective-permute-start(bf16[3,1024,128]{2,1,0:T(8,128)(2,1)} %get-tuple-element.69), channel_id=1, source_target_pairs={{0,4},{4,0},{1,5},{5,1},{2,6},{6,2},{3,7},{7,3},{8,12},{12,8},{9,1... | collective-permute-start | bytes 2359304 | tf_op jit(solution)/shard_map/ppermute | solution.py:391
  34.2 23.3 %collective-permute-start.6 = (bf16[3,1024,128]{2,1,0:T(8,128)(2,1)}, bf16[3,1024,128]{2,1,0:T(8,128)(2,1)}, u32[]{:S(2)}, u32[]{:S(2)}) collective-permute-start(bf16[3,1024,128]{2,1,0:T(8,128)(2,1)} %get-tuple-element.45), channel_id=1, source_target_pairs={{0,4},{4,0},{1,5},{5,1},{2,6},{6,2},{3,7},{7,3},{8,12},{12,8},{9,1... | collective-permute-start | bytes 2359304 | tf_op jit(solution)/shard_map/ppermute | solution.py:391
  36.9 20.5 %collective-permute-start.2 = (bf16[3,1024,128]{2,1,0:T(8,128)(2,1)}, bf16[3,1024,128]{2,1,0:T(8,128)(2,1)}, u32[]{:S(2)}, u32[]{:S(2)}) collective-permute-start(bf16[3,1024,128]{2,1,0:T(8,128)(2,1)} %collective-permute-done.1.rec), channel_id=1, source_target_pairs={{0,8},{8,16},{16,24},{24,32},{32,40},{40,48},{48,56},{56,64},{64,7... | collective-permute-start | bytes 2359304 | tf_op jit(solution)/shard_map/ppermute | solution.py:395
  36.9 20.5 %collective-permute-start.4 = (bf16[3,1024,128]{2,1,0:T(8,128)(2,1)}, bf16[3,1024,128]{2,1,0:T(8,128)(2,1)}, u32[]{:S(2)}, u32[]{:S(2)}) collective-permute-start(bf16[3,1024,128]{2,1,0:T(8,128)(2,1)} %collective-permute-done.1.rec), channel_id=1, source_target_pairs={{0,248},{8,0},{16,8},{24,16},{32,24},{40,32},{48,40},{56,48},{64,5... | collective-permute-start | bytes 2359304 | tf_op jit(solution)/shard_map/ppermute | solution.py:396
  50.9 56.3 %copy-start.2 = (bf16[2,1024,1024]{2,1,0:T(8,128)(2,1)}, bf16[2,1024,1024]{2,1,0:T(8,128)(2,1)S(1)}, u32[]{:S(2)}) copy-start(bf16[2,1024,1024]{2,1,0:T(8,128)(2,1)S(1)} %get-tuple-element.53.wl) | copy-start | bytes 12582916
  50.9 56.3 %copy-start.4 = (bf16[2,1024,1024]{2,1,0:T(8,128)(2,1)}, bf16[2,1024,1024]{2,1,0:T(8,128)(2,1)S(1)}, u32[]{:S(2)}) copy-start(bf16[2,1024,1024]{2,1,0:T(8,128)(2,1)S(1)} %get-tuple-element.52.wh) | copy-start | bytes 12582916
  57.5 19.3 %collective-permute-start.7 = (bf16[3,1024,128]{2,1,0:T(8,128)(2,1)S(1)}, bf16[3,1024,128]{2,1,0:T(8,128)(2,1)S(1)}, u32[]{:S(2)}, u32[]{:S(2)}) collective-permute-start(bf16[3,1024,128]{2,1,0:T(8,128)(2,1)S(1)} %get-tuple-element.46.own), channel_id=1, source_target_pairs={{0,8},{8,16},{16,24},{24,32},{32,40},{40,48},{48,56},{56,64},{64,7... | collective-permute-start | bytes 2359304 | tf_op jit(solution)/shard_map/ppermute | solution.py:395
  57.5 36.1 %collective-permute-start.9 = (bf16[3,1024,128]{2,1,0:T(8,128)(2,1)S(1)}, bf16[3,1024,128]{2,1,0:T(8,128)(2,1)S(1)}, u32[]{:S(2)}, u32[]{:S(2)}) collective-permute-start(bf16[3,1024,128]{2,1,0:T(8,128)(2,1)S(1)} %get-tuple-element.46.own), channel_id=1, source_target_pairs={{0,248},{8,0},{16,8},{24,16},{32,24},{40,32},{48,40},{56,48},{64,5... | collective-permute-start | bytes 2359304 | tf_op jit(solution)/shard_map/ppermute | solution.py:396
  62.2 31.4 %collective-permute-start.8 = (bf16[3,1024,128]{2,1,0:T(8,128)(2,1)}, bf16[3,1024,128]{2,1,0:T(8,128)(2,1)S(1)}, u32[]{:S(2)}, u32[]{:S(2)}) collective-permute-start(bf16[3,1024,128]{2,1,0:T(8,128)(2,1)} %collective-permute-done.6.rec), channel_id=1, source_target_pairs={{0,8},{8,16},{16,24},{24,32},{32,40},{40,48},{48,56},{56,64},{64,7... | collective-permute-start | bytes 2359304 | tf_op jit(solution)/shard_map/ppermute | solution.py:395
  62.3 31.4 %collective-permute-start.10 = (bf16[3,1024,128]{2,1,0:T(8,128)(2,1)}, bf16[3,1024,128]{2,1,0:T(8,128)(2,1)S(1)}, u32[]{:S(2)}, u32[]{:S(2)}) collective-permute-start(bf16[3,1024,128]{2,1,0:T(8,128)(2,1)} %collective-permute-done.6.rec), channel_id=1, source_target_pairs={{0,248},{8,0},{16,8},{24,16},{32,24},{40,32},{48,40},{56,48},{64,5... | collective-permute-start | bytes 2359304 | tf_op jit(solution)/shard_map/ppermute | solution.py:396
  73.6 33.3 %collective-permute-start.5 = (f32[3,1024,128]{2,1,0:T(8,128)S(1)}, f32[3,1024,128]{2,1,0:T(8,128)S(1)}, u32[]{:S(2)}, u32[]{:S(2)}) collective-permute-start(f32[3,1024,128]{2,1,0:T(8,128)S(1)} %get-tuple-element.43), channel_id=1, source_target_pairs={{0,4},{4,0},{1,5},{5,1},{2,6},{6,2},{3,7},{7,3},{8,12},{12,8},{9,1... | collective-permute-start | bytes 4718600 | tf_op jit(solution)/shard_map/ppermute | solution.py:391
  100.7 1.1 copy-start.12
  106.9 44.2 %collective-permute-start.11 = (f32[3,1024,128]{2,1,0:T(8,128)}, f32[3,1024,128]{2,1,0:T(8,128)S(1)}, u32[]{:S(2)}, u32[]{:S(2)}) collective-permute-start(f32[3,1024,128]{2,1,0:T(8,128)} %get-tuple-element.56), channel_id=1, source_target_pairs={{0,4},{4,0},{1,5},{5,1},{2,6},{6,2},{3,7},{7,3},{8,12},{12,8},{9,1... | collective-permute-start | bytes 4718600 | tf_op jit(solution)/shard_map/ppermute | solution.py:391
  114.9 49.8 %all-to-all-start = ((bf16[64,16,768]{2,1,0:T(8,128)(2,1)}), bf16[64,16,768]{2,1,0:T(8,128)(2,1)S(1)}, u32[]{:S(2)}, u32[]{:S(2)}) async-start(bf16[64,16,768]{2,1,0:T(8,128)(2,1)} %dft.2), calls=%async_computation | async-start | bytes 3145728 | tf_op jit(solution)/shard_map/all_to_all | solution.py:429
  151.1 2.2 copy-start.3
  153.3 2.2 copy-start.5
  155.5 1.4 copy-start.13
  164.6 5.9 %copy-start.9 = (bf16[256,256]{1,0:T(8,128)(2,1)S(1)}, bf16[256,256]{1,0:T(8,128)(2,1)}, u32[]{:S(2)}) copy-start(bf16[256,256]{1,0:T(8,128)(2,1)} %constant.55.clone.order) | copy-start | bytes 393220
  164.7 35.8 %all-to-all-start.1 = ((bf16[64,16,768]{2,1,0:T(8,128)(2,1)}), bf16[64,16,768]{2,1,0:T(8,128)(2,1)S(1)}, u32[]{:S(2)}, u32[]{:S(2)}) async-start(bf16[64,16,768]{2,1,0:T(8,128)(2,1)} %dft.3), calls=%async_computation.1 | async-start | bytes 3145728 | tf_op jit(solution)/shard_map/all_to_all | solution.py:429
  172.8 1.2 copy-start.6
  174.0 1.3 copy-start.10
  200.4 1.5 copy-start.11
  204.3 14.3 %collective-permute-start.12 = (f32[8,240,128]{2,1,0:T(8,128)S(1)}, f32[8,240,128]{2,1,0:T(8,128)S(1)}, u32[]{:S(2)}, u32[]{:S(2)}) collective-permute-start(f32[8,240,128]{2,1,0:T(8,128)S(1)} %slice.43), channel_id=1, source_target_pairs={{0,1},{1,0},{2,3},{3,2},{4,5},{5,4},{6,7},{7,6},{8,9},{9,8},{10,11... | collective-permute-start | bytes 2949128 | tf_op jit(solution)/shard_map/ppermute | solution.py:361
  218.8 25.9 %copy-start.7 = (bf16[16,192,256]{2,1,0:T(8,128)(2,1)S(1)}, bf16[16,192,256]{2,1,0:T(8,128)(2,1)}, u32[]{:S(2)}) copy-start(bf16[16,192,256]{2,1,0:T(8,128)(2,1)} %copy-done.6) | copy-start | bytes 4718596
  218.8 25.9 %copy-start.8 = (bf16[192,192]{1,0:T(8,128)(2,1)S(1)}, bf16[192,192]{1,0:T(8,128)(2,1)}, u32[]{:S(2)}) copy-start(bf16[192,192]{1,0:T(8,128)(2,1)} %constant.56.clone.perm) | copy-start | bytes 221188
  218.9 12.5 %collective-permute-start.13 = (f32[4,240,128]{2,1,0:T(8,128)S(1)}, f32[4,240,128]{2,1,0:T(8,128)S(1)}, u32[]{:S(2)}, u32[]{:S(2)}) collective-permute-start(f32[4,240,128]{2,1,0:T(8,128)S(1)} %slice.49), channel_id=1, source_target_pairs={{0,2},{2,0},{1,3},{3,1},{4,6},{6,4},{5,7},{7,5},{8,10},{10,8},{9,1... | collective-permute-start | bytes 1474568 | tf_op jit(solution)/shard_map/ppermute | solution.py:361
  250.0 3.7 %copy-start.1 = (f32[12,2048]{1,0:T(8,128)S(1)}, f32[12,2048]{1,0:T(8,128)}, u32[]{:S(2)}) copy-start(f32[12,2048]{1,0:T(8,128)} %param.7) | copy-start | bytes 294916

commit v3 on v2

--- a/solution.py
+++ b/solution.py
@@ -1,3 +1,4 @@
+import functools
 import math
 
 import jax
@@ -16,6 +17,8 @@
 SHIFT = 5
 BF = jnp.bfloat16
 F32 = jnp.float32
+FILTER_HINT = 40_000_000_000
+DFT_HINT = 40_000_000_000
 
 
 def cyclic(count, steps):
@@ -50,22 +53,30 @@
     return split2(jnp.stack(rows).reshape(2, half, half))
 
 
-def filter_kernel(side, up_own, up_rec, own, rec, down_own, down_rec, coef, kept, sent):
+def filter_kernel(side, coef, *refs, views):
+    kept, sent = refs[-2:]
     step = 16
     pair = 2 * SLOTS
 
+    def load(view, a, rows):
+        ref, lead, offset = refs[view[0]], view[1], view[2]
+        rows = pl.ds(rows + offset, step)
+        value = ref[a, rows, :] if lead is None else ref[lead, a, rows, :]
+        return value.astype(F32)
+
     def run(first, second, mine):
         def body(idx, carry):
-            rows = pl.ds(pl.multiple_of(idx * step, step), step)
+            start = pl.multiple_of(idx * step, step)
+            rows = pl.ds(start, step)
             cols = coef[rows, :]
             taps = [jnp.broadcast_to(cols[:, t : t + 1], (step, LANES)) for t in range(12)]
             acc = [None] * pair
             for block in range(3):
                 for half in range(2):
-                    ref = (first, second)[half][block]
+                    view = (first, second)[half][block]
                     for a in range(SLOTS):
                         at = pair * block + SLOTS * half + a
-                        frame = ref[a, rows, :].astype(F32)
+                        frame = load(view, a, start)
                         for j in range(pair):
                             t = at - j + SHIFT - 5
                             if 0 <= t < 12:
@@ -76,79 +87,104 @@
                 sent[r, rows, :] = acc[SLOTS * (1 - mine) + r]
             return carry
 
-        lax.fori_loop(0, own.shape[1] // step, body, 0, unroll=2)
-
-    mine = (up_own, own, down_own)
-    other = (up_rec, rec, down_rec)
+        lax.fori_loop(0, kept.shape[1] // step, body, 0, unroll=2)
+
+    own, rec = views[:3], views[3:]
 
     @pl.when(side[0] == 0)
     def _():
-        run(mine, other, 0)
+        run(own, rec, 0)
 
     @pl.when(side[0] != 0)
     def _():
-        run(other, mine, 1)
-
-
-def filtered(side, blocks, coef):
-    shape = jax.ShapeDtypeStruct(blocks[0].shape, F32)
+        run(rec, own, 1)
+
+
+def filtered(side, arrays, views, coef):
+    shape = jax.ShapeDtypeStruct((SLOTS, coef.shape[0], LANES), F32)
     in_vmem = pl.BlockSpec(memory_space=pltpu.VMEM)
     return pl.pallas_call(
-        filter_kernel,
+        functools.partial(filter_kernel, views=views),
         out_shape=(shape, shape),
-        in_specs=[pl.BlockSpec(memory_space=pltpu.SMEM)] + [in_vmem] * 7,
+        in_specs=[pl.BlockSpec(memory_space=pltpu.SMEM)] + [in_vmem] * (1 + len(arrays)),
         out_specs=(in_vmem, in_vmem),
         compiler_params=pltpu.CompilerParams(vmem_limit_bytes=4 << 20),
-        cost_estimate=pl.CostEstimate(flops=40_000_000_000, transcendentals=0, bytes_accessed=0),
+        cost_estimate=pl.CostEstimate(flops=FILTER_HINT, transcendentals=0, bytes_accessed=0),
         name="filter",
-    )(side, *blocks, coef)
-
-
-def dft_kernel(side, own, rec, wh, wl, out, fold):
-    half = own.shape[1]
-    step = 16
+    )(side, coef, *arrays)
+
+
+def dft_kernel(side, *refs):
+    subs = (len(refs) - 5) // 2
+    owns, recs = refs[:subs], refs[subs : 2 * subs]
+    wh, wl, out, fold, even = refs[2 * subs :]
+    tile = 16
     width = SLOTS * LANES
+    groups, per, _ = out.shape
     sign = jnp.where(side[0] == 0, 1.0, -1.0)
-
-    def body(idx, carry):
-        rows = pl.ds(pl.multiple_of(idx * step, step), step)
-        for r in range(SLOTS):
-            one, two = own[r, rows, :], rec[r, rows, :]
-            for parity in range(2):
-                value = one + two if parity == 0 else (one - two) * sign
-                top = value.astype(BF)
-                rest = (value - top.astype(F32)).astype(BF)
-                fold[parity, rows, r * LANES : (r + 1) * LANES] = top
-                fold[parity, rows, width + r * LANES : width + (r + 1) * LANES] = rest
-        return carry
-
-    lax.fori_loop(0, half // step, body, 0, unroll=2)
-    groups, per, _ = out.shape
-    parts = []
-    for parity in range(2):
-        full = jnp.dot(wh[parity], fold[parity], preferred_element_type=F32)
-        rest = jnp.dot(wl[parity], fold[parity, :, :width], preferred_element_type=F32)
-        total = full[:, :width] + full[:, width:] + rest
-        parts.append(total.reshape(2, groups, per // 2, width))
+    step = pl.program_id(0)
+
+    @pl.when(step == 0)
+    def _():
+        first = 0
+        for sub in range(subs):
+            size = owns[sub].shape[1]
+
+            def body(idx, carry):
+                start = pl.multiple_of(idx * tile, tile)
+                rows = pl.ds(start, tile)
+                at = pl.ds(start + first, tile)
+                for r in range(SLOTS):
+                    one, two = owns[sub][r, rows, :], recs[sub][r, rows, :]
+                    for par in range(2):
+                        value = one + two if par == 0 else (one - two) * sign
+                        top = value.astype(BF)
+                        rest = (value - top.astype(F32)).astype(BF)
+                        fold[par, at, r * LANES : (r + 1) * LANES] = top
+                        fold[par, at, width + r * LANES : width + (r + 1) * LANES] = rest
+                return carry
+
+            lax.fori_loop(0, size // tile, body, 0, unroll=2)
+            first += size
+
+    data = fold.at[step // 2]
+    full = jnp.dot(wh[0], data[...], preferred_element_type=F32)
+    rest = jnp.dot(wl[0], data[:, :width], preferred_element_type=F32)
+    total = (full[:, :width] + full[:, width:] + rest).reshape(groups, per // 2, width)
+
+    @pl.when(step < 2)
+    def _():
+        even[step] = total
+
     for kind in range(2):
-        both = jnp.concatenate([parts[0][kind], parts[1][kind]], axis=1).astype(BF)
-        out[:, :, kind * width : (kind + 1) * width] = both
-
-
-def dft(side, own, rec, table_h, table_l, groups):
-    half = own.shape[1]
+
+        @pl.when(step == 2 + kind)
+        def _():
+            both = jnp.concatenate([even[kind], total], axis=1).astype(BF)
+            out[:, :, kind * width : (kind + 1) * width] = both
+
+
+def dft(side, owns, recs, table_h, table_l, groups, room):
+    half = table_h.shape[1]
+    per = half // groups
     width = SLOTS * LANES
-    in_vmem = pl.BlockSpec(memory_space=pltpu.VMEM)
+    table = pl.BlockSpec((1, half // 2, half), lambda i: (i // 2, i % 2, 0))
     return pl.pallas_call(
         dft_kernel,
-        out_shape=jax.ShapeDtypeStruct((groups, half // groups, 2 * width), BF),
-        in_specs=[pl.BlockSpec(memory_space=pltpu.SMEM)] + [in_vmem] * 4,
-        out_specs=in_vmem,
-        scratch_shapes=[pltpu.VMEM((2, half, 2 * width), BF)],
-        compiler_params=pltpu.CompilerParams(vmem_limit_bytes=16 << 20),
-        cost_estimate=pl.CostEstimate(flops=40_000_000_000, transcendentals=0, bytes_accessed=0),
+        out_shape=jax.ShapeDtypeStruct((groups, per, 2 * width), BF),
+        grid=(4,),
+        in_specs=[pl.BlockSpec(memory_space=pltpu.SMEM)]
+        + [pl.BlockSpec(value.shape, lambda i: (0, 0, 0)) for value in owns + recs]
+        + [table, table],
+        out_specs=pl.BlockSpec((groups, per, 2 * width), lambda i: (0, 0, 0)),
+        scratch_shapes=[
+            pltpu.VMEM((2, half, 2 * width), BF),
+            pltpu.VMEM((2, groups, per // 2, width), F32),
+        ],
+        compiler_params=pltpu.CompilerParams(vmem_limit_bytes=room << 20),
+        cost_estimate=pl.CostEstimate(flops=DFT_HINT, transcendentals=0, bytes_accessed=0),
         name="dft",
-    )(side, own, rec, table_h, table_l)
+    )(side, *owns, *recs, table_h, table_l)
 
 
 NT = (((1,), (1,)), ((), ()))
@@ -264,11 +300,20 @@
     inverse = 1.0 / spectra
     rows = lax.broadcasted_iota(jnp.int32, (block, 1), 0)
     both = [unpack(gram_ref[c], spectra, block) for c in range(count)]
-    covs = [pair[0] for pair in both]
+    covs = [split3(pair[0]) for pair in both]
+
+    def times(value, parts):
+        a, b, c = split3(value)
+        lead = jnp.dot(jnp.concatenate([a, b, c], axis=0), parts[0], preferred_element_type=F32)
+        next_ = jnp.dot(jnp.concatenate([a, b], axis=0), parts[1], preferred_element_type=F32)
+        last = jnp.dot(a, parts[2], preferred_element_type=F32)
+        small = lead[2 * block :] + next_[block:] + last
+        return lead[:block] + (lead[block : 2 * block] + next_[:block] + small)
+
     proj = [pair[1] for pair in both]
     coef = [None] * count
     for iteration in range(ITERS):
-        mapped = [wide_dot(proj[c], covs[c], ((1,), (0,))) * inverse for c in range(count)]
+        mapped = [times(proj[c], covs[c]) * inverse for c in range(count)]
         gram = [wide_dot(mapped[c], proj[c], ((1,), (1,))) * inverse for c in range(count)]
         before = [proj[c] * inverse for c in range(count)]
         scale = [jnp.zeros((block, 1), F32)] * count
@@ -279,12 +324,13 @@
                 scale[c] = jnp.where(rows == j, 1.0 / jnp.sqrt(pivot), scale[c])
                 gram[c] = gram[c] - factor * gram[c][j : j + 1, :]
                 mapped[c] = mapped[c] - factor * mapped[c][j : j + 1, :]
-                before[c] = before[c] - factor * before[c][j : j + 1, :]
+                if iteration == ITERS - 1:
+                    before[c] = before[c] - factor * before[c][j : j + 1, :]
         proj = [mapped[c] * scale[c] for c in range(count)]
         coef = [before[c] * scale[c] for c in range(count)]
     for c in range(count):
         out[c, :block, :] = coef[c]
-        out[c, block:, :] = wide_dot(coef[c], covs[c], ((1,), (0,)))
+        out[c, block:, :] = times(coef[c], covs[c])
 
 
 def iterate(gram, spectra, block):
@@ -383,9 +429,9 @@
     coef = lax.dynamic_slice_in_dim(taps.T, me * half, half, 0)
     table_h, table_l = dft_tables(frame_len, groups)
 
-    def piece(chunk, which):
-        at = (0, which * half, chunk * LANES)
-        return lax.dynamic_slice(voltages, at, (slots, half, LANES)).astype(BF)
+    def piece(chunk, which, first, size):
+        at = (0, which * half + first, chunk * LANES)
+        return lax.dynamic_slice(voltages, at, (slots, size, LANES)).astype(BF)
 
     def swap(value):
         return lax.ppermute(value, "h", cyclic(2, 1))
@@ -400,33 +446,48 @@
     begin = lax.dynamic_slice_in_dim(start, rank * inputs, inputs, 2).astype(BF)
     begin = begin.reshape(block, 2, chunks, LANES).transpose(2, 0, 1, 3).reshape(chunks, block, -1)
 
-    sums = []
-    gate_x = gate_z = None
-    for chunk in range(chunks):
-        own, send = piece(chunk, me), piece(chunk, 1 - me)
-        if gate_x is not None:
-            own, send, _ = lax.optimization_barrier((own, send, gate_x))
-        rec = swap(send)
-        gate_x = rec
-        moving = (own, rec)
-        if gate_z is not None:
-            moving = lax.optimization_barrier((own, rec) + gate_z)[:2]
-        up_own, down_own = both_ways(moving[0])
-        up_rec, down_rec = both_ways(moving[1])
-        gate_z = (up_rec, down_rec)
-        blocks = (up_own, up_rec, own, rec, down_own, down_rec)
-        if chunk == 0:
-            blocks, (table_h, table_l) = lax.optimization_barrier((blocks, (table_h, table_l)))
-        sums.append(filtered(side, blocks, coef))
-    turned = []
-    for chunk in range(chunks):
-        kept, sent = sums[chunk]
-        back = swap(sent)
-        if chunk + 1 < chunks:
-            kept, back, later = lax.optimization_barrier((kept, back, sums[chunk + 1]))
-            sums[chunk + 1] = later
-        spec = dft(side, kept, back, table_h, table_l, groups)
-        turned.append(lax.all_to_all(spec, FREQ, split_axis=0, concat_axis=0, tiled=True))
+    fence = lax.optimization_barrier
+    sub = half // 2
+    cut = half * 8 // 16
+    coefs = [coef[:sub], coef[sub:]]
+    coefs_b = [coef[:cut], coef[cut:]]
+    parts_b = ((0, cut), (cut, half - cut))
+
+    own_a = piece(0, me, 0, half)
+    send_a = [piece(0, 1 - me, i * sub, sub) for i in range(2)]
+    up_own, down_own = both_ways(own_a)
+    rec_a = [swap(send_a[0])]
+    rec_a.append(swap(fence((send_a[1], rec_a[0]))[0]))
+    ways_a = [both_ways(value) for value in rec_a]
+    own_b = [piece(1, me, *part) for part in parts_b]
+    rec_b = []
+    for i in range(2):
+        rec_b.append(swap(fence((piece(1, 1 - me, *parts_b[i]), rec_a[1]))[0]))
+    both_b = [jnp.stack([own_b[i], rec_b[i]]) for i in range(2)]
+    ways_b = [both_ways(fence((both_b[i], ways_a[i]))[0]) for i in range(2)]
+
+    kept, back = [[], []], [[], []]
+    for i in range(2):
+        arrays = (up_own, own_a, down_own, ways_a[i][0], rec_a[i], ways_a[i][1])
+        views = tuple((n, None, i * sub if n < 3 else 0) for n in range(6))
+        if i == 0:
+            arrays, (table_h, table_l) = fence((arrays, (table_h, table_l)))
+        mine, sent = filtered(side, arrays, views, coefs[i])
+        kept[0].append(mine)
+        back[0].append(swap(sent))
+    specs = []
+    for i in range(2):
+        arrays = (ways_b[i][0], both_b[i], ways_b[i][1])
+        views = tuple((n % 3, n // 3, 0) for n in range(6))
+        if i == 1:
+            specs.append(dft(side, kept[0], back[0], table_h, table_l, groups, 30))
+        mine, sent = filtered(side, arrays, views, coefs_b[i])
+        kept[1].append(mine)
+        if i == 0:
+            kept[0], back[0], sent = fence((kept[0], back[0], sent))
+        back[1].append(swap(sent))
+    specs.append(dft(side, kept[1], back[1], table_h, table_l, groups, 58))
+    turned = [lax.all_to_all(spec, FREQ, split_axis=0, concat_axis=0, tiled=True) for spec in specs]
     place = jnp.stack([k_index, l_index])
     xs, packed = [], None
     for chunk in range(chunks):

time: 254 us -> 234 us (0.921)
  waiting for transfers between devices: 117 us -> 85.3 us
  starting transfers between devices: 51.8 us -> 69 us
  local copies, waits for them, and re-layouts: 15 us -> 10.9 us
    ppermute x4 -> x8, waiting for transfers between devices: 50.8 us -> 19.7 us  [swap(): return lax.ppermute(value, 'h', cyclic(2, 1))]
    ppermute x4 -> x8, starting transfers between devices: 6.01 us -> 12.9 us  [swap(): return lax.ppermute(value, 'h', cyclic(2, 1))]
    ppermute x4 -> x5, waiting for transfers between devices: 26.2 us -> 19.3 us  [both_ways(): lax.ppermute(value, ('y', 'z'), cyclic(rings, 1))]
    all_to_all x2, waiting for transfers between devices: 25.2 us -> 31.9 us  [shards(): lax.all_to_all(spec, FREQ, split_axis=0, concat_axis=0, tiled=True)]
    all_to_all x2, starting transfers between devices: 10.1 us -> 15.7 us  [shards(): lax.all_to_all(spec, FREQ, split_axis=0, concat_axis=0, tiled=True)]
    unnamed x30, local copies, waits for them, and re-layouts: 11.9 us -> 6.66 us
    ppermute x4 -> x5, starting transfers between devices: 20.7 us -> 25.6 us  [both_ways(): lax.ppermute(value, ('y', 'z'), cyclic(rings, -1))]
    another operation x0 -> x3, other arithmetic: none -> 4.08 us  [shards(): both_b = [jnp.stack([own_b[i], rec_b[i]]) for i in range(2)]]
  transfers between devices with their start and end apart: 16 -> 22, of which waited for: 9 -> 9; matrix products, arithmetic and copies ran while one was open for 5% -> 7% of each run, Pallas kernels for 12% -> 14%
where the time goes in v3:
time: 234 us
  waiting for transfers between devices  85.3 us (36%)
  starting transfers between devices  69 us (29%)
  Pallas kernels  44.9 us (19%)
  other arithmetic  15.1 us (6%)
  local copies, waits for them, and re-layouts  10.9 us (5%)
  blocking collectives  7.77 us (3%)
    all_to_all x2, waiting for transfers between devices, shards(): lax.all_to_all(spec, FREQ, split_axis=0, concat_axis=0, tiled=True)  31.9 us
    ppermute x5, starting transfers between devices, both_ways(): lax.ppermute(value, ('y', 'z'), cyclic(rings, -1))  25.6 us
    ppermute x8, waiting for transfers between devices, swap(): return lax.ppermute(value, 'h', cyclic(2, 1))  19.7 us
    pallas_call x2, Pallas kernels, dft(): pl.pallas_call(dft_kernel, out_shape=jax.ShapeDtypeStruct((groups, per, 2...  19.7 us
    ppermute x5, waiting for transfers between devices, both_ways(): lax.ppermute(value, ('y', 'z'), cyclic(rings, 1))  19.3 us
    all_to_all x2, starting transfers between devices, shards(): lax.all_to_all(spec, FREQ, split_axis=0, concat_axis=0, tiled=True)  15.7 us
    ppermute x2, waiting for transfers between devices, reduce_inputs(): packed = packed[:half] + lax.ppermute(packed[half:], axis, cyclic(2, 1))  14.3 us
    ppermute x8, starting transfers between devices, swap(): return lax.ppermute(value, 'h', cyclic(2, 1))  12.9 us
  transfers between devices with their start and end apart: 22, of which 9 were waited for; matrix products, arithmetic and copies ran while one was open for 7% of the time, Pallas kernels for 14%

profile of v3, /device:TPU:1, one launch (start us, length us, event | category | flops | bytes accessed | tf_op | source)
XLA Modules:
  0.0 233.8 jit_solution(1586093769520519663)
XLA Ops:
  0.7 1.6 dynamic-slice_convert_fusion.refs_1_
  2.2 2.5 %collective-permute-start = (bf16[3,1024,128]{2,1,0:T(8,128)(2,1)S(1)}, bf16[3,1024,128]{2,1,0:T(8,128)(2,1)S(1)}, u32[]{:S(2)}, u32[]{:S(2)}) collective-permute-start(bf16[3,1024,128]{2,1,0:T(8,128)(2,1)S(1)} %dynamic-slice_convert_fusion.refs_1_), channel_id=1, source_target_pairs={{0,8},{8,16},{16,24},{24,32},{32,40},{40,48},{48,56},{56,64},{64,7... | collective-permute-start | bytes 2359304 | tf_op jit(solution)/shard_map/ppermute | solution.py:441
  4.8 6.5 %collective-permute-start.1 = (bf16[3,1024,128]{2,1,0:T(8,128)(2,1)S(1)}, bf16[3,1024,128]{2,1,0:T(8,128)(2,1)S(1)}, u32[]{:S(2)}, u32[]{:S(2)}) collective-permute-start(bf16[3,1024,128]{2,1,0:T(8,128)(2,1)S(1)} %dynamic-slice_convert_fusion.refs_1_), channel_id=1, source_target_pairs={{0,248},{8,0},{16,8},{24,16},{32,24},{40,32},{48,40},{56,48},{64,5... | collective-permute-start | bytes 2359304 | tf_op jit(solution)/shard_map/ppermute | solution.py:442
  11.3 3.9 %fusion.2 = (bf16[1,3,512,128]{3,2,1,0:T(8,128)(2,1)}, bf16[3,512,128]{2,1,0:T(8,128)(2,1)}, bf16[1,3,512,128]{3,2,1,0:T(8,128)(2,1)}, bf16[3,512,128]{2,1,0:T(8...) fusion(s32[3,2048,256]{2,1,0:T(8,128)} %param.6, s32[]{:T(128)S(6)} %select_n.42, ...), kind=kLoop, calls=%fused_computation.20 | loop fusion | flops 1179648 | bytes 7077904 | tf_op jit(solution)/shard_map/stack | solution.py:466
  15.2 2.7 %collective-permute-start.2 = (bf16[3,512,128]{2,1,0:T(8,128)(2,1)}, bf16[3,512,128]{2,1,0:T(8,128)(2,1)S(1)}, u32[]{:S(2)}, u32[]{:S(2)}) collective-permute-start(bf16[3,512,128]{2,1,0:T(8,128)(2,1)} %get-tuple-element.84), channel_id=1, source_target_pairs={{0,4},{4,0},{1,5},{5,1},{2,6},{6,2},{3,7},{7,3},{8,12},{12,8},{9,1... | collective-permute-start | bytes 1179656 | tf_op jit(solution)/shard_map/ppermute | solution.py:437
  18.3 1.1 fusion.9
  19.4 1.1 subtract_bitcast_fusion.1
  21.3 5.3 %collective-permute-done.2.refs_4_ = bf16[3,512,128]{2,1,0:T(8,128)(2,1)S(1)} collective-permute-done((bf16[3,512,128]{2,1,0:T(8,128)(2,1)}, bf16[3,512,128]{2,1,0:T(8,128)(2,1)S(1)}, u32[]{:S(2)}, u32[]{:S(2)}) %collective-permute-start.2) | collective-permute-done | bytes 393248 | tf_op jit(solution)/shard_map/ppermute | solution.py:437
  26.6 2.7 %collective-permute-start.5 = (bf16[3,512,128]{2,1,0:T(8,128)(2,1)}, bf16[3,512,128]{2,1,0:T(8,128)(2,1)S(1)}, u32[]{:S(2)}, u32[]{:S(2)}) collective-permute-start(bf16[3,512,128]{2,1,0:T(8,128)(2,1)} %get-tuple-element.49), channel_id=1, source_target_pairs={{0,4},{4,0},{1,5},{5,1},{2,6},{6,2},{3,7},{7,3},{8,12},{12,8},{9,1... | collective-permute-start | bytes 1179656 | tf_op jit(solution)/shard_map/ppermute | solution.py:437
  29.3 4.8 %collective-permute-start.4 = (bf16[3,512,128]{2,1,0:T(8,128)(2,1)S(1)}, bf16[3,512,128]{2,1,0:T(8,128)(2,1)}, u32[]{:S(2)}, u32[]{:S(2)}) collective-permute-start(bf16[3,512,128]{2,1,0:T(8,128)(2,1)S(1)} %collective-permute-done.2.refs_4_), channel_id=1, source_target_pairs={{0,248},{8,0},{16,8},{24,16},{32,24},{40,32},{48,40},{56,48},{64,5... | collective-permute-start | bytes 1179656 | tf_op jit(solution)/shard_map/ppermute | solution.py:442
  34.1 5.2 %fusion = (bf16[2,1024,1024]{2,1,0:T(8,128)(2,1)}, bf16[2,1024,1024]{2,1,0:T(8,128)(2,1)}) fusion(f32[2,1024,1024]{2,1,0:T(8,128)S(1)} %bitcast.29), kind=kLoop, calls=%fused_computation.2 | loop fusion | flops 8388608 | bytes 16777216 | tf_op jit(solution)/shard_map/convert_element_type | solution.py:30
  39.4 1.0 copy.14
  40.4 1.1 fusion.17
  41.8 2.7 %collective-permute-start.10 = (bf16[3,512,128]{2,1,0:T(8,128)(2,1)}, bf16[3,512,128]{2,1,0:T(8,128)(2,1)S(1)}, u32[]{:S(2)}, u32[]{:S(2)}) collective-permute-start(bf16[3,512,128]{2,1,0:T(8,128)(2,1)} %get-tuple-element.53), channel_id=1, source_target_pairs={{0,4},{4,0},{1,5},{5,1},{2,6},{6,2},{3,7},{7,3},{8,12},{12,8},{9,1... | collective-permute-start | bytes 1179656 | tf_op jit(solution)/shard_map/ppermute | solution.py:437
  44.6 4.8 %collective-permute-start.7 = (bf16[3,512,128]{2,1,0:T(8,128)(2,1)S(1)}, bf16[3,512,128]{2,1,0:T(8,128)(2,1)S(1)}, u32[]{:S(2)}, u32[]{:S(2)}) collective-permute-start(bf16[3,512,128]{2,1,0:T(8,128)(2,1)S(1)} %collective-permute-done.5.refs_4_), channel_id=1, source_target_pairs={{0,248},{8,0},{16,8},{24,16},{32,24},{40,32},{48,40},{56,48},{64,5... | collective-permute-start | bytes 1179656 | tf_op jit(solution)/shard_map/ppermute | solution.py:442
  49.4 3.7 %filter.4 = (f32[3,512,128]{2,1,0:T(8,128)S(1)}, f32[3,512,128]{2,1,0:T(8,128)S(1)}) custom-call(s32[1]{0:T(128)} %bitcast.2.side, f32[512,12]{1,0:T(8,128)S(1)} %get-tuple-element.91.coef, bf16[3,1024,128]{2,1,0:T(8,128)(2,1)S(1)} %collective-permute-done.refs_0_, bf16[3,1024,128]{2,1,0:T(8,128)(2,1)S(1)} %dynamic-slice_convert_fusion.refs_1_, ...), custom_call_target="tpu_custom_call" | custom-call | flops 40000000000 | tf_op jit(solution)/shard_map/filter/pallas_call | solution.py:106
  53.4 1.9 collective-permute-done.6.refs_3_
  55.3 4.8 %collective-permute-start.15 = (bf16[2,3,512,128]{3,2,1,0:T(8,128)(2,1)S(1)}, bf16[2,3,512,128]{3,2,1,0:T(8,128)(2,1)S(1)}, u32[]{:S(2)}, u32[]{:S(2)}) collective-permute-start(bf16[2,3,512,128]{3,2,1,0:T(8,128)(2,1)S(1)} %pad_maximum_fusion.2.refs_1_), channel_id=1, source_target_pairs={{0,248},{8,0},{16,8},{24,16},{32,24},{40,32},{48,40},{56,48},{64,5... | collective-permute-start | bytes 2359304 | tf_op jit(solution)/shard_map/ppermute | solution.py:442
  60.2 4.8 %collective-permute-start.12 = (bf16[2,3,512,128]{3,2,1,0:T(8,128)(2,1)S(1)}, bf16[2,3,512,128]{3,2,1,0:T(8,128)(2,1)S(1)}, u32[]{:S(2)}, u32[]{:S(2)}) collective-permute-start(bf16[2,3,512,128]{3,2,1,0:T(8,128)(2,1)S(1)} %pad_maximum_fusion.1.refs_1_), channel_id=1, source_target_pairs={{0,248},{8,0},{16,8},{24,16},{32,24},{40,32},{48,40},{56,48},{64,5... | collective-permute-start | bytes 2359304 | tf_op jit(solution)/shard_map/ppermute | solution.py:442
  65.0 2.4 %filter.5 = (f32[3,512,128]{2,1,0:T(8,128)S(1)}, f32[3,512,128]{2,1,0:T(8,128)S(1)}) custom-call(s32[1]{0:T(128)} %bitcast.2.side, f32[512,12]{1,0:T(8,128)S(1)} %get-tuple-element.90.coef, bf16[3,1024,128]{2,1,0:T(8,128)(2,1)S(1)} %collective-permute-done.refs_0_, bf16[3,1024,128]{2,1,0:T(8,128)(2,1)S(1)} %dynamic-slice_convert_fusion.refs_1_, ...), custom_call_target="tpu_custom_call" | custom-call | flops 40000000000 | tf_op jit(solution)/shard_map/filter/pallas_call | solution.py:106
  67.4 6.0 %collective-permute-done.14.refs_0_ = bf16[2,3,512,128]{3,2,1,0:T(8,128)(2,1)S(1)} collective-permute-done((bf16[2,3,512,128]{3,2,1,0:T(8,128)(2,1)S(1)}, bf16[2,3,512,128]{3,2,1,0:T(8,128)(2,1)S(1)}, u32[]{:S(2)}, u32[]{:S(2)}) %collective-permute-start.14) | collective-permute-done | bytes 786464 | tf_op jit(solution)/shard_map/ppermute | solution.py:441
  73.5 1.2 collective-permute-start.9
  74.7 2.4 %filter.7 = (f32[3,512,128]{2,1,0:T(8,128)S(1)}, f32[3,512,128]{2,1,0:T(8,128)S(1)}) custom-call(s32[1]{0:T(128)} %bitcast.2.side, f32[512,12]{1,0:T(8,128)S(1)} %get-tuple-element.90.coef, bf16[2,3,512,128]{3,2,1,0:T(8,128)(2,1)S(1)} %collective-permute-done.14.refs_0_, bf16[2,3,512,128]{3,2,1,0:T(8,128)(2,1)S(1)} %pad_maximum_fusion.2.refs_1_, ...), custom_call_target="tpu_custom_call" | custom-call | flops 40000000000 | tf_op jit(solution)/shard_map/filter/pallas_call | solution.py:106
  77.1 1.8 collective-permute-start.17
  78.9 11.4 %collective-permute-done.11.refs_0_ = bf16[2,3,512,128]{3,2,1,0:T(8,128)(2,1)S(1)} collective-permute-done((bf16[2,3,512,128]{3,2,1,0:T(8,128)(2,1)S(1)}, bf16[2,3,512,128]{3,2,1,0:T(8,128)(2,1)S(1)}, u32[]{:S(2)}, u32[]{:S(2)}) %collective-permute-start.11) | collective-permute-done | bytes 786464 | tf_op jit(solution)/shard_map/ppermute | solution.py:441
  90.3 2.4 %filter.6 = (f32[3,512,128]{2,1,0:T(8,128)S(1)}, f32[3,512,128]{2,1,0:T(8,128)S(1)}) custom-call(s32[1]{0:T(128)} %bitcast.2.side, f32[512,12]{1,0:T(8,128)S(1)} %get-tuple-element.91.coef, bf16[2,3,512,128]{3,2,1,0:T(8,128)(2,1)S(1)} %collective-permute-done.11.refs_0_, bf16[2,3,512,128]{3,2,1,0:T(8,128)(2,1)S(1)} %pad_maximum_fusion.1.refs_1_, ...), custom_call_target="tpu_custom_call" | custom-call | flops 40000000000 | tf_op jit(solution)/shard_map/filter/pallas_call | solution.py:106
  92.7 0.9 copy-done.11
  93.6 1.2 collective-permute-start.16
  94.8 8.6 %dft.2 = bf16[64,16,768]{2,1,0:T(8,128)(2,1)} custom-call(s32[1]{0:T(128)} %bitcast.2.side, f32[3,512,128]{2,1,0:T(8,128)S(1)} %get-tuple-element.56.refs_0_, f32[3,512,128]{2,1,0:T(8,128)S(1)} %get-tuple-element.57.refs_1_, f32[3,512,128]{2,1,0:T(8,128)S(1)} %collective-permute-done.8.refs_2_, f32[3,512,128]{2,1,0:T(8,128)S(1)} %collective-permute-done.9.refs_3_, ...), custom_call_target="tpu_custom_call" | custom-call | flops 40000000000 | tf_op jit(solution)/shard_map/dft/pallas_call | solution.py:172
  103.4 8.3 %all-to-all-start = ((bf16[64,16,768]{2,1,0:T(8,128)(2,1)}), bf16[64,16,768]{2,1,0:T(8,128)(2,1)S(1)}, u32[]{:S(2)}, u32[]{:S(2)}) async-start(bf16[64,16,768]{2,1,0:T(8,128)(2,1)} %dft.2), calls=%async_computation | async-start | bytes 3145728 | tf_op jit(solution)/shard_map/all_to_all | solution.py:490
  111.7 14.4 %collective-permute-done.16.refs_2_ = f32[3,512,128]{2,1,0:T(8,128)} collective-permute-done((f32[3,512,128]{2,1,0:T(8,128)S(1)}, f32[3,512,128]{2,1,0:T(8,128)}, u32[]{:S(2)}, u32[]{:S(2)}) %collective-permute-start.16) | collective-permute-done | bytes 786464 | tf_op jit(solution)/shard_map/ppermute | solution.py:437
  126.1 11.1 %dft.3 = bf16[64,16,768]{2,1,0:T(8,128)(2,1)} custom-call(s32[1]{0:T(128)} %bitcast.2.side, f32[3,512,128]{2,1,0:T(8,128)} %copy-done.11, f32[3,512,128]{2,1,0:T(8,128)} %copy-done.10, f32[3,512,128]{2,1,0:T(8,128)} %collective-permute-done.16.refs_2_, f32[3,512,128]{2,1,0:T(8,128)} %collective-permute-done.17.refs_3_, ...), custom_call_target="tpu_custom_call" | custom-call | flops 40000000000 | tf_op jit(solution)/shard_map/dft/pallas_call | solution.py:172
  137.2 6.4 %all-to-all-done.turned = bf16[64,16,768]{2,1,0:T(8,128)(2,1)S(1)} async-done(((bf16[64,16,768]{2,1,0:T(8,128)(2,1)}), bf16[64,16,768]{2,1,0:T(8,128)(2,1)S(1)}, u32[]{:S(2)}, u32[]{:S(2)}) %all-to-all-start) | async-done | bytes 1572896 | tf_op jit(solution)/shard_map/all_to_all | solution.py:490
  143.6 7.4 %all-to-all-start.1 = ((bf16[64,16,768]{2,1,0:T(8,128)(2,1)}), bf16[64,16,768]{2,1,0:T(8,128)(2,1)S(1)}, u32[]{:S(2)}, u32[]{:S(2)}) async-start(bf16[64,16,768]{2,1,0:T(8,128)(2,1)} %dft.3), calls=%async_computation.1 | async-start | bytes 3145728 | tf_op jit(solution)/shard_map/all_to_all | solution.py:490
  151.9 2.3 gram.2
  154.2 1.2 copy-done.4
  155.4 1.3 copy-done.8
  156.6 25.5 %all-to-all-done.1.turned = bf16[64,16,768]{2,1,0:T(8,128)(2,1)S(1)} async-done(((bf16[64,16,768]{2,1,0:T(8,128)(2,1)}), bf16[64,16,768]{2,1,0:T(8,128)(2,1)S(1)}, u32[]{:S(2)}, u32[]{:S(2)}) %all-to-all-start.1) | async-done | bytes 1572896 | tf_op jit(solution)/shard_map/all_to_all | solution.py:490
  182.1 1.5 copy-done.9
  183.7 2.3 gram.3
  186.0 11.6 %collective-permute-start.18 = (f32[8,240,128]{2,1,0:T(8,128)S(1)}, f32[8,240,128]{2,1,0:T(8,128)S(1)}, u32[]{:S(2)}, u32[]{:S(2)}) collective-permute-start(f32[8,240,128]{2,1,0:T(8,128)S(1)} %slice.53), channel_id=1, source_target_pairs={{0,1},{1,0},{2,3},{3,2},{4,5},{5,4},{6,7},{7,6},{8,9},{9,8},{10,11... | collective-permute-start | bytes 2949128 | tf_op jit(solution)/shard_map/ppermute | solution.py:407
  197.6 2.2 collective-permute-done.18
  200.4 12.1 %collective-permute-done.19 = f32[4,240,128]{2,1,0:T(8,128)S(1)} collective-permute-done((f32[4,240,128]{2,1,0:T(8,128)S(1)}, f32[4,240,128]{2,1,0:T(8,128)S(1)}, u32[]{:S(2)}, u32[]{:S(2)}) %collective-permute-start.19) | collective-permute-done | bytes 491552 | tf_op jit(solution)/shard_map/ppermute | solution.py:407
  212.6 4.5 %iterate.1 = f32[4,16,192]{2,1,0:T(8,128)S(1)} custom-call(f32[4,240,128]{2,1,0:T(8,128)S(1)} %slice_add_fusion.1.g), custom_call_target="tpu_custom_call" | custom-call | tf_op jit(solution)/shard_map/iterate/pallas_call | solution.py:338
  217.0 3.8 %all_gather.6 = f32[8,16,192]{2,1,0:T(8,128)S(1)} all-gather(f32[4,16,192]{2,1,0:T(8,128)S(1)} %iterate.1), channel_id=1, replica_groups=mesh['y'=4,'z'=8,'h'=2,'l'=2,'k'=2] {'l'}, dimensions={0}, use_global_device_ids=true | all-gather | bytes 147456 | tf_op jit(solution)/shard_map/all_gather | solution.py:413
  220.8 4.0 %all_gather.7.pair = f32[16,16,192]{2,1,0:T(8,128)S(1)} all-gather(f32[8,16,192]{2,1,0:T(8,128)S(1)} %all_gather.6), channel_id=1, replica_groups=mesh['y'=4,'z'=8,'h'=2,'l'=2,'k'=2] {'k'}, dimensions={0}, use_global_device_ids=true | all-gather | bytes 294912 | tf_op jit(solution)/shard_map/all_gather | solution.py:413
  224.8 5.4 %clean.1 = (bf16[16,192,512]{2,1,0:T(8,128)(2,1)S(1)}, f32[16,8,8]{2,1,0:T(8,128)S(1)}) custom-call(bf16[16,192,256]{2,1,0:T(8,128)(2,1)S(1)} %copy-done.5, bf16[16,192,256]{2,1,0:T(8,128)(2,1)S(1)} %get-tuple-element.70.xb, f32[16,16,192]{2,1,0:T(8,128)S(1)} %all_gather.7.pair, bf16[192,192]{1,0:T(8,128)(2,1)S(1)} %copy-done.6), custom_call_target="tpu_custom_call" | custom-call | tf_op jit(solution)/shard_map/clean/pallas_call | solution.py:382
  230.2 2.9 %reshape.230 = bf16[16,192,2,256]{3,2,1,0:T(2,128)(2,1)} reshape(bf16[16,192,512]{2,1,0:T(8,128)(2,1)S(1)} %get-tuple-element.72) | data formatting | bytes 6291456 | tf_op jit(solution)/shard_map/reshape | solution.py:498
  (64 shorter events, 4.2 us)
Async XLA Ops:
  0.6 38.7 %copy-start = (f32[12,2048]{1,0:T(8,128)S(1)}, f32[12,2048]{1,0:T(8,128)}, u32[]{:S(2)}) copy-start(f32[12,2048]{1,0:T(8,128)} %param.7) | copy-start | bytes 294916
  2.2 42.3 %collective-permute-start = (bf16[3,1024,128]{2,1,0:T(8,128)(2,1)S(1)}, bf16[3,1024,128]{2,1,0:T(8,128)(2,1)S(1)}, u32[]{:S(2)}, u32[]{:S(2)}) collective-permute-start(bf16[3,1024,128]{2,1,0:T(8,128)(2,1)S(1)} %dynamic-slice_convert_fusion.refs_1_), channel_id=1, source_target_pairs={{0,8},{8,16},{16,24},{24,32},{32,40},{40,48},{48,56},{56,64},{64,7... | collective-permute-start | bytes 2359304 | tf_op jit(solution)/shard_map/ppermute | solution.py:441
  4.8 39.8 %collective-permute-start.1 = (bf16[3,1024,128]{2,1,0:T(8,128)(2,1)S(1)}, bf16[3,1024,128]{2,1,0:T(8,128)(2,1)S(1)}, u32[]{:S(2)}, u32[]{:S(2)}) collective-permute-start(bf16[3,1024,128]{2,1,0:T(8,128)(2,1)S(1)} %dynamic-slice_convert_fusion.refs_1_), channel_id=1, source_target_pairs={{0,248},{8,0},{16,8},{24,16},{32,24},{40,32},{48,40},{56,48},{64,5... | collective-permute-start | bytes 2359304 | tf_op jit(solution)/shard_map/ppermute | solution.py:442
  15.2 11.4 %collective-permute-start.2 = (bf16[3,512,128]{2,1,0:T(8,128)(2,1)}, bf16[3,512,128]{2,1,0:T(8,128)(2,1)S(1)}, u32[]{:S(2)}, u32[]{:S(2)}) collective-permute-start(bf16[3,512,128]{2,1,0:T(8,128)(2,1)} %get-tuple-element.84), channel_id=1, source_target_pairs={{0,4},{4,0},{1,5},{5,1},{2,6},{6,2},{3,7},{7,3},{8,12},{12,8},{9,1... | collective-permute-start | bytes 1179656 | tf_op jit(solution)/shard_map/ppermute | solution.py:437
  26.6 14.9 %collective-permute-start.5 = (bf16[3,512,128]{2,1,0:T(8,128)(2,1)}, bf16[3,512,128]{2,1,0:T(8,128)(2,1)S(1)}, u32[]{:S(2)}, u32[]{:S(2)}) collective-permute-start(bf16[3,512,128]{2,1,0:T(8,128)(2,1)} %get-tuple-element.49), channel_id=1, source_target_pairs={{0,4},{4,0},{1,5},{5,1},{2,6},{6,2},{3,7},{7,3},{8,12},{12,8},{9,1... | collective-permute-start | bytes 1179656 | tf_op jit(solution)/shard_map/ppermute | solution.py:437
  29.3 12.5 %collective-permute-start.3 = (bf16[3,512,128]{2,1,0:T(8,128)(2,1)S(1)}, bf16[3,512,128]{2,1,0:T(8,128)(2,1)}, u32[]{:S(2)}, u32[]{:S(2)}) collective-permute-start(bf16[3,512,128]{2,1,0:T(8,128)(2,1)S(1)} %collective-permute-done.2.refs_4_), channel_id=1, source_target_pairs={{0,8},{8,16},{16,24},{24,32},{32,40},{40,48},{48,56},{56,64},{64,7... | collective-permute-start | bytes 1179656 | tf_op jit(solution)/shard_map/ppermute | solution.py:441
  29.3 15.2 %collective-permute-start.4 = (bf16[3,512,128]{2,1,0:T(8,128)(2,1)S(1)}, bf16[3,512,128]{2,1,0:T(8,128)(2,1)}, u32[]{:S(2)}, u32[]{:S(2)}) collective-permute-start(bf16[3,512,128]{2,1,0:T(8,128)(2,1)S(1)} %collective-permute-done.2.refs_4_), channel_id=1, source_target_pairs={{0,248},{8,0},{16,8},{24,16},{32,24},{40,32},{48,40},{56,48},{64,5... | collective-permute-start | bytes 1179656 | tf_op jit(solution)/shard_map/ppermute | solution.py:442
  41.5 11.8 %collective-permute-start.13 = (bf16[3,512,128]{2,1,0:T(8,128)(2,1)}, bf16[3,512,128]{2,1,0:T(8,128)(2,1)S(1)}, u32[]{:S(2)}, u32[]{:S(2)}) collective-permute-start(bf16[3,512,128]{2,1,0:T(8,128)(2,1)} %get-tuple-element.64), channel_id=1, source_target_pairs={{0,4},{4,0},{1,5},{5,1},{2,6},{6,2},{3,7},{7,3},{8,12},{12,8},{9,1... | collective-permute-start | bytes 1179656 | tf_op jit(solution)/shard_map/ppermute | solution.py:437
  41.8 18.3 %collective-permute-start.10 = (bf16[3,512,128]{2,1,0:T(8,128)(2,1)}, bf16[3,512,128]{2,1,0:T(8,128)(2,1)S(1)}, u32[]{:S(2)}, u32[]{:S(2)}) collective-permute-start(bf16[3,512,128]{2,1,0:T(8,128)(2,1)} %get-tuple-element.53), channel_id=1, source_target_pairs={{0,4},{4,0},{1,5},{5,1},{2,6},{6,2},{3,7},{7,3},{8,12},{12,8},{9,1... | collective-permute-start | bytes 1179656 | tf_op jit(solution)/shard_map/ppermute | solution.py:437
  44.5 10.7 %collective-permute-start.6 = (bf16[3,512,128]{2,1,0:T(8,128)(2,1)S(1)}, bf16[3,512,128]{2,1,0:T(8,128)(2,1)S(1)}, u32[]{:S(2)}, u32[]{:S(2)}) collective-permute-start(bf16[3,512,128]{2,1,0:T(8,128)(2,1)S(1)} %collective-permute-done.5.refs_4_), channel_id=1, source_target_pairs={{0,8},{8,16},{16,24},{24,32},{32,40},{40,48},{48,56},{56,64},{64,7... | collective-permute-start | bytes 1179656 | tf_op jit(solution)/shard_map/ppermute | solution.py:441
  44.6 10.6 %collective-permute-start.7 = (bf16[3,512,128]{2,1,0:T(8,128)(2,1)S(1)}, bf16[3,512,128]{2,1,0:T(8,128)(2,1)S(1)}, u32[]{:S(2)}, u32[]{:S(2)}) collective-permute-start(bf16[3,512,128]{2,1,0:T(8,128)(2,1)S(1)} %collective-permute-done.5.refs_4_), channel_id=1, source_target_pairs={{0,248},{8,0},{16,8},{24,16},{32,24},{40,32},{48,40},{56,48},{64,5... | collective-permute-start | bytes 1179656 | tf_op jit(solution)/shard_map/ppermute | solution.py:442
  49.4 3.9 %copy-start.13 = (bf16[1,3,512,128]{3,2,1,0:T(8,128)(2,1)S(1)}, bf16[1,3,512,128]{3,2,1,0:T(8,128)(2,1)}, u32[]{:S(2)}) copy-start(bf16[1,3,512,128]{3,2,1,0:T(8,128)(2,1)} %get-tuple-element.80) | copy-start | bytes 1179652
  49.4 10.7 %copy-start.12 = (bf16[1,3,512,128]{3,2,1,0:T(8,128)(2,1)S(1)}, bf16[1,3,512,128]{3,2,1,0:T(8,128)(2,1)}, u32[]{:S(2)}) copy-start(bf16[1,3,512,128]{3,2,1,0:T(8,128)(2,1)} %get-tuple-element.82) | copy-start | bytes 1179652
  53.2 40.4 %collective-permute-start.8 = (f32[3,512,128]{2,1,0:T(8,128)S(1)}, f32[3,512,128]{2,1,0:T(8,128)S(1)}, u32[]{:S(2)}, u32[]{:S(2)}) collective-permute-start(f32[3,512,128]{2,1,0:T(8,128)S(1)} %get-tuple-element.51), channel_id=1, source_target_pairs={{0,4},{4,0},{1,5},{5,1},{2,6},{6,2},{3,7},{7,3},{8,12},{12,8},{9,1... | collective-permute-start | bytes 2359304 | tf_op jit(solution)/shard_map/ppermute | solution.py:437
  55.3 18.2 %collective-permute-start.14 = (bf16[2,3,512,128]{3,2,1,0:T(8,128)(2,1)S(1)}, bf16[2,3,512,128]{3,2,1,0:T(8,128)(2,1)S(1)}, u32[]{:S(2)}, u32[]{:S(2)}) collective-permute-start(bf16[2,3,512,128]{3,2,1,0:T(8,128)(2,1)S(1)} %pad_maximum_fusion.2.refs_1_), channel_id=1, source_target_pairs={{0,8},{8,16},{16,24},{24,32},{32,40},{40,48},{48,56},{56,64},{64,7... | collective-permute-start | bytes 2359304 | tf_op jit(solution)/shard_map/ppermute | solution.py:441
  55.3 19.4 %collective-permute-start.15 = (bf16[2,3,512,128]{3,2,1,0:T(8,128)(2,1)S(1)}, bf16[2,3,512,128]{3,2,1,0:T(8,128)(2,1)S(1)}, u32[]{:S(2)}, u32[]{:S(2)}) collective-permute-start(bf16[2,3,512,128]{3,2,1,0:T(8,128)(2,1)S(1)} %pad_maximum_fusion.2.refs_1_), channel_id=1, source_target_pairs={{0,248},{8,0},{16,8},{24,16},{32,24},{40,32},{48,40},{56,48},{64,5... | collective-permute-start | bytes 2359304 | tf_op jit(solution)/shard_map/ppermute | solution.py:442
  60.2 30.1 %collective-permute-start.11 = (bf16[2,3,512,128]{3,2,1,0:T(8,128)(2,1)S(1)}, bf16[2,3,512,128]{3,2,1,0:T(8,128)(2,1)S(1)}, u32[]{:S(2)}, u32[]{:S(2)}) collective-permute-start(bf16[2,3,512,128]{3,2,1,0:T(8,128)(2,1)S(1)} %pad_maximum_fusion.1.refs_1_), channel_id=1, source_target_pairs={{0,8},{8,16},{16,24},{24,32},{32,40},{40,48},{48,56},{56,64},{64,7... | collective-permute-start | bytes 2359304 | tf_op jit(solution)/shard_map/ppermute | solution.py:441
  60.2 30.1 %collective-permute-start.12 = (bf16[2,3,512,128]{3,2,1,0:T(8,128)(2,1)S(1)}, bf16[2,3,512,128]{3,2,1,0:T(8,128)(2,1)S(1)}, u32[]{:S(2)}, u32[]{:S(2)}) collective-permute-start(bf16[2,3,512,128]{3,2,1,0:T(8,128)(2,1)S(1)} %pad_maximum_fusion.1.refs_1_), channel_id=1, source_target_pairs={{0,248},{8,0},{16,8},{24,16},{32,24},{40,32},{48,40},{56,48},{64,5... | collective-permute-start | bytes 2359304 | tf_op jit(solution)/shard_map/ppermute | solution.py:442
  73.5 20.2 %collective-permute-start.9 = (f32[3,512,128]{2,1,0:T(8,128)S(1)}, f32[3,512,128]{2,1,0:T(8,128)S(1)}, u32[]{:S(2)}, u32[]{:S(2)}) collective-permute-start(f32[3,512,128]{2,1,0:T(8,128)S(1)} %get-tuple-element.52), channel_id=1, source_target_pairs={{0,4},{4,0},{1,5},{5,1},{2,6},{6,2},{3,7},{7,3},{8,12},{12,8},{9,1... | collective-permute-start | bytes 2359304 | tf_op jit(solution)/shard_map/ppermute | solution.py:437
  77.1 15.6 %copy-start.10 = (f32[3,512,128]{2,1,0:T(8,128)}, f32[3,512,128]{2,1,0:T(8,128)S(1)}, u32[]{:S(2)}) copy-start(f32[3,512,128]{2,1,0:T(8,128)S(1)} %get-tuple-element.66.refs_1_) | copy-start | bytes 2359300
  77.1 17.7 %copy-start.2 = (bf16[2,1024,1024]{2,1,0:T(8,128)(2,1)S(1)}, bf16[2,1024,1024]{2,1,0:T(8,128)(2,1)}, u32[]{:S(2)}) copy-start(bf16[2,1024,1024]{2,1,0:T(8,128)(2,1)} %get-tuple-element.61.refs_5_) | copy-start | bytes 12582916
  77.1 17.7 %copy-start.3 = (bf16[2,1024,1024]{2,1,0:T(8,128)(2,1)S(1)}, bf16[2,1024,1024]{2,1,0:T(8,128)(2,1)}, u32[]{:S(2)}) copy-start(bf16[2,1024,1024]{2,1,0:T(8,128)(2,1)} %get-tuple-element.60.refs_4_) | copy-start | bytes 12582916
  77.1 34.6 %collective-permute-start.17 = (f32[3,512,128]{2,1,0:T(8,128)S(1)}, f32[3,512,128]{2,1,0:T(8,128)}, u32[]{:S(2)}, u32[]{:S(2)}) collective-permute-start(f32[3,512,128]{2,1,0:T(8,128)S(1)} %get-tuple-element.68), channel_id=1, source_target_pairs={{0,4},{4,0},{1,5},{5,1},{2,6},{6,2},{3,7},{7,3},{8,12},{12,8},{9,1... | collective-permute-start | bytes 2359304 | tf_op jit(solution)/shard_map/ppermute | solution.py:437
  92.7 0.9 copy-start.11
  93.6 32.5 %collective-permute-start.16 = (f32[3,512,128]{2,1,0:T(8,128)S(1)}, f32[3,512,128]{2,1,0:T(8,128)}, u32[]{:S(2)}, u32[]{:S(2)}) collective-permute-start(f32[3,512,128]{2,1,0:T(8,128)S(1)} %get-tuple-element.67), channel_id=1, source_target_pairs={{0,4},{4,0},{1,5},{5,1},{2,6},{6,2},{3,7},{7,3},{8,12},{12,8},{9,1... | collective-permute-start | bytes 2359304 | tf_op jit(solution)/shard_map/ppermute | solution.py:437
  103.4 40.2 %all-to-all-start = ((bf16[64,16,768]{2,1,0:T(8,128)(2,1)}), bf16[64,16,768]{2,1,0:T(8,128)(2,1)S(1)}, u32[]{:S(2)}, u32[]{:S(2)}) async-start(bf16[64,16,768]{2,1,0:T(8,128)(2,1)} %dft.2), calls=%async_computation | async-start | bytes 3145728 | tf_op jit(solution)/shard_map/all_to_all | solution.py:490
  137.2 14.7 %copy-start.7 = (bf16[256,256]{1,0:T(8,128)(2,1)S(1)}, bf16[256,256]{1,0:T(8,128)(2,1)}, u32[]{:S(2)}) copy-start(bf16[256,256]{1,0:T(8,128)(2,1)} %constant.60.clone.order) | copy-start | bytes 393220
  143.6 38.5 %all-to-all-start.1 = ((bf16[64,16,768]{2,1,0:T(8,128)(2,1)}), bf16[64,16,768]{2,1,0:T(8,128)(2,1)S(1)}, u32[]{:S(2)}, u32[]{:S(2)}) async-start(bf16[64,16,768]{2,1,0:T(8,128)(2,1)} %dft.3), calls=%async_computation.1 | async-start | bytes 3145728 | tf_op jit(solution)/shard_map/all_to_all | solution.py:490
  154.2 1.2 copy-start.4
  155.4 1.3 copy-start.8
  182.1 1.5 copy-start.9
  186.0 13.8 %collective-permute-start.18 = (f32[8,240,128]{2,1,0:T(8,128)S(1)}, f32[8,240,128]{2,1,0:T(8,128)S(1)}, u32[]{:S(2)}, u32[]{:S(2)}) collective-permute-start(f32[8,240,128]{2,1,0:T(8,128)S(1)} %slice.53), channel_id=1, source_target_pairs={{0,1},{1,0},{2,3},{3,2},{4,5},{5,4},{6,7},{7,6},{8,9},{9,8},{10,11... | collective-permute-start | bytes 2949128 | tf_op jit(solution)/shard_map/ppermute | solution.py:407
  199.9 24.9 %copy-start.5 = (bf16[16,192,256]{2,1,0:T(8,128)(2,1)S(1)}, bf16[16,192,256]{2,1,0:T(8,128)(2,1)}, u32[]{:S(2)}) copy-start(bf16[16,192,256]{2,1,0:T(8,128)(2,1)} %copy-done.4) | copy-start | bytes 4718596
  199.9 24.9 %copy-start.6 = (bf16[192,192]{1,0:T(8,128)(2,1)S(1)}, bf16[192,192]{1,0:T(8,128)(2,1)}, u32[]{:S(2)}) copy-start(bf16[192,192]{1,0:T(8,128)(2,1)} %constant.61.clone.perm) | copy-start | bytes 221188
  200.0 12.5 %collective-permute-start.19 = (f32[4,240,128]{2,1,0:T(8,128)S(1)}, f32[4,240,128]{2,1,0:T(8,128)S(1)}, u32[]{:S(2)}, u32[]{:S(2)}) collective-permute-start(f32[4,240,128]{2,1,0:T(8,128)S(1)} %slice.61), channel_id=1, source_target_pairs={{0,2},{2,0},{1,3},{3,1},{4,6},{6,4},{5,7},{7,5},{8,10},{10,8},{9,1... | collective-permute-start | bytes 1474568 | tf_op jit(solution)/shard_map/ppermute | solution.py:407
  230.2 3.7 %copy-start.1 = (f32[12,2048]{1,0:T(8,128)S(1)}, f32[12,2048]{1,0:T(8,128)}, u32[]{:S(2)}) copy-start(f32[12,2048]{1,0:T(8,128)} %param.7) | copy-start | bytes 294916

commit v4 on v3

--- a/solution.py
+++ b/solution.py
@@ -476,11 +476,13 @@
         kept[0].append(mine)
         back[0].append(swap(sent))
     specs = []
+    back_first = back[0][0]
     for i in range(2):
         arrays = (ways_b[i][0], both_b[i], ways_b[i][1])
         views = tuple((n % 3, n // 3, 0) for n in range(6))
         if i == 1:
             specs.append(dft(side, kept[0], back[0], table_h, table_l, groups, 30))
+            arrays = fence((arrays, back_first))[0]
         mine, sent = filtered(side, arrays, views, coefs_b[i])
         kept[1].append(mine)
         if i == 0:

time: 234 us -> 235 us (level)
    ppermute x8, waiting for transfers between devices: 19.7 us -> 37.7 us  [swap(): return lax.ppermute(value, 'h', cyclic(2, 1))]
    ppermute x5, waiting for transfers between devices: 19.3 us -> 10 us  [both_ways(): lax.ppermute(value, ('y', 'z'), cyclic(rings, 1))]
    all_to_all x2, waiting for transfers between devices: 31.9 us -> 24.1 us  [shards(): lax.all_to_all(spec, FREQ, split_axis=0, concat_axis=0, tiled=True)]
    ppermute x2, starting transfers between devices: 12 us -> 14.6 us  [reduce_inputs(): packed = packed[:half] + lax.ppermute(packed[half:], axis, cyclic(2, 1))]
  transfers between devices with their start and end apart: 22 -> 22, of which waited for: 9 -> 8; matrix products, arithmetic and copies ran while one was open for 7% -> 7% of each run, Pallas kernels for 14% -> 14%
where the time goes in v4:
time: 235 us; the launch traced here: 234 us
  waiting for transfers between devices  85 us (36%)
  starting transfers between devices  69.8 us (30%)
  Pallas kernels  44.9 us (19%)
  other arithmetic  15.1 us (6%)
  local copies, waits for them, and re-layouts  10.9 us (5%)
  blocking collectives  7.76 us (3%)
    ppermute x8, waiting for transfers between devices, swap(): return lax.ppermute(value, 'h', cyclic(2, 1))  37.7 us
    ppermute x5, starting transfers between devices, both_ways(): lax.ppermute(value, ('y', 'z'), cyclic(rings, -1))  25.6 us
    all_to_all x2, waiting for transfers between devices, shards(): lax.all_to_all(spec, FREQ, split_axis=0, concat_axis=0, tiled=True)  24.1 us
    pallas_call x2, Pallas kernels, dft(): pl.pallas_call(dft_kernel, out_shape=jax.ShapeDtypeStruct((groups, per, 2...  19.7 us
    ppermute x2, starting transfers between devices, reduce_inputs(): packed = packed[:half] + lax.ppermute(packed[half:], axis, cyclic(2, 1))  14.6 us
    all_to_all x2, starting transfers between devices, shards(): lax.all_to_all(spec, FREQ, split_axis=0, concat_axis=0, tiled=True)  13.9 us
    ppermute x2, waiting for transfers between devices, reduce_inputs(): packed = packed[:half] + lax.ppermute(packed[half:], axis, cyclic(2, 1))  13.2 us
    ppermute x8, starting transfers between devices, swap(): return lax.ppermute(value, 'h', cyclic(2, 1))  13 us
  transfers between devices with their start and end apart: 22, of which 8 were waited for; matrix products, arithmetic and copies ran while one was open for 7% of the time, Pallas kernels for 14%

profile of v4, /device:TPU:1, one launch (start us, length us, event | category | flops | bytes accessed | tf_op | source)
XLA Modules:
  0.0 234.4 jit_solution(6406554773634053309)
XLA Ops:
  0.7 1.6 dynamic-slice_convert_fusion.refs_1_
  2.2 2.5 %collective-permute-start = (bf16[3,1024,128]{2,1,0:T(8,128)(2,1)S(1)}, bf16[3,1024,128]{2,1,0:T(8,128)(2,1)S(1)}, u32[]{:S(2)}, u32[]{:S(2)}) collective-permute-start(bf16[3,1024,128]{2,1,0:T(8,128)(2,1)S(1)} %dynamic-slice_convert_fusion.refs_1_), channel_id=1, source_target_pairs={{0,8},{8,16},{16,24},{24,32},{32,40},{40,48},{48,56},{56,64},{64,7... | collective-permute-start | bytes 2359304 | tf_op jit(solution)/shard_map/ppermute | solution.py:441
  4.8 6.5 %collective-permute-start.1 = (bf16[3,1024,128]{2,1,0:T(8,128)(2,1)S(1)}, bf16[3,1024,128]{2,1,0:T(8,128)(2,1)S(1)}, u32[]{:S(2)}, u32[]{:S(2)}) collective-permute-start(bf16[3,1024,128]{2,1,0:T(8,128)(2,1)S(1)} %dynamic-slice_convert_fusion.refs_1_), channel_id=1, source_target_pairs={{0,248},{8,0},{16,8},{24,16},{32,24},{40,32},{48,40},{56,48},{64,5... | collective-permute-start | bytes 2359304 | tf_op jit(solution)/shard_map/ppermute | solution.py:442
  11.3 3.9 %fusion.2 = (bf16[1,3,512,128]{3,2,1,0:T(8,128)(2,1)}, bf16[3,512,128]{2,1,0:T(8,128)(2,1)}, bf16[1,3,512,128]{3,2,1,0:T(8,128)(2,1)}, bf16[3,512,128]{2,1,0:T(8...) fusion(s32[3,2048,256]{2,1,0:T(8,128)} %param.6, s32[]{:T(128)S(6)} %select_n.42, ...), kind=kLoop, calls=%fused_computation.20 | loop fusion | flops 1179648 | bytes 7077904 | tf_op jit(solution)/shard_map/stack | solution.py:466
  15.2 2.7 %collective-permute-start.2 = (bf16[3,512,128]{2,1,0:T(8,128)(2,1)}, bf16[3,512,128]{2,1,0:T(8,128)(2,1)S(1)}, u32[]{:S(2)}, u32[]{:S(2)}) collective-permute-start(bf16[3,512,128]{2,1,0:T(8,128)(2,1)} %get-tuple-element.90), channel_id=1, source_target_pairs={{0,4},{4,0},{1,5},{5,1},{2,6},{6,2},{3,7},{7,3},{8,12},{12,8},{9,1... | collective-permute-start | bytes 1179656 | tf_op jit(solution)/shard_map/ppermute | solution.py:437
  18.3 1.1 fusion.9
  19.4 1.1 subtract_bitcast_fusion.1
  20.5 0.8 pad_maximum_fusion
  21.3 5.3 %collective-permute-done.2.refs_4_ = bf16[3,512,128]{2,1,0:T(8,128)(2,1)S(1)} collective-permute-done((bf16[3,512,128]{2,1,0:T(8,128)(2,1)}, bf16[3,512,128]{2,1,0:T(8,128)(2,1)S(1)}, u32[]{:S(2)}, u32[]{:S(2)}) %collective-permute-start.2) | collective-permute-done | bytes 393248 | tf_op jit(solution)/shard_map/ppermute | solution.py:437
  26.6 2.7 %collective-permute-start.5 = (bf16[3,512,128]{2,1,0:T(8,128)(2,1)}, bf16[3,512,128]{2,1,0:T(8,128)(2,1)S(1)}, u32[]{:S(2)}, u32[]{:S(2)}) collective-permute-start(bf16[3,512,128]{2,1,0:T(8,128)(2,1)} %get-tuple-element.52), channel_id=1, source_target_pairs={{0,4},{4,0},{1,5},{5,1},{2,6},{6,2},{3,7},{7,3},{8,12},{12,8},{9,1... | collective-permute-start | bytes 1179656 | tf_op jit(solution)/shard_map/ppermute | solution.py:437
  29.3 4.8 %collective-permute-start.4 = (bf16[3,512,128]{2,1,0:T(8,128)(2,1)S(1)}, bf16[3,512,128]{2,1,0:T(8,128)(2,1)}, u32[]{:S(2)}, u32[]{:S(2)}) collective-permute-start(bf16[3,512,128]{2,1,0:T(8,128)(2,1)S(1)} %collective-permute-done.2.refs_4_), channel_id=1, source_target_pairs={{0,248},{8,0},{16,8},{24,16},{32,24},{40,32},{48,40},{56,48},{64,5... | collective-permute-start | bytes 1179656 | tf_op jit(solution)/shard_map/ppermute | solution.py:442
  34.1 5.2 %fusion = (bf16[2,1024,1024]{2,1,0:T(8,128)(2,1)}, bf16[2,1024,1024]{2,1,0:T(8,128)(2,1)}) fusion(f32[2,1024,1024]{2,1,0:T(8,128)S(1)} %bitcast.29), kind=kLoop, calls=%fused_computation.2 | loop fusion | flops 8388608 | bytes 16777216 | tf_op jit(solution)/shard_map/convert_element_type | solution.py:30
  39.4 1.0 copy.14
  40.4 1.1 fusion.17
  41.8 2.7 %collective-permute-start.10 = (bf16[3,512,128]{2,1,0:T(8,128)(2,1)}, bf16[3,512,128]{2,1,0:T(8,128)(2,1)S(1)}, u32[]{:S(2)}, u32[]{:S(2)}) collective-permute-start(bf16[3,512,128]{2,1,0:T(8,128)(2,1)} %get-tuple-element.56), channel_id=1, source_target_pairs={{0,4},{4,0},{1,5},{5,1},{2,6},{6,2},{3,7},{7,3},{8,12},{12,8},{9,1... | collective-permute-start | bytes 1179656 | tf_op jit(solution)/shard_map/ppermute | solution.py:437
  44.6 4.8 %collective-permute-start.7 = (bf16[3,512,128]{2,1,0:T(8,128)(2,1)S(1)}, bf16[3,512,128]{2,1,0:T(8,128)(2,1)S(1)}, u32[]{:S(2)}, u32[]{:S(2)}) collective-permute-start(bf16[3,512,128]{2,1,0:T(8,128)(2,1)S(1)} %collective-permute-done.5.refs_4_), channel_id=1, source_target_pairs={{0,248},{8,0},{16,8},{24,16},{32,24},{40,32},{48,40},{56,48},{64,5... | collective-permute-start | bytes 1179656 | tf_op jit(solution)/shard_map/ppermute | solution.py:442
  49.4 3.7 %filter.4 = (f32[3,512,128]{2,1,0:T(8,128)S(1)}, f32[3,512,128]{2,1,0:T(8,128)S(1)}) custom-call(s32[1]{0:T(128)} %bitcast.2.side, f32[512,12]{1,0:T(8,128)S(1)} %get-tuple-element.97.coef, bf16[3,1024,128]{2,1,0:T(8,128)(2,1)S(1)} %collective-permute-done.refs_0_, bf16[3,1024,128]{2,1,0:T(8,128)(2,1)S(1)} %dynamic-slice_convert_fusion.refs_1_, ...), custom_call_target="tpu_custom_call" | custom-call | flops 40000000000 | tf_op jit(solution)/shard_map/filter/pallas_call | solution.py:106
  53.3 1.8 collective-permute-done.6.refs_3_
  55.2 4.8 %collective-permute-start.15 = (bf16[2,3,512,128]{3,2,1,0:T(8,128)(2,1)S(1)}, bf16[2,3,512,128]{3,2,1,0:T(8,128)(2,1)S(1)}, u32[]{:S(2)}, u32[]{:S(2)}) collective-permute-start(bf16[2,3,512,128]{3,2,1,0:T(8,128)(2,1)S(1)} %pad_maximum_fusion.2.refs_1_), channel_id=1, source_target_pairs={{0,248},{8,0},{16,8},{24,16},{32,24},{40,32},{48,40},{56,48},{64,5... | collective-permute-start | bytes 2359304 | tf_op jit(solution)/shard_map/ppermute | solution.py:442
  60.1 4.8 %collective-permute-start.12 = (bf16[2,3,512,128]{3,2,1,0:T(8,128)(2,1)S(1)}, bf16[2,3,512,128]{3,2,1,0:T(8,128)(2,1)S(1)}, u32[]{:S(2)}, u32[]{:S(2)}) collective-permute-start(bf16[2,3,512,128]{3,2,1,0:T(8,128)(2,1)S(1)} %pad_maximum_fusion.1.refs_1_), channel_id=1, source_target_pairs={{0,248},{8,0},{16,8},{24,16},{32,24},{40,32},{48,40},{56,48},{64,5... | collective-permute-start | bytes 2359304 | tf_op jit(solution)/shard_map/ppermute | solution.py:442
  64.9 2.4 %filter.5 = (f32[3,512,128]{2,1,0:T(8,128)S(1)}, f32[3,512,128]{2,1,0:T(8,128)S(1)}) custom-call(s32[1]{0:T(128)} %bitcast.2.side, f32[512,12]{1,0:T(8,128)S(1)} %get-tuple-element.96.coef, bf16[3,1024,128]{2,1,0:T(8,128)(2,1)S(1)} %collective-permute-done.refs_0_, bf16[3,1024,128]{2,1,0:T(8,128)(2,1)S(1)} %dynamic-slice_convert_fusion.refs_1_, ...), custom_call_target="tpu_custom_call" | custom-call | flops 40000000000 | tf_op jit(solution)/shard_map/filter/pallas_call | solution.py:106
  67.3 9.1 %collective-permute-done.8.refs_2_ = f32[3,512,128]{2,1,0:T(8,128)S(1)} collective-permute-done((f32[3,512,128]{2,1,0:T(8,128)S(1)}, f32[3,512,128]{2,1,0:T(8,128)S(1)}, u32[]{:S(2)}, u32[]{:S(2)}) %collective-permute-start.8) | collective-permute-done | bytes 786464 | tf_op jit(solution)/shard_map/ppermute | solution.py:437
  76.6 2.4 %filter.7 = (f32[3,512,128]{2,1,0:T(8,128)S(1)}, f32[3,512,128]{2,1,0:T(8,128)S(1)}) custom-call(s32[1]{0:T(128)} %bitcast.2.side, f32[512,12]{1,0:T(8,128)S(1)} %get-tuple-element.96.coef, bf16[2,3,512,128]{3,2,1,0:T(8,128)(2,1)S(1)} %collective-permute-done.14.refs_0_, bf16[2,3,512,128]{3,2,1,0:T(8,128)(2,1)S(1)} %pad_maximum_fusion.2.refs_1_, ...), custom_call_target="tpu_custom_call" | custom-call | flops 40000000000 | tf_op jit(solution)/shard_map/filter/pallas_call | solution.py:106
  79.1 2.8 %collective-permute-start.17 = (f32[3,512,128]{2,1,0:T(8,128)S(1)}, f32[3,512,128]{2,1,0:T(8,128)}, u32[]{:S(2)}, u32[]{:S(2)}) collective-permute-start(f32[3,512,128]{2,1,0:T(8,128)S(1)} %get-tuple-element.74), channel_id=1, source_target_pairs={{0,4},{4,0},{1,5},{5,1},{2,6},{6,2},{3,7},{7,3},{8,12},{12,8},{9,1... | collective-permute-start | bytes 2359304 | tf_op jit(solution)/shard_map/ppermute | solution.py:437
  81.9 8.2 %collective-permute-done.11.refs_0_ = bf16[2,3,512,128]{3,2,1,0:T(8,128)(2,1)S(1)} collective-permute-done((bf16[2,3,512,128]{3,2,1,0:T(8,128)(2,1)S(1)}, bf16[2,3,512,128]{3,2,1,0:T(8,128)(2,1)S(1)}, u32[]{:S(2)}, u32[]{:S(2)}) %collective-permute-start.11) | collective-permute-done | bytes 786464 | tf_op jit(solution)/shard_map/ppermute | solution.py:441
  90.1 2.4 %filter.6 = (f32[3,512,128]{2,1,0:T(8,128)S(1)}, f32[3,512,128]{2,1,0:T(8,128)S(1)}) custom-call(s32[1]{0:T(128)} %bitcast.2.side, f32[512,12]{1,0:T(8,128)S(1)} %get-tuple-element.97.coef, bf16[2,3,512,128]{3,2,1,0:T(8,128)(2,1)S(1)} %collective-permute-done.11.refs_0_, bf16[2,3,512,128]{3,2,1,0:T(8,128)(2,1)S(1)} %pad_maximum_fusion.1.refs_1_, ...), custom_call_target="tpu_custom_call" | custom-call | flops 40000000000 | tf_op jit(solution)/shard_map/filter/pallas_call | solution.py:106
  92.5 0.9 copy-done.11
  93.4 1.3 collective-permute-start.16
  94.7 8.6 %dft.2 = bf16[64,16,768]{2,1,0:T(8,128)(2,1)} custom-call(s32[1]{0:T(128)} %bitcast.2.side, f32[3,512,128]{2,1,0:T(8,128)S(1)} %get-tuple-element.59.refs_0_, f32[3,512,128]{2,1,0:T(8,128)S(1)} %get-tuple-element.60.refs_1_, f32[3,512,128]{2,1,0:T(8,128)S(1)} %collective-permute-done.8.refs_2_, f32[3,512,128]{2,1,0:T(8,128)S(1)} %collective-permute-done.9.refs_3_, ...), custom_call_target="tpu_custom_call" | custom-call | flops 40000000000 | tf_op jit(solution)/shard_map/dft/pallas_call | solution.py:172
  103.3 8.2 %all-to-all-start = ((bf16[64,16,768]{2,1,0:T(8,128)(2,1)}), bf16[64,16,768]{2,1,0:T(8,128)(2,1)S(1)}, u32[]{:S(2)}, u32[]{:S(2)}) async-start(bf16[64,16,768]{2,1,0:T(8,128)(2,1)} %dft.2), calls=%async_computation | async-start | bytes 3145728 | tf_op jit(solution)/shard_map/all_to_all | solution.py:492
  111.5 23.3 %collective-permute-done.16.refs_2_ = f32[3,512,128]{2,1,0:T(8,128)} collective-permute-done((f32[3,512,128]{2,1,0:T(8,128)S(1)}, f32[3,512,128]{2,1,0:T(8,128)}, u32[]{:S(2)}, u32[]{:S(2)}) %collective-permute-start.16) | collective-permute-done | bytes 786464 | tf_op jit(solution)/shard_map/ppermute | solution.py:437
  134.7 11.1 %dft.3 = bf16[64,16,768]{2,1,0:T(8,128)(2,1)} custom-call(s32[1]{0:T(128)} %bitcast.2.side, f32[3,512,128]{2,1,0:T(8,128)} %copy-done.11, f32[3,512,128]{2,1,0:T(8,128)} %copy-done.10, f32[3,512,128]{2,1,0:T(8,128)} %collective-permute-done.16.refs_2_, f32[3,512,128]{2,1,0:T(8,128)} %collective-permute-done.17.refs_3_, ...), custom_call_target="tpu_custom_call" | custom-call | flops 40000000000 | tf_op jit(solution)/shard_map/dft/pallas_call | solution.py:172
  145.8 5.8 %all-to-all-start.1 = ((bf16[64,16,768]{2,1,0:T(8,128)(2,1)}), bf16[64,16,768]{2,1,0:T(8,128)(2,1)S(1)}, u32[]{:S(2)}, u32[]{:S(2)}) async-start(bf16[64,16,768]{2,1,0:T(8,128)(2,1)} %dft.3), calls=%async_computation.1 | async-start | bytes 3145728 | tf_op jit(solution)/shard_map/all_to_all | solution.py:492
  152.4 2.3 gram.2
  154.7 1.2 copy-done.4
  155.9 1.3 copy-done.8
  157.2 24.1 %all-to-all-done.1.turned = bf16[64,16,768]{2,1,0:T(8,128)(2,1)S(1)} async-done(((bf16[64,16,768]{2,1,0:T(8,128)(2,1)}), bf16[64,16,768]{2,1,0:T(8,128)(2,1)S(1)}, u32[]{:S(2)}, u32[]{:S(2)}) %all-to-all-start.1) | async-done | bytes 1572896 | tf_op jit(solution)/shard_map/all_to_all | solution.py:492
  181.3 1.5 copy-done.9
  182.8 2.3 gram.3
  185.2 13.0 %collective-permute-start.18 = (f32[8,240,128]{2,1,0:T(8,128)S(1)}, f32[8,240,128]{2,1,0:T(8,128)S(1)}, u32[]{:S(2)}, u32[]{:S(2)}) collective-permute-start(f32[8,240,128]{2,1,0:T(8,128)S(1)} %slice.53), channel_id=1, source_target_pairs={{0,1},{1,0},{2,3},{3,2},{4,5},{5,4},{6,7},{7,6},{8,9},{9,8},{10,11... | collective-permute-start | bytes 2949128 | tf_op jit(solution)/shard_map/ppermute | solution.py:407
  198.2 2.2 collective-permute-done.18
  200.5 1.6 collective-permute-start.19
  202.1 11.0 %collective-permute-done.19 = f32[4,240,128]{2,1,0:T(8,128)S(1)} collective-permute-done((f32[4,240,128]{2,1,0:T(8,128)S(1)}, f32[4,240,128]{2,1,0:T(8,128)S(1)}, u32[]{:S(2)}, u32[]{:S(2)}) %collective-permute-start.19) | collective-permute-done | bytes 491552 | tf_op jit(solution)/shard_map/ppermute | solution.py:407
  213.1 4.5 %iterate.1 = f32[4,16,192]{2,1,0:T(8,128)S(1)} custom-call(f32[4,240,128]{2,1,0:T(8,128)S(1)} %slice_add_fusion.1.g), custom_call_target="tpu_custom_call" | custom-call | tf_op jit(solution)/shard_map/iterate/pallas_call | solution.py:338
  217.6 3.8 %all_gather.6 = f32[8,16,192]{2,1,0:T(8,128)S(1)} all-gather(f32[4,16,192]{2,1,0:T(8,128)S(1)} %iterate.1), channel_id=1, replica_groups=mesh['y'=4,'z'=8,'h'=2,'l'=2,'k'=2] {'l'}, dimensions={0}, use_global_device_ids=true | all-gather | bytes 147456 | tf_op jit(solution)/shard_map/all_gather | solution.py:413
  221.4 4.0 %all_gather.7.pair = f32[16,16,192]{2,1,0:T(8,128)S(1)} all-gather(f32[8,16,192]{2,1,0:T(8,128)S(1)} %all_gather.6), channel_id=1, replica_groups=mesh['y'=4,'z'=8,'h'=2,'l'=2,'k'=2] {'k'}, dimensions={0}, use_global_device_ids=true | all-gather | bytes 294912 | tf_op jit(solution)/shard_map/all_gather | solution.py:413
  225.4 5.4 %clean.1 = (bf16[16,192,512]{2,1,0:T(8,128)(2,1)S(1)}, f32[16,8,8]{2,1,0:T(8,128)S(1)}) custom-call(bf16[16,192,256]{2,1,0:T(8,128)(2,1)S(1)} %copy-done.5, bf16[16,192,256]{2,1,0:T(8,128)(2,1)S(1)} %get-tuple-element.76.xb, f32[16,16,192]{2,1,0:T(8,128)S(1)} %all_gather.7.pair, bf16[192,192]{1,0:T(8,128)(2,1)S(1)} %copy-done.6), custom_call_target="tpu_custom_call" | custom-call | tf_op jit(solution)/shard_map/clean/pallas_call | solution.py:382
  230.7 2.9 %reshape.230 = bf16[16,192,2,256]{3,2,1,0:T(2,128)(2,1)} reshape(bf16[16,192,512]{2,1,0:T(8,128)(2,1)S(1)} %get-tuple-element.78) | data formatting | bytes 6291456 | tf_op jit(solution)/shard_map/reshape | solution.py:500
  (64 shorter events, 3.1 us)
Async XLA Ops:
  0.6 38.7 %copy-start = (f32[12,2048]{1,0:T(8,128)S(1)}, f32[12,2048]{1,0:T(8,128)}, u32[]{:S(2)}) copy-start(f32[12,2048]{1,0:T(8,128)} %param.7) | copy-start | bytes 294916
  2.2 39.2 %collective-permute-start = (bf16[3,1024,128]{2,1,0:T(8,128)(2,1)S(1)}, bf16[3,1024,128]{2,1,0:T(8,128)(2,1)S(1)}, u32[]{:S(2)}, u32[]{:S(2)}) collective-permute-start(bf16[3,1024,128]{2,1,0:T(8,128)(2,1)S(1)} %dynamic-slice_convert_fusion.refs_1_), channel_id=1, source_target_pairs={{0,8},{8,16},{16,24},{24,32},{32,40},{40,48},{48,56},{56,64},{64,7... | collective-permute-start | bytes 2359304 | tf_op jit(solution)/shard_map/ppermute | solution.py:441
  4.8 36.7 %collective-permute-start.1 = (bf16[3,1024,128]{2,1,0:T(8,128)(2,1)S(1)}, bf16[3,1024,128]{2,1,0:T(8,128)(2,1)S(1)}, u32[]{:S(2)}, u32[]{:S(2)}) collective-permute-start(bf16[3,1024,128]{2,1,0:T(8,128)(2,1)S(1)} %dynamic-slice_convert_fusion.refs_1_), channel_id=1, source_target_pairs={{0,248},{8,0},{16,8},{24,16},{32,24},{40,32},{48,40},{56,48},{64,5... | collective-permute-start | bytes 2359304 | tf_op jit(solution)/shard_map/ppermute | solution.py:442
  15.2 11.4 %collective-permute-start.2 = (bf16[3,512,128]{2,1,0:T(8,128)(2,1)}, bf16[3,512,128]{2,1,0:T(8,128)(2,1)S(1)}, u32[]{:S(2)}, u32[]{:S(2)}) collective-permute-start(bf16[3,512,128]{2,1,0:T(8,128)(2,1)} %get-tuple-element.90), channel_id=1, source_target_pairs={{0,4},{4,0},{1,5},{5,1},{2,6},{6,2},{3,7},{7,3},{8,12},{12,8},{9,1... | collective-permute-start | bytes 1179656 | tf_op jit(solution)/shard_map/ppermute | solution.py:437
  26.6 14.9 %collective-permute-start.5 = (bf16[3,512,128]{2,1,0:T(8,128)(2,1)}, bf16[3,512,128]{2,1,0:T(8,128)(2,1)S(1)}, u32[]{:S(2)}, u32[]{:S(2)}) collective-permute-start(bf16[3,512,128]{2,1,0:T(8,128)(2,1)} %get-tuple-element.52), channel_id=1, source_target_pairs={{0,4},{4,0},{1,5},{5,1},{2,6},{6,2},{3,7},{7,3},{8,12},{12,8},{9,1... | collective-permute-start | bytes 1179656 | tf_op jit(solution)/shard_map/ppermute | solution.py:437
  29.3 12.1 %collective-permute-start.3 = (bf16[3,512,128]{2,1,0:T(8,128)(2,1)S(1)}, bf16[3,512,128]{2,1,0:T(8,128)(2,1)}, u32[]{:S(2)}, u32[]{:S(2)}) collective-permute-start(bf16[3,512,128]{2,1,0:T(8,128)(2,1)S(1)} %collective-permute-done.2.refs_4_), channel_id=1, source_target_pairs={{0,8},{8,16},{16,24},{24,32},{32,40},{40,48},{48,56},{56,64},{64,7... | collective-permute-start | bytes 1179656 | tf_op jit(solution)/shard_map/ppermute | solution.py:441
  29.3 12.1 %collective-permute-start.4 = (bf16[3,512,128]{2,1,0:T(8,128)(2,1)S(1)}, bf16[3,512,128]{2,1,0:T(8,128)(2,1)}, u32[]{:S(2)}, u32[]{:S(2)}) collective-permute-start(bf16[3,512,128]{2,1,0:T(8,128)(2,1)S(1)} %collective-permute-done.2.refs_4_), channel_id=1, source_target_pairs={{0,248},{8,0},{16,8},{24,16},{32,24},{40,32},{48,40},{56,48},{64,5... | collective-permute-start | bytes 1179656 | tf_op jit(solution)/shard_map/ppermute | solution.py:442
  41.5 11.7 %collective-permute-start.13 = (bf16[3,512,128]{2,1,0:T(8,128)(2,1)}, bf16[3,512,128]{2,1,0:T(8,128)(2,1)S(1)}, u32[]{:S(2)}, u32[]{:S(2)}) collective-permute-start(bf16[3,512,128]{2,1,0:T(8,128)(2,1)} %get-tuple-element.67), channel_id=1, source_target_pairs={{0,4},{4,0},{1,5},{5,1},{2,6},{6,2},{3,7},{7,3},{8,12},{12,8},{9,1... | collective-permute-start | bytes 1179656 | tf_op jit(solution)/shard_map/ppermute | solution.py:437
  41.8 18.1 %collective-permute-start.10 = (bf16[3,512,128]{2,1,0:T(8,128)(2,1)}, bf16[3,512,128]{2,1,0:T(8,128)(2,1)S(1)}, u32[]{:S(2)}, u32[]{:S(2)}) collective-permute-start(bf16[3,512,128]{2,1,0:T(8,128)(2,1)} %get-tuple-element.56), channel_id=1, source_target_pairs={{0,4},{4,0},{1,5},{5,1},{2,6},{6,2},{3,7},{7,3},{8,12},{12,8},{9,1... | collective-permute-start | bytes 1179656 | tf_op jit(solution)/shard_map/ppermute | solution.py:437
  44.6 10.6 %collective-permute-start.6 = (bf16[3,512,128]{2,1,0:T(8,128)(2,1)S(1)}, bf16[3,512,128]{2,1,0:T(8,128)(2,1)S(1)}, u32[]{:S(2)}, u32[]{:S(2)}) collective-permute-start(bf16[3,512,128]{2,1,0:T(8,128)(2,1)S(1)} %collective-permute-done.5.refs_4_), channel_id=1, source_target_pairs={{0,8},{8,16},{16,24},{24,32},{32,40},{40,48},{48,56},{56,64},{64,7... | collective-permute-start | bytes 1179656 | tf_op jit(solution)/shard_map/ppermute | solution.py:441
  44.6 10.6 %collective-permute-start.7 = (bf16[3,512,128]{2,1,0:T(8,128)(2,1)S(1)}, bf16[3,512,128]{2,1,0:T(8,128)(2,1)S(1)}, u32[]{:S(2)}, u32[]{:S(2)}) collective-permute-start(bf16[3,512,128]{2,1,0:T(8,128)(2,1)S(1)} %collective-permute-done.5.refs_4_), channel_id=1, source_target_pairs={{0,248},{8,0},{16,8},{24,16},{32,24},{40,32},{48,40},{56,48},{64,5... | collective-permute-start | bytes 1179656 | tf_op jit(solution)/shard_map/ppermute | solution.py:442
  49.4 3.9 %copy-start.13 = (bf16[1,3,512,128]{3,2,1,0:T(8,128)(2,1)S(1)}, bf16[1,3,512,128]{3,2,1,0:T(8,128)(2,1)}, u32[]{:S(2)}) copy-start(bf16[1,3,512,128]{3,2,1,0:T(8,128)(2,1)} %get-tuple-element.86) | copy-start | bytes 1179652
  49.4 10.6 %copy-start.12 = (bf16[1,3,512,128]{3,2,1,0:T(8,128)(2,1)S(1)}, bf16[1,3,512,128]{3,2,1,0:T(8,128)(2,1)}, u32[]{:S(2)}) copy-start(bf16[1,3,512,128]{3,2,1,0:T(8,128)(2,1)} %get-tuple-element.88) | copy-start | bytes 1179652
  53.1 23.3 %collective-permute-start.8 = (f32[3,512,128]{2,1,0:T(8,128)S(1)}, f32[3,512,128]{2,1,0:T(8,128)S(1)}, u32[]{:S(2)}, u32[]{:S(2)}) collective-permute-start(f32[3,512,128]{2,1,0:T(8,128)S(1)} %get-tuple-element.54), channel_id=1, source_target_pairs={{0,4},{4,0},{1,5},{5,1},{2,6},{6,2},{3,7},{7,3},{8,12},{12,8},{9,1... | collective-permute-start | bytes 2359304 | tf_op jit(solution)/shard_map/ppermute | solution.py:437
  55.2 21.5 %collective-permute-start.14 = (bf16[2,3,512,128]{3,2,1,0:T(8,128)(2,1)S(1)}, bf16[2,3,512,128]{3,2,1,0:T(8,128)(2,1)S(1)}, u32[]{:S(2)}, u32[]{:S(2)}) collective-permute-start(bf16[2,3,512,128]{3,2,1,0:T(8,128)(2,1)S(1)} %pad_maximum_fusion.2.refs_1_), channel_id=1, source_target_pairs={{0,8},{8,16},{16,24},{24,32},{32,40},{40,48},{48,56},{56,64},{64,7... | collective-permute-start | bytes 2359304 | tf_op jit(solution)/shard_map/ppermute | solution.py:441
  55.2 21.5 %collective-permute-start.15 = (bf16[2,3,512,128]{3,2,1,0:T(8,128)(2,1)S(1)}, bf16[2,3,512,128]{3,2,1,0:T(8,128)(2,1)S(1)}, u32[]{:S(2)}, u32[]{:S(2)}) collective-permute-start(bf16[2,3,512,128]{3,2,1,0:T(8,128)(2,1)S(1)} %pad_maximum_fusion.2.refs_1_), channel_id=1, source_target_pairs={{0,248},{8,0},{16,8},{24,16},{32,24},{40,32},{48,40},{56,48},{64,5... | collective-permute-start | bytes 2359304 | tf_op jit(solution)/shard_map/ppermute | solution.py:442
  60.0 30.1 %collective-permute-start.11 = (bf16[2,3,512,128]{3,2,1,0:T(8,128)(2,1)S(1)}, bf16[2,3,512,128]{3,2,1,0:T(8,128)(2,1)S(1)}, u32[]{:S(2)}, u32[]{:S(2)}) collective-permute-start(bf16[2,3,512,128]{3,2,1,0:T(8,128)(2,1)S(1)} %pad_maximum_fusion.1.refs_1_), channel_id=1, source_target_pairs={{0,8},{8,16},{16,24},{24,32},{32,40},{40,48},{48,56},{56,64},{64,7... | collective-permute-start | bytes 2359304 | tf_op jit(solution)/shard_map/ppermute | solution.py:441
  60.1 30.0 %collective-permute-start.12 = (bf16[2,3,512,128]{3,2,1,0:T(8,128)(2,1)S(1)}, bf16[2,3,512,128]{3,2,1,0:T(8,128)(2,1)S(1)}, u32[]{:S(2)}, u32[]{:S(2)}) collective-permute-start(bf16[2,3,512,128]{3,2,1,0:T(8,128)(2,1)S(1)} %pad_maximum_fusion.1.refs_1_), channel_id=1, source_target_pairs={{0,248},{8,0},{16,8},{24,16},{32,24},{40,32},{48,40},{56,48},{64,5... | collective-permute-start | bytes 2359304 | tf_op jit(solution)/shard_map/ppermute | solution.py:442
  76.4 17.0 %collective-permute-start.9 = (f32[3,512,128]{2,1,0:T(8,128)S(1)}, f32[3,512,128]{2,1,0:T(8,128)S(1)}, u32[]{:S(2)}, u32[]{:S(2)}) collective-permute-start(f32[3,512,128]{2,1,0:T(8,128)S(1)} %get-tuple-element.55), channel_id=1, source_target_pairs={{0,4},{4,0},{1,5},{5,1},{2,6},{6,2},{3,7},{7,3},{8,12},{12,8},{9,1... | collective-permute-start | bytes 2359304 | tf_op jit(solution)/shard_map/ppermute | solution.py:437
  79.0 13.4 %copy-start.10 = (f32[3,512,128]{2,1,0:T(8,128)}, f32[3,512,128]{2,1,0:T(8,128)S(1)}, u32[]{:S(2)}) copy-start(f32[3,512,128]{2,1,0:T(8,128)S(1)} %get-tuple-element.72.refs_1_) | copy-start | bytes 2359300
  79.0 15.6 %copy-start.2 = (bf16[2,1024,1024]{2,1,0:T(8,128)(2,1)S(1)}, bf16[2,1024,1024]{2,1,0:T(8,128)(2,1)}, u32[]{:S(2)}) copy-start(bf16[2,1024,1024]{2,1,0:T(8,128)(2,1)} %get-tuple-element.64.refs_5_) | copy-start | bytes 12582916
  79.1 15.6 %copy-start.3 = (bf16[2,1024,1024]{2,1,0:T(8,128)(2,1)S(1)}, bf16[2,1024,1024]{2,1,0:T(8,128)(2,1)}, u32[]{:S(2)}) copy-start(bf16[2,1024,1024]{2,1,0:T(8,128)(2,1)} %get-tuple-element.63.refs_4_) | copy-start | bytes 12582916
  79.1 32.4 %collective-permute-start.17 = (f32[3,512,128]{2,1,0:T(8,128)S(1)}, f32[3,512,128]{2,1,0:T(8,128)}, u32[]{:S(2)}, u32[]{:S(2)}) collective-permute-start(f32[3,512,128]{2,1,0:T(8,128)S(1)} %get-tuple-element.74), channel_id=1, source_target_pairs={{0,4},{4,0},{1,5},{5,1},{2,6},{6,2},{3,7},{7,3},{8,12},{12,8},{9,1... | collective-permute-start | bytes 2359304 | tf_op jit(solution)/shard_map/ppermute | solution.py:437
  92.5 0.9 copy-start.11
  93.4 41.3 %collective-permute-start.16 = (f32[3,512,128]{2,1,0:T(8,128)S(1)}, f32[3,512,128]{2,1,0:T(8,128)}, u32[]{:S(2)}, u32[]{:S(2)}) collective-permute-start(f32[3,512,128]{2,1,0:T(8,128)S(1)} %get-tuple-element.73), channel_id=1, source_target_pairs={{0,4},{4,0},{1,5},{5,1},{2,6},{6,2},{3,7},{7,3},{8,12},{12,8},{9,1... | collective-permute-start | bytes 2359304 | tf_op jit(solution)/shard_map/ppermute | solution.py:437
  103.3 42.6 %all-to-all-start = ((bf16[64,16,768]{2,1,0:T(8,128)(2,1)}), bf16[64,16,768]{2,1,0:T(8,128)(2,1)S(1)}, u32[]{:S(2)}, u32[]{:S(2)}) async-start(bf16[64,16,768]{2,1,0:T(8,128)(2,1)} %dft.2), calls=%async_computation | async-start | bytes 3145728 | tf_op jit(solution)/shard_map/all_to_all | solution.py:492
  145.8 6.6 %copy-start.7 = (bf16[256,256]{1,0:T(8,128)(2,1)S(1)}, bf16[256,256]{1,0:T(8,128)(2,1)}, u32[]{:S(2)}) copy-start(bf16[256,256]{1,0:T(8,128)(2,1)} %constant.60.clone.order) | copy-start | bytes 393220
  145.8 35.4 %all-to-all-start.1 = ((bf16[64,16,768]{2,1,0:T(8,128)(2,1)}), bf16[64,16,768]{2,1,0:T(8,128)(2,1)S(1)}, u32[]{:S(2)}, u32[]{:S(2)}) async-start(bf16[64,16,768]{2,1,0:T(8,128)(2,1)} %dft.3), calls=%async_computation.1 | async-start | bytes 3145728 | tf_op jit(solution)/shard_map/all_to_all | solution.py:492
  154.7 1.2 copy-start.4
  155.9 1.3 copy-start.8
  181.3 1.5 copy-start.9
  185.2 15.2 %collective-permute-start.18 = (f32[8,240,128]{2,1,0:T(8,128)S(1)}, f32[8,240,128]{2,1,0:T(8,128)S(1)}, u32[]{:S(2)}, u32[]{:S(2)}) collective-permute-start(f32[8,240,128]{2,1,0:T(8,128)S(1)} %slice.53), channel_id=1, source_target_pairs={{0,1},{1,0},{2,3},{3,2},{4,5},{5,4},{6,7},{7,6},{8,9},{9,8},{10,11... | collective-permute-start | bytes 2949128 | tf_op jit(solution)/shard_map/ppermute | solution.py:407
  200.5 24.9 %copy-start.5 = (bf16[16,192,256]{2,1,0:T(8,128)(2,1)S(1)}, bf16[16,192,256]{2,1,0:T(8,128)(2,1)}, u32[]{:S(2)}) copy-start(bf16[16,192,256]{2,1,0:T(8,128)(2,1)} %copy-done.4) | copy-start | bytes 4718596
  200.5 24.9 %copy-start.6 = (bf16[192,192]{1,0:T(8,128)(2,1)S(1)}, bf16[192,192]{1,0:T(8,128)(2,1)}, u32[]{:S(2)}) copy-start(bf16[192,192]{1,0:T(8,128)(2,1)} %constant.61.clone.perm) | copy-start | bytes 221188
  200.5 12.5 %collective-permute-start.19 = (f32[4,240,128]{2,1,0:T(8,128)S(1)}, f32[4,240,128]{2,1,0:T(8,128)S(1)}, u32[]{:S(2)}, u32[]{:S(2)}) collective-permute-start(f32[4,240,128]{2,1,0:T(8,128)S(1)} %slice.61), channel_id=1, source_target_pairs={{0,2},{2,0},{1,3},{3,1},{4,6},{6,4},{5,7},{7,5},{8,10},{10,8},{9,1... | collective-permute-start | bytes 1474568 | tf_op jit(solution)/shard_map/ppermute | solution.py:407
  230.7 3.7 %copy-start.1 = (f32[12,2048]{1,0:T(8,128)S(1)}, f32[12,2048]{1,0:T(8,128)}, u32[]{:S(2)}) copy-start(f32[12,2048]{1,0:T(8,128)} %param.7) | copy-start | bytes 294916
